TPU v7x, 32 devices: a whole 2x2x4 slice. The times are simulated.
32 devices in a mesh: groups: 2 (over y), seq: 8 (over z, core), section: 2 (over x), tp: 1.
Axes of the slice: x: 2, y: 2, z: 4, core: 2. Of those that a mesh axis runs over, the one named last changes fastest.
Arguments:
- stream: bfloat16 [4, 512, 1536], P('groups', 'seq', 'tp'), parts along dimension 0, may hold values from -30 to 30
- set_views: int32 [4, 6], P('groups'), parts along dimension 0, may hold values from 1 to 2, 8 in all within a row
- modulation: bfloat16 [2, 4, 6, 2, 1536], P('section', 'groups', None, None, 'tp'), parts along dimension 1, may hold values from -2.5 to 2.5
- set_gate: bfloat16 [2, 4, 6, 1536], P('section', 'groups', None, 'tp'), parts along dimension 1, may hold values from 0.5 to 1.5
- qkv_weight: bfloat16 [2, 1536, 3, 1536], P('section', 'seq', None, 'tp'), may hold values from -0.15625 to 0.15625
- norm_gain: float32 [2, 2, 128], P('section'), may hold values from 0.1 to 1.9
- out_weight: bfloat16 [2, 1536, 1536], P('section', None, 'tp'), may hold values from -0.15625 to 0.15625
Outputs:
- hidden: bfloat16 [2, 4, 512, 1536], P('section', 'groups', 'seq', 'tp'), parts along dimension 1
There are 2 independent parts, one for each index of `groups`. A program takes and returns all parts, laid end to end along the dimension named above; an argument that names none is the same for every part. Nothing has to cross between parts.
Inputs may be any that keep to these rules, and one draw needn't show every extreme that they name: Each row of set_views sums to 8; every row has a set of 2 views.
All inputs are finite; a program needn't handle non-finite values.
Results may differ from a plain program's by a relative error of at most 0.01.
Values may be sent and summed in bfloat16 or wider, within the bound.
No kernel may reach another device: no remote copies, remote signals or barrier semaphores. Data moves between devices by JAX's collectives and lax.ppermute only.
A program may use at most 64 MiB of HBM per device.

v0:
```python
import jax
import jax.numpy as jnp
from jax import lax
from jax.sharding import PartitionSpec as P

REACH = 1


epsilon = 1e-06


def shifted(array, axis, by):
    size = lax.axis_size(axis)
    pairs = [(i, i + by) for i in range(size) if 0 <= i + by < size]
    return lax.ppermute(array, axis, pairs)


def view_sets(set_views, count):
    starts = jnp.cumsum(set_views) - set_views
    position = jnp.arange(count, dtype=jnp.int32)
    inside = (starts[None, :] <= position[:, None]).astype(jnp.int32)
    return jnp.sum(inside, axis=1) - 1


def unit_rms(values, scaling):
    return values * lax.rsqrt(jnp.mean(values * values, axis=-1, keepdims=True) + epsilon) * scaling


def relay_cycle(payload):
    moving = payload
    moving = shifted(moving, "seq", 1)
    below_list = [moving]
    moving = payload
    moving = shifted(moving, "seq", -1)
    above_list = [moving]
    return below_list[::-1] + [payload] + above_list


def body(stream, set_views, modulation, set_gate, qkv_weight, norm_gain, out_weight):
    micro_count, view_tok, local_width = stream.shape
    head_size = norm_gain.shape[2]
    head_count = local_width // head_size
    seq_count = lax.axis_size("seq")
    section_count = lax.axis_size("section")
    seq_place = lax.axis_index("seq")
    section_place = lax.axis_index("section")
    full_width = local_width * lax.axis_size("tp")
    whole_qkv = lax.all_gather(qkv_weight[0], "seq", axis=0, tiled=True)
    qkv_flat = whole_qkv.reshape(whole_qkv.shape[0], 3 * local_width)
    gain_pair = norm_gain[0]
    out_rows = out_weight[0]
    score_scale = head_size ** (-0.5)
    offsets = list(range(-REACH, REACH + 1))
    ticks = micro_count + section_count - 1
    carried = jnp.zeros((view_tok, local_width), jnp.bfloat16)
    hidden = jnp.zeros((micro_count, view_tok, local_width), jnp.bfloat16)
    for moment in range(ticks):
        fresh_input = stream[min(moment, micro_count - 1)]
        section_input = jnp.where(section_place == 0, fresh_input, carried)
        micro_raw = moment - section_place
        micro_index = jnp.clip(micro_raw, 0, micro_count - 1)
        owners = view_sets(set_views[micro_index], seq_count)
        own_set = owners[seq_place]
        widened = section_input.astype(jnp.float32)
        totals, squares = lax.psum(
            (jnp.sum(widened, axis=1), jnp.sum(widened * widened, axis=1)), "tp"
        )
        average = (totals / full_width)[:, None]
        spread = (squares / full_width)[:, None] - average * average
        factors = modulation[0, micro_index, own_set].astype(jnp.float32)
        normed = (
            (widened - average) * lax.rsqrt(spread + epsilon) * (1.0 + factors[1]) + factors[0]
        ).astype(jnp.bfloat16)
        section_projected = jnp.dot(
            lax.all_gather(normed, "tp", axis=1, tiled=True),
            qkv_flat,
            preferred_element_type=jnp.float32,
        )
        queries = unit_rms(
            section_projected.reshape(view_tok, 3, head_count, head_size)[:, 0], gain_pair[0]
        ).astype(jnp.bfloat16)
        parts = section_projected.reshape(view_tok, 3, head_count, head_size)
        keys_here = unit_rms(parts[:, 1], gain_pair[1]).astype(jnp.bfloat16)
        values_here = parts[:, 2].astype(jnp.bfloat16)
        key_list = []
        value_list = []
        stacked = jnp.stack(
            [keys_here.reshape(view_tok, local_width), values_here.reshape(view_tok, local_width)]
        )
        arrived = relay_cycle(stacked)
        for received in arrived:
            key_list.append(received[0].reshape(view_tok, head_count, head_size))
            value_list.append(received[1].reshape(view_tok, head_count, head_size))
        visible = []
        for offset in offsets:
            neighbour = seq_place + offset
            in_range = (neighbour >= 0) & (neighbour < seq_count)
            same_set = owners[jnp.clip(neighbour, 0, seq_count - 1)] == own_set
            visible.append((in_range & same_set).astype(jnp.float32))
        keys_cat = jnp.concatenate(key_list, axis=0)
        values_cat = jnp.concatenate(value_list, axis=0)
        mask_row = jnp.repeat(jnp.stack(visible), view_tok)
        scores = (
            jnp.einsum("qhd,khd->hqk", queries, keys_cat, preferred_element_type=jnp.float32)
            * score_scale
        )
        exponent = jnp.exp(scores) * mask_row
        denominator = jnp.sum(exponent, axis=-1)
        numerator = jnp.einsum(
            "hqk,khd->qhd",
            exponent.astype(jnp.bfloat16),
            values_cat,
            preferred_element_type=jnp.float32,
        )
        attended = (
            (numerator / jnp.transpose(denominator)[:, :, None])
            .astype(jnp.bfloat16)
            .reshape(view_tok, local_width)
        )
        mixed_out = jnp.dot(
            lax.all_gather(attended, "tp", axis=1, tiled=True),
            out_rows,
            preferred_element_type=jnp.float32,
        )
        gating = set_gate[0, micro_index, own_set].astype(jnp.float32)
        result = (widened + gating * mixed_out).astype(jnp.bfloat16)
        in_range = (micro_raw >= 0) & (micro_raw < micro_count)
        hidden = jnp.where(in_range, hidden.at[micro_index].set(result), hidden)
        if moment + 1 < ticks:
            carried = shifted(result, "section", 1)
    return hidden[None]


def solution(mesh):
    placed = (
        P("groups", "seq", "tp"),
        P("groups", None),
        P("section", "groups", None, None, "tp"),
        P("section", "groups", None, "tp"),
        P("section", "seq", None, "tp"),
        P("section", None, None),
        P("section", None, "tp"),
    )
    return jax.shard_map(
        body,
        mesh=mesh,
        in_specs=placed,
        out_specs=P("section", "groups", "seq", "tp"),
        check_vma=False,
    )
```

profile of v0, /device:TPU:11, one launch (start us, length us, event | category | flops | bytes accessed | tf_op | source)
XLA Modules:
  0.0 267.1 jit_solution(7791036206823551094)
XLA Ops:
  25.9 111.5 %all-gather.3.cloned.1.call-done = bf16[1,1536,3,1536]{3,1,2,0:T(8,128)(2,1)} async-done(((bf16[1,192,3,1536]{3,1,2,0:T(8,128)(2,1)}), bf16[1,1536,3,1536]{3,1,2,0:T(8,128)(2,1)}) %all-gather.3.cloned.1.call-update) | async-done | bytes 14155792 | tf_op jit(solution)/shard_map/all_gather | solution.py:48
  137.5 18.7 %copy.58 = bf16[1,1536,3,1536]{1,3,2,0:T(8,128)(2,1)} copy(bf16[1,1536,3,1536]{3,1,2,0:T(8,128)(2,1)} %all-gather.3.cloned.1.call-done) | data formatting | bytes 28311552 | tf_op jit(solution)/shard_map/all_gather | solution.py:48
  156.1 7.5 %fusion.129 = f32[64,3,12,128]{3,0,2,1:T(8,128)S(1)} fusion(bf16[3,12,128,1536]{3,2,1,0:T(8,128)(2,1)} %bitcast.253, f32[1536]{0:T(1024)S(1)} %get-tuple-element.59, f32[1536]{0:T(1024)S(1)} %get-tuple-element.58, f32[64]{0:T(128)S(1)} %get-tuple-element.102, f32[64]{0:T(128)S(1)} %get-tuple-element.101, bf16[2,64,1536]{2,1,0:T(8,128)(2,1)S(1)} %copy-done.6, ...), kind=kOutput, calls=%fused_computation.139 | convolution fusion | flops 906657792 | bytes 15549441 | tf_op jit(solution)/shard_map/dot_general | solution.py:74
  166.5 2.3 collective-permute-start.1
  168.8 4.0 %collective-permute-start = (bf16[2,64,1536]{2,1,0:T(8,128)(2,1)S(1)}, bf16[2,64,1536]{2,1,0:T(8,128)(2,1)S(1)}, u32[]{:S(2)}, u32[]{:S(2)}) collective-permute-start(bf16[2,64,1536]{2,1,0:T(8,128)(2,1)S(1)} %pad_maximum_fusion), channel_id=1, source_target_pairs={{0,2},{2,4},{4,6},{6,8},{8,10},{10,12},{12,14},{1,3},{3,5},{5,7},{... | collective-permute-start | bytes 1179656 | tf_op jit(solution)/shard_map/ppermute | solution.py:15
  173.6 2.9 %collective-permute-done.1 = bf16[2,64,1536]{2,1,0:T(8,128)(2,1)S(1)} collective-permute-done((bf16[2,64,1536]{2,1,0:T(8,128)(2,1)S(1)}, bf16[2,64,1536]{2,1,0:T(8,128)(2,1)S(1)}, u32[]{:S(2)}, u32[]{:S(2)}) %collective-permute-start.1) | collective-permute-done | bytes 393248 | tf_op jit(solution)/shard_map/ppermute | solution.py:15
  179.7 3.9 %bitcast_dynamic-update-slice_fusion = (bf16[2,64,1536]{2,1,0:T(8,128)(2,1)S(1)}, bf16[64,1536]{1,0:T(8,128)(2,1)S(1)}) fusion(bf16[2,64,1536]{2,1,0:T(8,128)(2,1)S(1)} %broadcast_in_dim.16, s32[]{:T(128)} %min.31, pred[]{:T(512)} %get-tuple-element.90, pred[]{:T(512)S(6)} %and.71, bf16[1,1536,1536]{2,1,0:T(8,128)(2,1)} %param.19, ...), kind=kOutput, calls=%fused_computation.148 | convolution fusion | flops 302678016 | bytes 5513223 | tf_op jit(solution)/shard_map/dot_general | solution.py:120
  183.6 1.3 collective-permute-start.2
  188.7 1.4 collective-permute-done.2
  190.2 7.6 %fusion.126 = f32[64,3,12,128]{3,0,2,1:T(8,128)S(1)} fusion(bf16[3,12,128,1536]{3,2,1,0:T(8,128)(2,1)} %bitcast.254, bf16[64,1536]{1,0:T(8,128)(2,1)S(1)} %get-tuple-element.63, f32[1536]{0:T(1024)S(1)} %get-tuple-element.57, f32[1536]{0:T(1024)S(1)} %get-tuple-element.56, f32[64]{0:T(128)S(1)} %get-tuple-element.96, f32[64]{0:T(128)S(1)} %get-tuple-element.95), kind=kOutput, calls=%fused_computation.137 | convolution fusion | flops 906559488 | bytes 15544832 | tf_op jit(solution)/shard_map/dot_general | solution.py:74
  201.7 6.6 %collective-permute-start.4 = (bf16[2,64,1536]{2,1,0:T(8,128)(2,1)S(1)}, bf16[2,64,1536]{2,1,0:T(8,128)(2,1)S(1)}, u32[]{:S(2)}, u32[]{:S(2)}) collective-permute-start(bf16[2,64,1536]{2,1,0:T(8,128)(2,1)S(1)} %pad_maximum_fusion.1), channel_id=1, source_target_pairs={{2,0},{4,2},{6,4},{8,6},{10,8},{12,10},{14,12},{3,1},{5,3},{7,5},{... | collective-permute-start | bytes 1179656 | tf_op jit(solution)/shard_map/ppermute | solution.py:15
  208.3 1.9 collective-permute-start.3
  211.1 2.6 collective-permute-done.4
  215.0 1.0 fusion.167
  216.5 1.6 fusion.175
  218.4 4.0 %fusion.121 = (bf16[2,64,1536]{2,1,0:T(8,128)(2,1)S(1)}, bf16[64,1536]{1,0:T(8,128)(2,1)S(1)}) fusion(bf16[2,64,1536]{2,1,0:T(8,128)(2,1)S(1)} %get-tuple-element.107, s32[]{:T(128)} %min.36, pred[]{:T(512)} %get-tuple-element.61, pred[]{:T(512)S(6)} %and.79, bf16[1,1536,1536]{2,1,0:T(8,128)(2,1)} %param.19, bf16[12,8,8,128]{3,2,1,0:T(8,128)(2,1)S(1)} %fusion.61, ...), kind=kOutput, calls=%fused_computation.133 | convolution fusion | flops 302579712 | bytes 5709830 | tf_op jit(solution)/shard_map/dot_general | solution.py:120
  222.4 1.5 collective-permute-start.5
  224.9 3.9 %collective-permute-done.5 = bf16[64,1536]{1,0:T(8,128)(2,1)S(1)} collective-permute-done((bf16[64,1536]{1,0:T(8,128)(2,1)S(1)}, bf16[64,1536]{1,0:T(8,128)(2,1)S(1)}, u32[]{:S(2)}, u32[]{:S(2)}) %collective-permute-start.5) | collective-permute-done | bytes 196640 | tf_op jit(solution)/shard_map/ppermute | solution.py:15
  229.0 7.6 %fusion.123 = f32[64,3,12,128]{3,0,2,1:T(8,128)S(1)} fusion(bf16[3,12,128,1536]{3,2,1,0:T(8,128)(2,1)} %bitcast.255, bf16[64,1536]{1,0:T(8,128)(2,1)S(1)} %get-tuple-element.62, f32[1536]{0:T(1024)S(1)} %get-tuple-element.55, f32[1536]{0:T(1024)S(1)} %get-tuple-element.54, f32[64]{0:T(128)S(1)} %get-tuple-element.89, f32[64]{0:T(128)S(1)} %get-tuple-element.88), kind=kOutput, calls=%fused_computation.135 | convolution fusion | flops 906559488 | bytes 15544832 | tf_op jit(solution)/shard_map/dot_general | solution.py:74
  239.4 5.8 %collective-permute-start.7 = (bf16[2,64,1536]{2,1,0:T(8,128)(2,1)S(1)}, bf16[2,64,1536]{2,1,0:T(8,128)(2,1)S(1)}, u32[]{:S(2)}, u32[]{:S(2)}) collective-permute-start(bf16[2,64,1536]{2,1,0:T(8,128)(2,1)S(1)} %pad_maximum_fusion.2), channel_id=1, source_target_pairs={{2,0},{4,2},{6,4},{8,6},{10,8},{12,10},{14,12},{3,1},{5,3},{7,5},{... | collective-permute-start | bytes 1179656 | tf_op jit(solution)/shard_map/ppermute | solution.py:15
  245.2 1.9 collective-permute-start.6
  248.0 2.9 %collective-permute-done.7 = bf16[2,64,1536]{2,1,0:T(8,128)(2,1)S(1)} collective-permute-done((bf16[2,64,1536]{2,1,0:T(8,128)(2,1)S(1)}, bf16[2,64,1536]{2,1,0:T(8,128)(2,1)S(1)}, u32[]{:S(2)}, u32[]{:S(2)}) %collective-permute-start.7) | collective-permute-done | bytes 393248 | tf_op jit(solution)/shard_map/ppermute | solution.py:15
  253.7 1.6 fusion.176
  255.6 4.6 %fusion.45 = bf16[1,2,64,1536]{3,2,1,0:T(8,128)(2,1)} fusion(bf16[1,2,64,1536]{3,2,1,0:T(8,128)(2,1)} %copy.110, s32[]{:T(128)} %min.38, bf16[1,1536,1536]{2,1,0:T(8,128)(2,1)} %param.19, bf16[64,1536]{1,0:T(8,128)(2,1)S(1)} %get-tuple-element.62, bf16[12,8,8,128]{3,2,1,0:T(8,128)(2,1)S(1)} %fusion.62, bf16[2,64,1536]{2,1,0:T(8,128)(2,1)S(1)} %get-tuple-element.109, ...), kind=kOutput, calls=%fused_computation.19 | convolution fusion | flops 302579712 | bytes 5512193 | tf_op jit(solution)/shard_map/dot_general | solution.py:120
  (166 shorter events, 27.3 us)
Async XLA Ops:
  6.5 17.4 %copy-start.17 = (s32[3]{0:T(128)S(1)}, s32[3]{0:T(128)}, u32[]{:S(2)}) copy-start(s32[3]{0:T(128)} %constant.115.clone.1) | copy-start | bytes 40
  6.5 17.3 %copy-start.14 = (bf16[1,2,6,1536]{3,1,2,0:T(2,128)(2,1)S(1)}, bf16[1,2,6,1536]{3,1,2,0:T(2,128)(2,1)}, u32[]{:S(2)}) copy-start(bf16[1,2,6,1536]{3,1,2,0:T(2,128)(2,1)} %param.16) | copy-start | bytes 110596
  6.5 19.1 %copy-start.6 = (bf16[2,64,1536]{2,1,0:T(8,128)(2,1)S(1)}, bf16[2,64,1536]{2,1,0:T(8,128)(2,1)}, u32[]{:S(2)}) copy-start(bf16[2,64,1536]{2,1,0:T(8,128)(2,1)} %param.13) | copy-start | bytes 1179652
  6.5 19.4 %copy-start.16 = (f32[1,2,128]{2,1,0:T(2,128)S(1)}, f32[1,2,128]{2,1,0:T(2,128)}, u32[]{:S(2)}) copy-start(f32[1,2,128]{2,1,0:T(2,128)} %param.18) | copy-start | bytes 3076
  6.5 130.9 %all-gather.3.cloned.1.call-start = ((), (), s32[]{:S(2)}) async-start(), calls=%async_computation | async-start | bytes 15925248 | tf_op jit(solution)/shard_map/all_gather | solution.py:48
  163.7 1.1 copy-start.2
  166.3 6.5 %copy-start.3 = (f32[64,3,12,128]{3,0,2,1:T(8,128)S(1)}, f32[64,3,12,128]{3,0,2,1:T(8,128)}, u32[]{:S(2)}) copy-start(f32[64,3,12,128]{3,0,2,1:T(8,128)} %copy-done.2) | copy-start | bytes 3538948
  166.5 10.1 %collective-permute-start.1 = (bf16[2,64,1536]{2,1,0:T(8,128)(2,1)S(1)}, bf16[2,64,1536]{2,1,0:T(8,128)(2,1)S(1)}, u32[]{:S(2)}, u32[]{:S(2)}) collective-permute-start(bf16[2,64,1536]{2,1,0:T(8,128)(2,1)S(1)} %pad_maximum_fusion), channel_id=1, source_target_pairs={{2,0},{4,2},{6,4},{8,6},{10,8},{12,10},{14,12},{3,1},{5,3},{7,5},{... | collective-permute-start | bytes 1179656 | tf_op jit(solution)/shard_map/ppermute | solution.py:15
  168.8 8.7 %collective-permute-start = (bf16[2,64,1536]{2,1,0:T(8,128)(2,1)S(1)}, bf16[2,64,1536]{2,1,0:T(8,128)(2,1)S(1)}, u32[]{:S(2)}, u32[]{:S(2)}) collective-permute-start(bf16[2,64,1536]{2,1,0:T(8,128)(2,1)S(1)} %pad_maximum_fusion), channel_id=1, source_target_pairs={{0,2},{2,4},{4,6},{6,8},{8,10},{10,12},{12,14},{1,3},{3,5},{5,7},{... | collective-permute-start | bytes 1179656 | tf_op jit(solution)/shard_map/ppermute | solution.py:15
  183.6 6.4 %collective-permute-start.2 = (bf16[64,1536]{1,0:T(8,128)(2,1)S(1)}, bf16[64,1536]{1,0:T(8,128)(2,1)S(1)}, u32[]{:S(2)}, u32[]{:S(2)}) collective-permute-start(bf16[64,1536]{1,0:T(8,128)(2,1)S(1)} %get-tuple-element.108), channel_id=1, source_target_pairs={{0,1},{2,3},{4,5},{6,7},{8,9},{10,11},{12,13},{14,15},{16,17},{18,... | collective-permute-start | bytes 589832 | tf_op jit(solution)/shard_map/ppermute | solution.py:15
  197.8 1.1 copy-start.4
  198.9 1.1 slice-start.2
  200.5 9.8 %copy-start.5 = (f32[64,3,12,128]{3,0,2,1:T(8,128)S(1)}, f32[64,3,12,128]{3,0,2,1:T(8,128)}, u32[]{:S(2)}) copy-start(f32[64,3,12,128]{3,0,2,1:T(8,128)} %copy-done.4) | copy-start | bytes 3538948
  201.7 12.0 %collective-permute-start.4 = (bf16[2,64,1536]{2,1,0:T(8,128)(2,1)S(1)}, bf16[2,64,1536]{2,1,0:T(8,128)(2,1)S(1)}, u32[]{:S(2)}, u32[]{:S(2)}) collective-permute-start(bf16[2,64,1536]{2,1,0:T(8,128)(2,1)S(1)} %pad_maximum_fusion.1), channel_id=1, source_target_pairs={{2,0},{4,2},{6,4},{8,6},{10,8},{12,10},{14,12},{3,1},{5,3},{7,5},{... | collective-permute-start | bytes 1179656 | tf_op jit(solution)/shard_map/ppermute | solution.py:15
  208.3 6.6 %collective-permute-start.3 = (bf16[2,64,1536]{2,1,0:T(8,128)(2,1)S(1)}, bf16[2,64,1536]{2,1,0:T(8,128)(2,1)}, u32[]{:S(2)}, u32[]{:S(2)}) collective-permute-start(bf16[2,64,1536]{2,1,0:T(8,128)(2,1)S(1)} %pad_maximum_fusion.1), channel_id=1, source_target_pairs={{0,2},{2,4},{4,6},{6,8},{8,10},{10,12},{12,14},{1,3},{3,5},{5,7},{... | collective-permute-start | bytes 1179656 | tf_op jit(solution)/shard_map/ppermute | solution.py:15
  216.5 1.6 copy-start.9
  216.5 1.6 copy-start.12
  222.4 6.4 %collective-permute-start.5 = (bf16[64,1536]{1,0:T(8,128)(2,1)S(1)}, bf16[64,1536]{1,0:T(8,128)(2,1)S(1)}, u32[]{:S(2)}, u32[]{:S(2)}) collective-permute-start(bf16[64,1536]{1,0:T(8,128)(2,1)S(1)} %get-tuple-element.110), channel_id=1, source_target_pairs={{0,1},{2,3},{4,5},{6,7},{8,9},{10,11},{12,13},{14,15},{16,17},{18,... | collective-permute-start | bytes 589832 | tf_op jit(solution)/shard_map/ppermute | solution.py:15
  236.6 1.1 copy-start
  239.2 7.9 %copy-start.1 = (f32[64,3,12,128]{3,0,2,1:T(8,128)S(1)}, f32[64,3,12,128]{3,0,2,1:T(8,128)}, u32[]{:S(2)}) copy-start(f32[64,3,12,128]{3,0,2,1:T(8,128)} %copy-done) | copy-start | bytes 3538948
  239.4 11.5 %collective-permute-start.7 = (bf16[2,64,1536]{2,1,0:T(8,128)(2,1)S(1)}, bf16[2,64,1536]{2,1,0:T(8,128)(2,1)S(1)}, u32[]{:S(2)}, u32[]{:S(2)}) collective-permute-start(bf16[2,64,1536]{2,1,0:T(8,128)(2,1)S(1)} %pad_maximum_fusion.2), channel_id=1, source_target_pairs={{2,0},{4,2},{6,4},{8,6},{10,8},{12,10},{14,12},{3,1},{5,3},{7,5},{... | collective-permute-start | bytes 1179656 | tf_op jit(solution)/shard_map/ppermute | solution.py:15
  245.2 7.5 %collective-permute-start.6 = (bf16[2,64,1536]{2,1,0:T(8,128)(2,1)S(1)}, bf16[2,64,1536]{2,1,0:T(8,128)(2,1)S(1)}, u32[]{:S(2)}, u32[]{:S(2)}) collective-permute-start(bf16[2,64,1536]{2,1,0:T(8,128)(2,1)S(1)} %pad_maximum_fusion.2), channel_id=1, source_target_pairs={{0,2},{2,4},{4,6},{6,8},{8,10},{10,12},{12,14},{1,3},{3,5},{5,7},{... | collective-permute-start | bytes 1179656 | tf_op jit(solution)/shard_map/ppermute | solution.py:15
  253.7 1.6 copy-start.8
  253.7 1.6 copy-start.10
  (6 other events, 5.6 us)
Sparse Core Ops, SparseCore 0:
  9.0 128.4 all-gather.2
where the time goes:
time: 269 us; the launch traced here: 267 us
  waiting for transfers between devices  126 us (47%)
  matrix products  40 us (15%)
  local copies, waits for them, and re-layouts  35.9 us (13%)
  between operations  31.1 us (12%)
  starting transfers between devices  25.3 us (9%)
  other arithmetic  8.29 us (3%)
    all_gather x1, waiting for transfers between devices, body(): whole_qkv = lax.all_gather(qkv_weight[0], 'seq', axis=0, tiled=True)  112 us
    ppermute x8, starting transfers between devices, shifted(): return lax.ppermute(array, axis, pairs)  25.3 us
    dot_general x3, matrix products, body(): jnp.dot(lax.all_gather(normed, 'tp', axis=1, tiled=True), qkv_flat, prefe...  22.7 us
    all_gather x1, local copies, waits for them, and re-layouts, body(): whole_qkv = lax.all_gather(qkv_weight[0], 'seq', axis=0, tiled=True)  18.7 us
    ppermute x8, waiting for transfers between devices, shifted(): return lax.ppermute(array, axis, pairs)  14.3 us
    dot_general x3, matrix products, body(): jnp.dot(lax.all_gather(attended, 'tp', axis=1, tiled=True), out_rows, pre...  12.5 us
  transfers between devices with their start and end apart: 9, of which 8 were waited for; matrix products, arithmetic and copies ran while one was open for 5% of the time, Pallas kernels for 0%

commit v1 on v0

--- a/solution.py
+++ b/solution.py
@@ -1,12 +1,375 @@
+import functools
+
 import jax
 import jax.numpy as jnp
 from jax import lax
+from jax.experimental import pallas as pl
+from jax.experimental.pallas import tpu as pltpu
 from jax.sharding import PartitionSpec as P
 
 REACH = 1
 
 
 epsilon = 1e-06
+
+
+def view_sets(set_views, count):
+    amount = set_views.shape[0]
+    before = jnp.arange(amount)[:, None] > jnp.arange(amount)[None, :]
+    starts = jnp.sum(jnp.where(before, set_views[None, :], 0), axis=1)
+    position = jnp.arange(count, dtype=jnp.int32)
+    inside = (starts[None, :] <= position[:, None]).astype(jnp.int32)
+    return jnp.sum(inside, axis=1) - 1
+
+
+def attend_kernel(
+    table,
+    own,
+    pair,
+    halo,
+    pair_halo,
+    modulation,
+    gains,
+    home,
+    home_pair,
+    o_first,
+    o_mid1,
+    o_end1,
+    o_mid2,
+    o_end2,
+    d_first,
+    d_mid1,
+    d_end1,
+    d_mid2,
+    d_end2,
+    att_own,
+    att_pair,
+    weights,
+    normed,
+    sems,
+):
+    micro_count, view_tok, width = own.shape
+    rows = weights.shape[0] // 8
+    part = weights.shape[1] // 3
+    head = gains.shape[1]
+    middle = table[0]
+
+    def piece(source, index):
+        start = pl.multiple_of(table[1 + index] * rows, rows)
+        return pltpu.make_async_copy(
+            source, weights.at[pl.ds(start, rows), :], sems.at[index]
+        )
+
+    def load(index, mid, end):
+        @pl.when(middle == 1)
+        def _():
+            piece(mid, index).start()
+
+        @pl.when(middle == 0)
+        def _():
+            piece(end, index).start()
+
+    piece(home, 0).start()
+    piece(home_pair, 1).start()
+    piece(o_first, 2).start()
+    piece(d_first, 3).start()
+    load(4, o_mid1, o_end1)
+    load(5, d_mid1, d_end1)
+    load(6, o_mid2, o_end2)
+    load(7, d_mid2, d_end2)
+
+    half = 2 * micro_count * view_tok
+    for slot, source in enumerate((own, pair, halo, pair_halo)):
+        for m in range(micro_count):
+            wide = source[m].astype(jnp.float32)
+            average = jnp.mean(wide, axis=-1, keepdims=True)
+            squares = jnp.mean(wide * wide, axis=-1, keepdims=True)
+            spread = squares - average * average
+            factors = modulation[m, table[9 + 4 * m + slot]].astype(jnp.float32)
+            value = (wide - average) * lax.rsqrt(spread + epsilon) * (
+                1.0 + factors[1:2]
+            ) + factors[0:1]
+            first = half * (slot // 2) + (2 * m + slot % 2) * view_tok
+            normed[first : first + view_tok, :] = value.astype(jnp.bfloat16)
+
+    for index in range(8):
+        piece(home, index).wait()
+
+    two = 2 * view_tok
+    low_row = lax.broadcasted_iota(jnp.int32, (two, two), 0) < view_tok
+    low_col = lax.broadcasted_iota(jnp.int32, (two, two), 1) < view_tok
+    near_masks, far_masks = [], []
+    for m in range(micro_count):
+        base = 9 + 4 * micro_count + 3 * m
+        together = jnp.where(table[base] == 1, 1.0, 0.0)
+        below = jnp.where(table[base + 1] == 1, 1.0, 0.0)
+        above = jnp.where(table[base + 2] == 1, 1.0, 0.0)
+        near_masks.append(jnp.where(low_row == low_col, 1.0, together))
+        far_masks.append(
+            jnp.where(
+                low_row & low_col,
+                below,
+                jnp.where(low_row | low_col, 0.0, above),
+            )
+        )
+
+    def unit(values, gain):
+        return (
+            values
+            * lax.rsqrt(jnp.mean(values * values, axis=-1, keepdims=True) + epsilon)
+            * gain
+        ).astype(jnp.bfloat16)
+
+    def dot(a, b):
+        return jnp.dot(a, b, preferred_element_type=jnp.float32)
+
+    def dot_t(a, b):
+        return lax.dot_general(
+            a, b, (((1,), (1,)), ((), ())), preferred_element_type=jnp.float32
+        )
+
+    query_gain = gains[0:1, :]
+    key_gain = gains[1:2, :]
+    block = 2 * head
+
+    def heads(step, carry):
+        offset = pl.multiple_of(step * block, block)
+        raw_q = dot(normed[0:half, :], weights[:, pl.ds(offset, block)])
+        raw_k = dot(normed[...], weights[:, pl.ds(part + offset, block)])
+        raw_v = dot(normed[...], weights[:, pl.ds(2 * part + offset, block)])
+        outs = [[None] * 2 for _ in range(micro_count)]
+        for i in range(2):
+            cols = slice(i * head, (i + 1) * head)
+            queries = unit(raw_q[:, cols], query_gain)
+            keys = unit(raw_k[:, cols], key_gain)
+            values = raw_v[:, cols].astype(jnp.bfloat16)
+            for m in range(micro_count):
+                near = slice(m * two, (m + 1) * two)
+                far = slice(half + m * two, half + (m + 1) * two)
+                q = queries[near]
+                scale = head ** (-0.5)
+                e_near = jnp.exp(dot_t(q, keys[near]) * scale) * near_masks[m]
+                e_far = jnp.exp(dot_t(q, keys[far]) * scale) * far_masks[m]
+                total = jnp.sum(e_near, axis=-1, keepdims=True) + jnp.sum(
+                    e_far, axis=-1, keepdims=True
+                )
+                mixed = dot(e_near.astype(jnp.bfloat16), values[near]) + dot(
+                    e_far.astype(jnp.bfloat16), values[far]
+                )
+                outs[m][i] = (mixed / total).astype(jnp.bfloat16)
+        for m in range(micro_count):
+            joined = jnp.concatenate(outs[m], axis=1)
+            att_own[m, :, pl.ds(offset, block)] = joined[:view_tok]
+            att_pair[m, :, pl.ds(offset, block)] = joined[view_tok:]
+        return carry
+
+    lax.fori_loop(0, part // block, heads, 0)
+
+
+def project_kernel(
+    table, att_own, att_got, stream, gates, out_weight, result, weights, sems
+):
+    micro_count, view_tok, part = att_own.shape
+    width = out_weight.shape[1]
+    mine = table[0]
+    blocks = sems.shape[0]
+    block = width // blocks
+
+    def piece(index):
+        return pltpu.make_async_copy(
+            out_weight.at[:, pl.ds(index * block, block)],
+            weights.at[:, pl.ds(index * block, block)],
+            sems.at[index],
+        )
+
+    for index in range(blocks):
+        piece(index).start()
+    tokens = micro_count * view_tok
+    here = att_own[...].reshape(tokens, part)
+    there = att_got[...].reshape(tokens, part)
+    first = pl.multiple_of(mine * part, part)
+    second = pl.multiple_of((1 - mine) * part, part)
+    for index in range(blocks):
+        piece(index).wait()
+        cols = slice(index * block, (index + 1) * block)
+        mixed = jnp.dot(
+            here, weights[pl.ds(first, part), cols], preferred_element_type=jnp.float32
+        ) + jnp.dot(
+            there,
+            weights[pl.ds(second, part), cols],
+            preferred_element_type=jnp.float32,
+        )
+        for m in range(micro_count):
+            gate = gates[m, table[1 + m]][:, cols].astype(jnp.float32)
+            result[m, :, cols] = (
+                stream[m, :, cols].astype(jnp.float32)
+                + gate * mixed[m * view_tok : (m + 1) * view_tok]
+            ).astype(jnp.bfloat16)
+
+
+def paired_body(
+    stream, set_views, modulation, set_gate, qkv_weight, norm_gain, out_weight
+):
+    micro_count, view_tok, width = stream.shape
+    head = norm_gain.shape[2]
+    part = width // 2
+    rows = qkv_weight.shape[1]
+    seq_count = lax.axis_size("seq")
+    section_count = lax.axis_size("section")
+    group = lax.axis_index("groups")
+    place = lax.axis_index("seq")
+    core = place % 2
+    chip = place // 2
+    mine = core ^ group
+    line_axes = ("groups", "seq")
+
+    def along(steps):
+        return [
+            (g * seq_count + 2 * a + c, g * seq_count + 2 * b + c)
+            for g in range(2)
+            for c in range(2)
+            for a, b in steps
+        ]
+
+    def across(chips):
+        return [
+            (g * seq_count + 2 * a + c, (1 - g) * seq_count + 2 * a + 1 - c)
+            for g in range(2)
+            for c in range(2)
+            for a in chips
+        ]
+
+    def send(value, pairs):
+        return lax.ppermute(value, line_axes, pairs)
+
+    swap_cores = [(i, i ^ 1) for i in range(seq_count)]
+    swap_edges = [(i, i + 1) for i in range(1, seq_count - 1, 2)] + [
+        (i + 1, i) for i in range(1, seq_count - 1, 2)
+    ]
+
+    halves = qkv_weight[0].reshape(rows, 3, 2, part)
+    home = lax.dynamic_index_in_dim(halves, mine, 2, False).reshape(rows, 3 * part)
+    lent = lax.dynamic_index_in_dim(halves, 1 - mine, 2, False).reshape(rows, 3 * part)
+
+    o_first = send(home, along([(0, 1), (1, 0), (2, 3), (3, 2)]))
+    o_mid1 = send(home, along([(1, 2), (2, 1)]))
+    home_pair = lax.ppermute(lent, "seq", swap_cores)
+    o_mid2 = send(o_first, along([(1, 2), (2, 1)]))
+    o_end1 = send(o_mid1, along([(1, 0), (2, 3)]))
+    d_first = send(o_first, across(range(4)))
+    d_mid1 = send(o_mid1, across([1, 2]))
+    d_end1 = send(o_end1, across([0, 3]))
+    o_end2 = send(o_mid2, along([(1, 0), (2, 3)]))
+    d_mid2 = send(o_mid2, across([1, 2]))
+    d_end2 = send(o_end2, across([0, 3]))
+
+    middle = ((chip == 1) | (chip == 2)).astype(jnp.int32)
+    first_chip = chip ^ 1
+    second_chip = jnp.where(middle == 1, 3 - chip, chip ^ 2)
+    third_chip = jnp.where(middle == 1, (3 - chip) ^ 1, 3 - chip)
+    order = []
+    for other in (chip, first_chip, second_chip, third_chip):
+        order += [2 * other + core, 2 * other + 1 - core]
+
+    owners = jnp.stack([view_sets(set_views[m], seq_count) for m in range(micro_count)])
+    outward = jnp.where(core == 0, -1, 1)
+    pair_place = place + outward * -1
+    halo_place = place + outward
+    pair_halo_place = pair_place - outward
+    sets, masks = [], []
+
+    def owner(m, where):
+        return owners[m, jnp.clip(where, 0, seq_count - 1)]
+
+    def inside(where):
+        return (where >= 0) & (where < seq_count)
+
+    for m in range(micro_count):
+        own_set, pair_set = owner(m, place), owner(m, pair_place)
+        halo_set, pair_halo_set = owner(m, halo_place), owner(m, pair_halo_place)
+        sets += [own_set, pair_set, halo_set, pair_halo_set]
+        masks += [
+            own_set == pair_set,
+            inside(halo_place) & (own_set == halo_set),
+            inside(pair_halo_place) & (pair_set == pair_halo_set),
+        ]
+    table = jnp.stack(
+        [middle] + order + sets + [m.astype(jnp.int32) for m in masks]
+    ).astype(jnp.int32)
+    gate_table = jnp.stack(
+        [mine] + [owner(m, place) for m in range(micro_count)]
+    ).astype(jnp.int32)
+    gates = set_gate[0][:, :, None, :]
+
+    vmem = pl.BlockSpec(memory_space=pltpu.VMEM)
+    smem = pl.BlockSpec(memory_space=pltpu.SMEM)
+    anywhere = pl.BlockSpec(memory_space=pl.ANY)
+    half_shape = jax.ShapeDtypeStruct((micro_count, view_tok, part), jnp.bfloat16)
+    attend = pl.pallas_call(
+        attend_kernel,
+        out_shape=(half_shape, half_shape),
+        in_specs=[smem] + [vmem] * 6 + [anywhere] * 12,
+        out_specs=(vmem, vmem),
+        scratch_shapes=[
+            pltpu.VMEM((width, 3 * part), jnp.bfloat16),
+            pltpu.VMEM((4 * micro_count * view_tok, width), jnp.bfloat16),
+            pltpu.SemaphoreType.DMA((8,)),
+        ],
+        compiler_params=pltpu.CompilerParams(vmem_limit_bytes=40 * 1024 * 1024),
+        name="attend",
+    )
+    project = pl.pallas_call(
+        project_kernel,
+        out_shape=jax.ShapeDtypeStruct(stream.shape, jnp.bfloat16),
+        in_specs=[smem] + [vmem] * 4 + [anywhere],
+        out_specs=vmem,
+        scratch_shapes=[
+            pltpu.VMEM((width, width), jnp.bfloat16),
+            pltpu.SemaphoreType.DMA((3,)),
+        ],
+        compiler_params=pltpu.CompilerParams(vmem_limit_bytes=24 * 1024 * 1024),
+        name="project",
+    )
+
+    section_place = lax.axis_index("section")
+    own = stream
+    hidden = None
+    for moment in range(section_count):
+        halo = lax.ppermute(own, "seq", swap_edges)
+        pair = lax.ppermute(own, "seq", swap_cores)
+        pair_halo = lax.ppermute(halo, "seq", swap_cores)
+        att_own, att_pair = attend(
+            table,
+            own,
+            pair,
+            halo,
+            pair_halo,
+            modulation[0],
+            norm_gain[0],
+            home,
+            home_pair,
+            o_first,
+            o_mid1,
+            o_end1,
+            o_mid2,
+            o_end2,
+            d_first,
+            d_mid1,
+            d_end1,
+            d_mid2,
+            d_end2,
+        )
+        att_got = lax.ppermute(att_pair, "seq", swap_cores)
+        result = project(gate_table, att_own, att_got, own, gates, out_weight[0])
+        if moment == 0:
+            hidden = result
+        else:
+            hidden = jnp.where(section_place == moment, result, hidden)
+        if moment + 1 < section_count:
+            own = lax.ppermute(
+                result, "section", [(i, i + 1) for i in range(section_count - 1)]
+            )
+    return hidden[None]
 
 
 def shifted(array, axis, by):
@@ -15,28 +378,17 @@
     return lax.ppermute(array, axis, pairs)
 
 
-def view_sets(set_views, count):
-    starts = jnp.cumsum(set_views) - set_views
-    position = jnp.arange(count, dtype=jnp.int32)
-    inside = (starts[None, :] <= position[:, None]).astype(jnp.int32)
-    return jnp.sum(inside, axis=1) - 1
-
-
 def unit_rms(values, scaling):
-    return values * lax.rsqrt(jnp.mean(values * values, axis=-1, keepdims=True) + epsilon) * scaling
-
-
-def relay_cycle(payload):
-    moving = payload
-    moving = shifted(moving, "seq", 1)
-    below_list = [moving]
-    moving = payload
-    moving = shifted(moving, "seq", -1)
-    above_list = [moving]
-    return below_list[::-1] + [payload] + above_list
-
-
-def body(stream, set_views, modulation, set_gate, qkv_weight, norm_gain, out_weight):
+    return (
+        values
+        * lax.rsqrt(jnp.mean(values * values, axis=-1, keepdims=True) + epsilon)
+        * scaling
+    )
+
+
+def general_body(
+    stream, set_views, modulation, set_gate, qkv_weight, norm_gain, out_weight
+):
     micro_count, view_tok, local_width = stream.shape
     head_size = norm_gain.shape[2]
     head_count = local_width // head_size
@@ -69,28 +421,27 @@
         spread = (squares / full_width)[:, None] - average * average
         factors = modulation[0, micro_index, own_set].astype(jnp.float32)
         normed = (
-            (widened - average) * lax.rsqrt(spread + epsilon) * (1.0 + factors[1]) + factors[0]
+            (widened - average) * lax.rsqrt(spread + epsilon) * (1.0 + factors[1])
+            + factors[0]
         ).astype(jnp.bfloat16)
-        section_projected = jnp.dot(
+        projected = jnp.dot(
             lax.all_gather(normed, "tp", axis=1, tiled=True),
             qkv_flat,
             preferred_element_type=jnp.float32,
         )
-        queries = unit_rms(
-            section_projected.reshape(view_tok, 3, head_count, head_size)[:, 0], gain_pair[0]
-        ).astype(jnp.bfloat16)
-        parts = section_projected.reshape(view_tok, 3, head_count, head_size)
+        parts = projected.reshape(view_tok, 3, head_count, head_size)
+        queries = unit_rms(parts[:, 0], gain_pair[0]).astype(jnp.bfloat16)
         keys_here = unit_rms(parts[:, 1], gain_pair[1]).astype(jnp.bfloat16)
         values_here = parts[:, 2].astype(jnp.bfloat16)
-        key_list = []
-        value_list = []
-        stacked = jnp.stack(
-            [keys_here.reshape(view_tok, local_width), values_here.reshape(view_tok, local_width)]
-        )
-        arrived = relay_cycle(stacked)
-        for received in arrived:
-            key_list.append(received[0].reshape(view_tok, head_count, head_size))
-            value_list.append(received[1].reshape(view_tok, head_count, head_size))
+        payload = jnp.stack(
+            [
+                keys_here.reshape(view_tok, local_width),
+                values_here.reshape(view_tok, local_width),
+            ]
+        )
+        arrived = [shifted(payload, "seq", 1), payload, shifted(payload, "seq", -1)]
+        key_list = [r[0].reshape(view_tok, head_count, head_size) for r in arrived]
+        value_list = [r[1].reshape(view_tok, head_count, head_size) for r in arrived]
         visible = []
         for offset in offsets:
             neighbour = seq_place + offset
@@ -101,7 +452,9 @@
         values_cat = jnp.concatenate(value_list, axis=0)
         mask_row = jnp.repeat(jnp.stack(visible), view_tok)
         scores = (
-            jnp.einsum("qhd,khd->hqk", queries, keys_cat, preferred_element_type=jnp.float32)
+            jnp.einsum(
+                "qhd,khd->hqk", queries, keys_cat, preferred_element_type=jnp.float32
+            )
             * score_scale
         )
         exponent = jnp.exp(scores) * mask_row
@@ -141,8 +494,10 @@
         P("section", None, None),
         P("section", None, "tp"),
     )
+    sizes = mesh.shape
+    paired = sizes["tp"] == 1 and sizes["groups"] == 2 and sizes["seq"] == 8
     return jax.shard_map(
-        body,
+        paired_body if paired else general_body,
         mesh=mesh,
         in_specs=placed,
         out_specs=P("section", "groups", "seq", "tp"),

time: 269 us -> 206 us (0.77)
  matrix products: 40 us -> 0 us
  waiting for transfers between devices: 126 us -> 90.2 us
  starting transfers between devices: 25.3 us -> 53 us
  Pallas kernels: 0 us -> 26.3 us
  between operations: 31.1 us -> 7.73 us
  local copies, waits for them, and re-layouts: 35.9 us -> 23.9 us
  other arithmetic: 8.29 us -> 2.57 us
    all_gather x1 -> x0, waiting for transfers between devices: 112 us -> none  [body(): whole_qkv = lax.all_gather(qkv_weight[0], 'seq', axis=0, tiled=True)]
    ppermute x8 -> x20, waiting for transfers between devices: 14.3 us -> 90.2 us  [the longest x10 65.6 us: send(): return lax.ppermute(value, line_axes, pairs)]
    dot_general x12 -> x0, matrix products: 40 us -> none  [the longest x3 22.7 us: body(): jnp.dot(lax.all_gather(normed, 'tp', axis=1, tiled=True), qkv_flat, prefe...]
    ppermute x8 -> x20, starting transfers between devices: 25.3 us -> 53 us  [the longest x10 22.1 us: send(): return lax.ppermute(value, line_axes, pairs)]
    pallas_call x0 -> x4, Pallas kernels: none -> 26.3 us  [the longest x2 21.7 us: paired_body(): attend(table, own, pair, halo, pair_halo, modulation[0], norm_gain[0], ho...]
    all_gather x1 -> x0, local copies, waits for them, and re-layouts: 18.7 us -> none  [body(): whole_qkv = lax.all_gather(qkv_weight[0], 'seq', axis=0, tiled=True)]
    unnamed x40 -> x36, local copies, waits for them, and re-layouts: 2.32 us -> 10.5 us
    another operation x24 -> x3, local copies, waits for them, and re-layouts: 4.45 us -> 9.05 us  [the longest x1 5.03 us: paired_body(): jnp.stack([middle] + order + sets + [m.astype(jnp.int32) for m in masks])]
  transfers between devices with their start and end apart: 9 -> 20, of which waited for: 8 -> 10; matrix products, arithmetic and copies ran while one was open for 5% -> 5% of each run, Pallas kernels for 0% -> 0%
where the time goes in v1:
time: 206 us; the launch traced here: 204 us
  waiting for transfers between devices  90.2 us (44%)
  starting transfers between devices  53 us (26%)
  Pallas kernels  26.3 us (13%)
  local copies, waits for them, and re-layouts  23.9 us (12%)
  between operations  7.73 us (4%)
  other arithmetic  2.57 us (1%)
    ppermute x10, waiting for transfers between devices, send(): return lax.ppermute(value, line_axes, pairs)  65.6 us
    ppermute x10, starting transfers between devices, send(): return lax.ppermute(value, line_axes, pairs)  22.1 us
    pallas_call x2, Pallas kernels, paired_body(): attend(table, own, pair, halo, pair_halo, modulation[0], norm_gain[0], ho...  21.7 us
    ppermute x2, starting transfers between devices, paired_body(): pair_halo = lax.ppermute(halo, 'seq', swap_cores)  17.2 us
    ppermute x2, waiting for transfers between devices, paired_body(): halo = lax.ppermute(own, 'seq', swap_edges)  11.1 us
    ppermute x1, waiting for transfers between devices, paired_body(): lax.ppermute(result, 'section', [(i, i + 1) for i in range(section_count...  10.8 us
    unnamed x36, local copies, waits for them, and re-layouts  10.5 us
    ppermute x2, starting transfers between devices, paired_body(): halo = lax.ppermute(own, 'seq', swap_edges)  9.61 us
  transfers between devices with their start and end apart: 20, of which 10 were waited for; matrix products, arithmetic and copies ran while one was open for 5% of the time, Pallas kernels for 0%

profile of v1, /device:TPU:11, one launch (start us, length us, event | category | flops | bytes accessed | tf_op | source)
XLA Modules:
  0.0 203.7 jit_solution(13327951759217087164)
XLA Ops:
  0.0 4.0 %reshape_squeeze.3 = bf16[192,3,2,768]{3,2,0,1:T(2,128)(2,1)S(1)} reshape(bf16[1,192,3,1536]{3,1,2,0:T(8,128)(2,1)} %param.11) | data formatting | bytes 3538944 | tf_op jit(solution)/shard_map/reshape;squeeze | solution.py:250
  4.0 3.6 %constant_dynamic-slice_fusion = (bf16[192,3,1,768]{3,2,0,1:T(2,128)(2,1)S(1)}, bf16[192,3,1,768]{3,2,0,1:T(2,128)(2,1)S(1)}) fusion(bf16[192,3,2,768]{3,2,0,1:T(2,128)(2,1)S(1)} %reshape_squeeze.3, s32[]{:T(128)S(6)} %select_n.62, s32[]{:T(128)S(6)} %select_n.61), kind=kLoop, calls=%fused_computation.8 | loop fusion | bytes 3538952 | tf_op jit(solution)/shard_map/jit(dynamic_index_in_dim)/dynamic_slice | solution.py:252
  9.2 4.3 %collective-permute-start.5 = (bf16[192,2304]{1,0:T(8,128)(2,1)S(1)}, bf16[192,2304]{1,0:T(8,128)(2,1)S(1)}, u32[]{:S(2)}, u32[]{:S(2)}) collective-permute-start(bf16[192,2304]{1,0:T(8,128)(2,1)S(1)} %bitcast.59), channel_id=1, source_target_pairs={{4,8},{8,4},{6,10},{10,6},{20,24},{24,20},{22,26},{26,22},{5,9},{9... | collective-permute-start | bytes 2654216 | tf_op jit(solution)/shard_map/ppermute | solution.py:243
  13.5 16.0 %collective-permute-done.4.o_first = bf16[192,2304]{1,0:T(8,128)(2,1)S(1)} collective-permute-done((bf16[192,2304]{1,0:T(8,128)(2,1)S(1)}, bf16[192,2304]{1,0:T(8,128)(2,1)S(1)}, u32[]{:S(2)}, u32[]{:S(2)}) %collective-permute-start.4) | collective-permute-done | bytes 884768 | tf_op jit(solution)/shard_map/ppermute | solution.py:243
  29.6 3.2 %collective-permute-start.7 = (bf16[192,2304]{1,0:T(8,128)(2,1)S(1)}, bf16[192,2304]{1,0:T(8,128)(2,1)S(1)}, u32[]{:S(2)}, u32[]{:S(2)}) collective-permute-start(bf16[192,2304]{1,0:T(8,128)(2,1)S(1)} %collective-permute-done.4.o_first), channel_id=1, source_target_pairs={{4,8},{8,4},{6,10},{10,6},{20,24},{24,20},{22,26},{26,22},{5,9},{9... | collective-permute-start | bytes 2654216 | tf_op jit(solution)/shard_map/ppermute | solution.py:243
  36.9 2.2 %collective-permute-start.6 = (bf16[192,2304]{1,0:T(8,128)(2,1)S(1)}, bf16[192,2304]{1,0:T(8,128)(2,1)}, u32[]{:S(2)}, u32[]{:S(2)}) collective-permute-start(bf16[192,2304]{1,0:T(8,128)(2,1)S(1)} %collective-permute-done.5.o_mid1), channel_id=1, source_target_pairs={{4,0},{8,12},{6,2},{10,14},{20,16},{24,28},{22,18},{26,30},{5,1},{... | collective-permute-start | bytes 2654216 | tf_op jit(solution)/shard_map/ppermute | solution.py:243
  39.1 11.9 %collective-permute-done.7.o_mid2 = bf16[192,2304]{1,0:T(8,128)(2,1)S(1)} collective-permute-done((bf16[192,2304]{1,0:T(8,128)(2,1)S(1)}, bf16[192,2304]{1,0:T(8,128)(2,1)S(1)}, u32[]{:S(2)}, u32[]{:S(2)}) %collective-permute-start.7) | collective-permute-done | bytes 884768 | tf_op jit(solution)/shard_map/ppermute | solution.py:243
  51.0 2.2 %collective-permute-start.8 = (bf16[192,2304]{1,0:T(8,128)(2,1)S(1)}, bf16[192,2304]{1,0:T(8,128)(2,1)}, u32[]{:S(2)}, u32[]{:S(2)}) collective-permute-start(bf16[192,2304]{1,0:T(8,128)(2,1)S(1)} %collective-permute-done.7.o_mid2), channel_id=1, source_target_pairs={{4,0},{8,12},{6,2},{10,14},{20,16},{24,28},{22,18},{26,30},{5,1},{... | collective-permute-start | bytes 2654216 | tf_op jit(solution)/shard_map/ppermute | solution.py:243
  53.3 5.5 %collective-permute-start.1 = (bf16[2,64,1536]{2,1,0:T(8,128)(2,1)}, bf16[2,64,1536]{2,1,0:T(8,128)(2,1)}, u32[]{:S(2)}, u32[]{:S(2)}) collective-permute-start(bf16[2,64,1536]{2,1,0:T(8,128)(2,1)} %stream.1), channel_id=1, source_target_pairs={{2,4},{6,8},{10,12},{4,2},{8,6},{12,10},{3,5},{7,9},{11,13},{5,3},... | collective-permute-start | bytes 1179656 | tf_op jit(solution)/shard_map/ppermute | solution.py:338
  58.9 5.8 %collective-permute-done.1.halo = bf16[2,64,1536]{2,1,0:T(8,128)(2,1)} collective-permute-done((bf16[2,64,1536]{2,1,0:T(8,128)(2,1)}, bf16[2,64,1536]{2,1,0:T(8,128)(2,1)}, u32[]{:S(2)}, u32[]{:S(2)}) %collective-permute-start.1) | collective-permute-done | bytes 393248 | tf_op jit(solution)/shard_map/ppermute | solution.py:338
  64.7 16.6 %collective-permute-start.2 = (bf16[2,64,1536]{2,1,0:T(8,128)(2,1)}, bf16[2,64,1536]{2,1,0:T(8,128)(2,1)}, u32[]{:S(2)}, u32[]{:S(2)}) collective-permute-start(bf16[2,64,1536]{2,1,0:T(8,128)(2,1)} %collective-permute-done.1.halo), channel_id=1, source_target_pairs={{0,2},{2,0},{4,6},{6,4},{8,10},{10,8},{12,14},{14,12},{1,3},{3,1},... | collective-permute-start | bytes 1179656 | tf_op jit(solution)/shard_map/ppermute | solution.py:340
  81.3 3.0 %collective-permute-start.10 = (bf16[192,2304]{1,0:T(8,128)(2,1)S(1)}, bf16[192,2304]{1,0:T(8,128)(2,1)}, u32[]{:S(2)}, u32[]{:S(2)}) collective-permute-start(bf16[192,2304]{1,0:T(8,128)(2,1)S(1)} %collective-permute-done.5.o_mid1), channel_id=1, source_target_pairs={{4,22},{8,26},{6,20},{10,24},{20,6},{24,10},{22,4},{26,8},{5,23},{... | collective-permute-start | bytes 2654216 | tf_op jit(solution)/shard_map/ppermute | solution.py:243
  85.1 3.0 %collective-permute-start.12 = (bf16[192,2304]{1,0:T(8,128)(2,1)S(1)}, bf16[192,2304]{1,0:T(8,128)(2,1)}, u32[]{:S(2)}, u32[]{:S(2)}) collective-permute-start(bf16[192,2304]{1,0:T(8,128)(2,1)S(1)} %collective-permute-done.7.o_mid2), channel_id=1, source_target_pairs={{4,22},{8,26},{6,20},{10,24},{20,6},{24,10},{22,4},{26,8},{5,23},{... | collective-permute-start | bytes 2654216 | tf_op jit(solution)/shard_map/ppermute | solution.py:243
  99.9 5.0 %stack.101.table = s32[23]{0:T(128)S(1)} concatenate(s32[1]{0:T(128)} %bitcast.7, s32[1]{0:T(128)} %bitcast.8, s32[1]{0:T(128)} %bitcast.9, s32[1]{0:T(128)} %bitcast.10, s32[1]{0:T(128)} %bitcast.11, s32[1]{0:T(128)} %bitcast.12, s32[1]{0:T(128)} %bitcast.13, s32[1]{0:T(128)} %bitcast.14, s32[1]{0:T(128)} %bitcast.15, s32[1]{0:T(128)} %bitcast.5, s32[1]{0:T(128)} %bitcast.16, ...), dimensions={0} | concatenate | bytes 184 | tf_op jit(solution)/shard_map/stack | solution.py:296
  105.5 19.0 %collective-permute-done.9.d_first = bf16[192,2304]{1,0:T(8,128)(2,1)} collective-permute-done((bf16[192,2304]{1,0:T(8,128)(2,1)S(1)}, bf16[192,2304]{1,0:T(8,128)(2,1)}, u32[]{:S(2)}, u32[]{:S(2)}) %collective-permute-start.9) | collective-permute-done | bytes 884768 | tf_op jit(solution)/shard_map/ppermute | solution.py:243
  124.5 18.0 %collective-permute-done.12.d_mid2 = bf16[192,2304]{1,0:T(8,128)(2,1)} collective-permute-done((bf16[192,2304]{1,0:T(8,128)(2,1)S(1)}, bf16[192,2304]{1,0:T(8,128)(2,1)}, u32[]{:S(2)}, u32[]{:S(2)}) %collective-permute-start.12) | collective-permute-done | bytes 884768 | tf_op jit(solution)/shard_map/ppermute | solution.py:243
  143.6 11.1 %attend.2 = (bf16[2,64,768]{2,1,0:T(8,128)(2,1)S(1)}, bf16[2,64,768]{2,1,0:T(8,128)(2,1)S(1)}) custom-call(s32[23]{0:T(128)S(1)} %stack.101.table, bf16[2,64,1536]{2,1,0:T(8,128)(2,1)} %stream.1, bf16[2,64,1536]{2,1,0:T(8,128)(2,1)} %collective-permute-done.pair, bf16[2,64,1536]{2,1,0:T(8,128)(2,1)} %collective-permute-done.1.halo, ...), custom_call_target="tpu_custom_call" | custom-call | tf_op jit(solution)/shard_map/attend/pallas_call | solution.py:341
  156.3 2.5 %project.2 = bf16[2,64,1536]{2,1,0:T(8,128)(2,1)S(1)} custom-call(s32[3]{0:T(128)S(1)} %pad_add_fusion.1.table, bf16[2,64,768]{2,1,0:T(8,128)(2,1)S(1)} %get-tuple-element.9.att_own, bf16[2,64,768]{2,1,0:T(8,128)(2,1)S(1)} %collective-permute-done.14.att_got, bf16[2,64,1536]{2,1,0:T(8,128)(2,1)} %stream.1, bf16[2,6,1,1536]{3,2,1,0:T(2,128)(2,1)S(1)} %copy.17.gates, ...), custom_call_target="tpu_custom_call" | custom-call | tf_op jit(solution)/shard_map/project/pallas_call | solution.py:363
  160.2 10.8 %collective-permute-done.15.own.stream = bf16[2,64,1536]{2,1,0:T(8,128)(2,1)S(1)} collective-permute-done((bf16[2,64,1536]{2,1,0:T(8,128)(2,1)S(1)}, bf16[2,64,1536]{2,1,0:T(8,128)(2,1)S(1)}, u32[]{:S(2)}, u32[]{:S(2)}) %collective-permute-start.15) | collective-permute-done | bytes 393248 | tf_op jit(solution)/shard_map/ppermute | solution.py:369
  171.0 4.1 %collective-permute-start.17 = (bf16[2,64,1536]{2,1,0:T(8,128)(2,1)S(1)}, bf16[2,64,1536]{2,1,0:T(8,128)(2,1)S(1)}, u32[]{:S(2)}, u32[]{:S(2)}) collective-permute-start(bf16[2,64,1536]{2,1,0:T(8,128)(2,1)S(1)} %collective-permute-done.15.own.stream), channel_id=1, source_target_pairs={{2,4},{6,8},{10,12},{4,2},{8,6},{12,10},{3,5},{7,9},{11,13},{5,3},... | collective-permute-start | bytes 1179656 | tf_op jit(solution)/shard_map/ppermute | solution.py:338
  175.5 5.3 %collective-permute-done.17.halo = bf16[2,64,1536]{2,1,0:T(8,128)(2,1)S(1)} collective-permute-done((bf16[2,64,1536]{2,1,0:T(8,128)(2,1)S(1)}, bf16[2,64,1536]{2,1,0:T(8,128)(2,1)S(1)}, u32[]{:S(2)}, u32[]{:S(2)}) %collective-permute-start.17) | collective-permute-done | bytes 393248 | tf_op jit(solution)/shard_map/ppermute | solution.py:338
  182.7 10.6 %attend.3 = (bf16[2,64,768]{2,1,0:T(8,128)(2,1)S(1)}, bf16[2,64,768]{2,1,0:T(8,128)(2,1)}) custom-call(s32[23]{0:T(128)S(1)} %stack.101.table, bf16[2,64,1536]{2,1,0:T(8,128)(2,1)S(1)} %collective-permute-done.15.own.stream, bf16[2,64,1536]{2,1,0:T(8,128)(2,1)S(1)} %collective-permute-done.16.pair, bf16[2,64,1536]{2,1,0:T(8,128)(2,1)S(1)} %collective-permute-done.17.halo, ...), custom_call_target="tpu_custom_call" | custom-call | tf_op jit(solution)/shard_map/attend/pallas_call | solution.py:341
  195.7 2.3 %copy-done = bf16[1,1536,1536]{2,1,0:T(8,128)(2,1)S(1)} copy-done((bf16[1,1536,1536]{2,1,0:T(8,128)(2,1)S(1)}, bf16[1,1536,1536]{2,1,0:T(8,128)(2,1)}, u32[]{:S(2)}) %copy-start) | copy-done | bytes 4718616
  200.9 2.0 %project.3 = bf16[2,64,1536]{2,1,0:T(8,128)(2,1)S(1)} custom-call(s32[3]{0:T(128)S(1)} %pad_add_fusion.1.table, bf16[2,64,768]{2,1,0:T(8,128)(2,1)S(1)} %copy-done.10, bf16[2,64,768]{2,1,0:T(8,128)(2,1)S(1)} %collective-permute-done.19.att_got, bf16[2,64,1536]{2,1,0:T(8,128)(2,1)S(1)} %copy-done.2, bf16[2,6,1,1536]{3,2,1,0:T(2,128)(2,1)S(1)} %copy-done.6, ...), custom_call_target="tpu_custom_call" | custom-call | tf_op jit(solution)/shard_map/project/pallas_call | solution.py:363
  (71 shorter events, 23.6 us)
Async XLA Ops:
  9.0 20.6 %collective-permute-start.4 = (bf16[192,2304]{1,0:T(8,128)(2,1)S(1)}, bf16[192,2304]{1,0:T(8,128)(2,1)S(1)}, u32[]{:S(2)}, u32[]{:S(2)}) collective-permute-start(bf16[192,2304]{1,0:T(8,128)(2,1)S(1)} %bitcast.58), channel_id=1, source_target_pairs={{0,4},{4,0},{8,12},{12,8},{2,6},{6,2},{10,14},{14,10},{16,20},{20,... | collective-permute-start | bytes 2654216 | tf_op jit(solution)/shard_map/ppermute | solution.py:243
  9.2 27.7 %collective-permute-start.5 = (bf16[192,2304]{1,0:T(8,128)(2,1)S(1)}, bf16[192,2304]{1,0:T(8,128)(2,1)S(1)}, u32[]{:S(2)}, u32[]{:S(2)}) collective-permute-start(bf16[192,2304]{1,0:T(8,128)(2,1)S(1)} %bitcast.59), channel_id=1, source_target_pairs={{4,8},{8,4},{6,10},{10,6},{20,24},{24,20},{22,26},{26,22},{5,9},{9... | collective-permute-start | bytes 2654216 | tf_op jit(solution)/shard_map/ppermute | solution.py:243
  29.6 21.5 %collective-permute-start.7 = (bf16[192,2304]{1,0:T(8,128)(2,1)S(1)}, bf16[192,2304]{1,0:T(8,128)(2,1)S(1)}, u32[]{:S(2)}, u32[]{:S(2)}) collective-permute-start(bf16[192,2304]{1,0:T(8,128)(2,1)S(1)} %collective-permute-done.4.o_first), channel_id=1, source_target_pairs={{4,8},{8,4},{6,10},{10,6},{20,24},{24,20},{22,26},{26,22},{5,9},{9... | collective-permute-start | bytes 2654216 | tf_op jit(solution)/shard_map/ppermute | solution.py:243
  34.0 47.3 %copy-start.13 = (s32[2,6]{1,0:T(2,128)S(1)}, s32[2,6]{1,0:T(2,128)}, u32[]{:S(2)}) copy-start(s32[2,6]{1,0:T(2,128)} %param.8) | copy-start | bytes 148
  34.0 108.5 %copy-start.11 = (f32[1,2,128]{2,1,0:T(2,128)S(1)}, f32[1,2,128]{2,1,0:T(2,128)}, u32[]{:S(2)}) copy-start(f32[1,2,128]{2,1,0:T(2,128)} %param.12) | copy-start | bytes 3076
  35.1 50.0 %collective-permute-start.3 = (bf16[192,2304]{1,0:T(8,128)(2,1)}, bf16[192,2304]{1,0:T(8,128)(2,1)}, u32[]{:S(2)}, u32[]{:S(2)}) collective-permute-start(bf16[192,2304]{1,0:T(8,128)(2,1)} %bitcast.46), channel_id=1, source_target_pairs={{0,2},{2,0},{4,6},{6,4},{8,10},{10,8},{12,14},{14,12},{1,3},{3,1},... | collective-permute-start | bytes 2654216 | tf_op jit(solution)/shard_map/ppermute | solution.py:256
  36.9 51.2 %collective-permute-start.6 = (bf16[192,2304]{1,0:T(8,128)(2,1)S(1)}, bf16[192,2304]{1,0:T(8,128)(2,1)}, u32[]{:S(2)}, u32[]{:S(2)}) collective-permute-start(bf16[192,2304]{1,0:T(8,128)(2,1)S(1)} %collective-permute-done.5.o_mid1), channel_id=1, source_target_pairs={{4,0},{8,12},{6,2},{10,14},{20,16},{24,28},{22,18},{26,30},{5,1},{... | collective-permute-start | bytes 2654216 | tf_op jit(solution)/shard_map/ppermute | solution.py:243
  51.0 38.7 %collective-permute-start.8 = (bf16[192,2304]{1,0:T(8,128)(2,1)S(1)}, bf16[192,2304]{1,0:T(8,128)(2,1)}, u32[]{:S(2)}, u32[]{:S(2)}) collective-permute-start(bf16[192,2304]{1,0:T(8,128)(2,1)S(1)} %collective-permute-done.7.o_mid2), channel_id=1, source_target_pairs={{4,0},{8,12},{6,2},{10,14},{20,16},{24,28},{22,18},{26,30},{5,1},{... | collective-permute-start | bytes 2654216 | tf_op jit(solution)/shard_map/ppermute | solution.py:243
  53.3 11.5 %collective-permute-start.1 = (bf16[2,64,1536]{2,1,0:T(8,128)(2,1)}, bf16[2,64,1536]{2,1,0:T(8,128)(2,1)}, u32[]{:S(2)}, u32[]{:S(2)}) collective-permute-start(bf16[2,64,1536]{2,1,0:T(8,128)(2,1)} %stream.1), channel_id=1, source_target_pairs={{2,4},{6,8},{10,12},{4,2},{8,6},{12,10},{3,5},{7,9},{11,13},{5,3},... | collective-permute-start | bytes 1179656 | tf_op jit(solution)/shard_map/ppermute | solution.py:338
  58.8 22.5 %collective-permute-start = (bf16[2,64,1536]{2,1,0:T(8,128)(2,1)}, bf16[2,64,1536]{2,1,0:T(8,128)(2,1)}, u32[]{:S(2)}, u32[]{:S(2)}) collective-permute-start(bf16[2,64,1536]{2,1,0:T(8,128)(2,1)} %stream.1), channel_id=1, source_target_pairs={{0,2},{2,0},{4,6},{6,4},{8,10},{10,8},{12,14},{14,12},{1,3},{3,1},... | collective-permute-start | bytes 1179656 | tf_op jit(solution)/shard_map/ppermute | solution.py:339
  64.7 19.7 %collective-permute-start.2 = (bf16[2,64,1536]{2,1,0:T(8,128)(2,1)}, bf16[2,64,1536]{2,1,0:T(8,128)(2,1)}, u32[]{:S(2)}, u32[]{:S(2)}) collective-permute-start(bf16[2,64,1536]{2,1,0:T(8,128)(2,1)} %collective-permute-done.1.halo), channel_id=1, source_target_pairs={{0,2},{2,0},{4,6},{6,4},{8,10},{10,8},{12,14},{14,12},{1,3},{3,1},... | collective-permute-start | bytes 1179656 | tf_op jit(solution)/shard_map/ppermute | solution.py:340
  81.3 24.2 %collective-permute-start.10 = (bf16[192,2304]{1,0:T(8,128)(2,1)S(1)}, bf16[192,2304]{1,0:T(8,128)(2,1)}, u32[]{:S(2)}, u32[]{:S(2)}) collective-permute-start(bf16[192,2304]{1,0:T(8,128)(2,1)S(1)} %collective-permute-done.5.o_mid1), channel_id=1, source_target_pairs={{4,22},{8,26},{6,20},{10,24},{20,6},{24,10},{22,4},{26,8},{5,23},{... | collective-permute-start | bytes 2654216 | tf_op jit(solution)/shard_map/ppermute | solution.py:243
  84.4 40.1 %collective-permute-start.9 = (bf16[192,2304]{1,0:T(8,128)(2,1)S(1)}, bf16[192,2304]{1,0:T(8,128)(2,1)}, u32[]{:S(2)}, u32[]{:S(2)}) collective-permute-start(bf16[192,2304]{1,0:T(8,128)(2,1)S(1)} %collective-permute-done.4.o_first), channel_id=1, source_target_pairs={{0,18},{4,22},{8,26},{12,30},{2,16},{6,20},{10,24},{14,28},{16,2},... | collective-permute-start | bytes 2654216 | tf_op jit(solution)/shard_map/ppermute | solution.py:243
  85.1 57.4 %collective-permute-start.12 = (bf16[192,2304]{1,0:T(8,128)(2,1)S(1)}, bf16[192,2304]{1,0:T(8,128)(2,1)}, u32[]{:S(2)}, u32[]{:S(2)}) collective-permute-start(bf16[192,2304]{1,0:T(8,128)(2,1)S(1)} %collective-permute-done.7.o_mid2), channel_id=1, source_target_pairs={{4,22},{8,26},{6,20},{10,24},{20,6},{24,10},{22,4},{26,8},{5,23},{... | collective-permute-start | bytes 2654216 | tf_op jit(solution)/shard_map/ppermute | solution.py:243
  88.1 36.4 %collective-permute-start.11 = (bf16[192,2304]{1,0:T(8,128)(2,1)}, bf16[192,2304]{1,0:T(8,128)(2,1)}, u32[]{:S(2)}, u32[]{:S(2)}) collective-permute-start(bf16[192,2304]{1,0:T(8,128)(2,1)} %collective-permute-done.6.o_end1), channel_id=1, source_target_pairs={{0,18},{12,30},{2,16},{14,28},{16,2},{28,14},{18,0},{30,12},{1,19}... | collective-permute-start | bytes 2654216 | tf_op jit(solution)/shard_map/ppermute | solution.py:243
  89.8 52.8 %collective-permute-start.13 = (bf16[192,2304]{1,0:T(8,128)(2,1)}, bf16[192,2304]{1,0:T(8,128)(2,1)}, u32[]{:S(2)}, u32[]{:S(2)}) collective-permute-start(bf16[192,2304]{1,0:T(8,128)(2,1)} %collective-permute-done.8.o_end2), channel_id=1, source_target_pairs={{0,18},{12,30},{2,16},{14,28},{16,2},{28,14},{18,0},{30,12},{1,19}... | collective-permute-start | bytes 2654216 | tf_op jit(solution)/shard_map/ppermute | solution.py:243
  154.7 1.6 collective-permute-start.14
  156.3 26.4 %copy-start.8 = (bf16[1,2,6,2,1536]{4,3,2,1,0:T(2,128)(2,1)S(1)}, bf16[1,2,6,2,1536]{4,3,2,1,0:T(2,128)(2,1)}, u32[]{:S(2)}) copy-start(bf16[1,2,6,2,1536]{4,3,2,1,0:T(2,128)(2,1)} %param.9) | copy-start | bytes 221188
  158.9 34.5 %copy-start.3 = (bf16[2,64,1536]{2,1,0:T(8,128)(2,1)}, bf16[2,64,1536]{2,1,0:T(8,128)(2,1)S(1)}, u32[]{:S(2)}) copy-start(bf16[2,64,1536]{2,1,0:T(8,128)(2,1)S(1)} %project.2) | copy-start | bytes 1179652
  158.9 12.1 %collective-permute-start.15 = (bf16[2,64,1536]{2,1,0:T(8,128)(2,1)S(1)}, bf16[2,64,1536]{2,1,0:T(8,128)(2,1)S(1)}, u32[]{:S(2)}, u32[]{:S(2)}) collective-permute-start(bf16[2,64,1536]{2,1,0:T(8,128)(2,1)S(1)} %project.2), channel_id=1, source_target_pairs={{0,1},{2,3},{4,5},{6,7},{8,9},{10,11},{12,13},{14,15},{16,17},{18,... | collective-permute-start | bytes 1179656 | tf_op jit(solution)/shard_map/ppermute | solution.py:369
  171.0 9.8 %collective-permute-start.17 = (bf16[2,64,1536]{2,1,0:T(8,128)(2,1)S(1)}, bf16[2,64,1536]{2,1,0:T(8,128)(2,1)S(1)}, u32[]{:S(2)}, u32[]{:S(2)}) collective-permute-start(bf16[2,64,1536]{2,1,0:T(8,128)(2,1)S(1)} %collective-permute-done.15.own.stream), channel_id=1, source_target_pairs={{2,4},{6,8},{10,12},{4,2},{8,6},{12,10},{3,5},{7,9},{11,13},{5,3},... | collective-permute-start | bytes 1179656 | tf_op jit(solution)/shard_map/ppermute | solution.py:338
  175.1 6.3 %collective-permute-start.16 = (bf16[2,64,1536]{2,1,0:T(8,128)(2,1)S(1)}, bf16[2,64,1536]{2,1,0:T(8,128)(2,1)S(1)}, u32[]{:S(2)}, u32[]{:S(2)}) collective-permute-start(bf16[2,64,1536]{2,1,0:T(8,128)(2,1)S(1)} %collective-permute-done.15.own.stream), channel_id=1, source_target_pairs={{0,2},{2,0},{4,6},{6,4},{8,10},{10,8},{12,14},{14,12},{1,3},{3,1},... | collective-permute-start | bytes 1179656 | tf_op jit(solution)/shard_map/ppermute | solution.py:339
  180.8 1.9 collective-permute-start.18
  194.1 1.7 collective-permute-start.19
  (12 other events, 73.0 us)

commit v2 on v1

--- a/solution.py
+++ b/solution.py
@@ -22,88 +22,108 @@
     return jnp.sum(inside, axis=1) - 1
 
 
-def attend_kernel(
-    table,
-    own,
-    pair,
-    halo,
-    pair_halo,
-    modulation,
-    gains,
-    home,
-    home_pair,
-    o_first,
-    o_mid1,
-    o_end1,
-    o_mid2,
-    o_end2,
-    d_first,
-    d_mid1,
-    d_end1,
-    d_mid2,
-    d_end2,
-    att_own,
-    att_pair,
-    weights,
-    normed,
-    sems,
-):
-    micro_count, view_tok, width = own.shape
+def owner_of(views, m, place):
+    start, owner = jnp.int32(0), jnp.int32(-1)
+    for j in range(views.shape[1]):
+        owner = owner + jnp.where(start <= place, 1, 0)
+        start = start + views[m, j]
+    return owner
+
+
+def attend_table(views):
+    count = lax.axis_size("seq")
+    place = lax.axis_index("seq")
+    core = place % 2
+    chip = place // 2
+    middle = (chip == 1) | (chip == 2)
+    others = (
+        chip,
+        chip + 1 - 2 * (chip % 2),
+        jnp.where(middle, 3 - chip, (chip + 2) % 4),
+        jnp.where(middle, jnp.where(chip == 1, 3, 0), 3 - chip),
+    )
+    order = []
+    for other in others:
+        order += [2 * other + core, 2 * other + 1 - core]
+    outward = 2 * core - 1
+    pair_place = place - outward
+    halo_place = place + outward
+    pair_halo_place = pair_place - outward
+    places = (place, pair_place, halo_place, pair_halo_place)
+    sets, masks = [], []
+    for m in range(views.shape[0]):
+        found = [
+            owner_of(views, m, jnp.clip(where, 0, count - 1)) for where in places
+        ]
+        sets.append(found)
+        masks.append(
+            (
+                found[0] == found[1],
+                (halo_place >= 0) & (halo_place < count) & (found[0] == found[2]),
+                (pair_halo_place >= 0)
+                & (pair_halo_place < count)
+                & (found[1] == found[3]),
+            )
+        )
+    return order, sets, masks
+
+
+def attend_kernel(*refs):
+    views, own, pair, halo, pair_halo, modulation_src, gains = refs[:7]
+    pieces = refs[7:31]
+    att_own, att_pair = refs[31:33]
+    weights, normed, streams, modulation, sems, stream_sems = refs[33:]
+    _, micro_count, view_tok, width = streams.shape
     rows = weights.shape[0] // 8
     part = weights.shape[1] // 3
     head = gains.shape[1]
-    middle = table[0]
-
-    def piece(source, index):
-        start = pl.multiple_of(table[1 + index] * rows, rows)
+    order, sets, masks = attend_table(views)
+
+    def piece(index):
+        start = pl.multiple_of(order[index // 3] * rows, rows)
         return pltpu.make_async_copy(
-            source, weights.at[pl.ds(start, rows), :], sems.at[index]
-        )
-
-    def load(index, mid, end):
-        @pl.when(middle == 1)
-        def _():
-            piece(mid, index).start()
-
-        @pl.when(middle == 0)
-        def _():
-            piece(end, index).start()
-
-    piece(home, 0).start()
-    piece(home_pair, 1).start()
-    piece(o_first, 2).start()
-    piece(d_first, 3).start()
-    load(4, o_mid1, o_end1)
-    load(5, d_mid1, d_end1)
-    load(6, o_mid2, o_end2)
-    load(7, d_mid2, d_end2)
+            pieces[index],
+            weights.at[pl.ds(start, rows), pl.ds(index % 3 * part, part)],
+            sems.at[index],
+        )
+
+    sources = (own, pair, halo, pair_halo)
+    scales = pltpu.make_async_copy(modulation_src, modulation, stream_sems.at[4])
+    incoming = [
+        pltpu.make_async_copy(sources[slot], streams.at[slot], stream_sems.at[slot])
+        for slot in range(4)
+    ]
+    scales.start()
+    for slot in range(4):
+        incoming[slot].start()
+    for index in range(24):
+        piece(index).start()
 
     half = 2 * micro_count * view_tok
-    for slot, source in enumerate((own, pair, halo, pair_halo)):
+    scales.wait()
+    for slot in range(4):
+        incoming[slot].wait()
         for m in range(micro_count):
-            wide = source[m].astype(jnp.float32)
+            wide = streams[slot, m].astype(jnp.float32)
             average = jnp.mean(wide, axis=-1, keepdims=True)
             squares = jnp.mean(wide * wide, axis=-1, keepdims=True)
             spread = squares - average * average
-            factors = modulation[m, table[9 + 4 * m + slot]].astype(jnp.float32)
+            factors = modulation[m, sets[m][slot]].astype(jnp.float32)
             value = (wide - average) * lax.rsqrt(spread + epsilon) * (
                 1.0 + factors[1:2]
             ) + factors[0:1]
             first = half * (slot // 2) + (2 * m + slot % 2) * view_tok
             normed[first : first + view_tok, :] = value.astype(jnp.bfloat16)
 
-    for index in range(8):
-        piece(home, index).wait()
+    for index in range(24):
+        piece(index).wait()
 
     two = 2 * view_tok
     low_row = lax.broadcasted_iota(jnp.int32, (two, two), 0) < view_tok
     low_col = lax.broadcasted_iota(jnp.int32, (two, two), 1) < view_tok
     near_masks, far_masks = [], []
     for m in range(micro_count):
-        base = 9 + 4 * micro_count + 3 * m
-        together = jnp.where(table[base] == 1, 1.0, 0.0)
-        below = jnp.where(table[base + 1] == 1, 1.0, 0.0)
-        above = jnp.where(table[base + 2] == 1, 1.0, 0.0)
+        together, below, above = (jnp.where(mask, 1.0, 0.0) for mask in masks[m])
         near_masks.append(jnp.where(low_row == low_col, 1.0, together))
         far_masks.append(
             jnp.where(
@@ -166,12 +186,22 @@
     lax.fori_loop(0, part // block, heads, 0)
 
 
-def project_kernel(
-    table, att_own, att_got, stream, gates, out_weight, result, weights, sems
-):
+def project_kernel(last, *refs):
+    views, att_own_src, att_got_src, stream_src, gates_src, out_weight = refs[:6]
+    refs = refs[6:]
+    if last:
+        keep_src, refs = refs[0], refs[1:]
+    result, weights, att_own, att_got, stream, gates = refs[:6]
+    refs = refs[6:]
+    if last:
+        keep, refs = refs[0], refs[1:]
+    sems, small_sems = refs
     micro_count, view_tok, part = att_own.shape
     width = out_weight.shape[1]
-    mine = table[0]
+    place = lax.axis_index("seq")
+    mine = (place + lax.axis_index("groups")) % 2
+    newest = lax.axis_index("section") == lax.axis_size("section") - 1
+    sets = [owner_of(views, m, place) for m in range(views.shape[0])]
     blocks = sems.shape[0]
     block = width // blocks
 
@@ -182,8 +212,24 @@
             sems.at[index],
         )
 
+    moves = [
+        (att_own_src, att_own),
+        (att_got_src, att_got),
+        (stream_src, stream),
+        (gates_src, gates),
+    ]
+    if last:
+        moves.append((keep_src, keep))
+    copies = [
+        pltpu.make_async_copy(source, target, small_sems.at[i])
+        for i, (source, target) in enumerate(moves)
+    ]
+    for copy in copies:
+        copy.start()
     for index in range(blocks):
         piece(index).start()
+    for copy in copies:
+        copy.wait()
     tokens = micro_count * view_tok
     here = att_own[...].reshape(tokens, part)
     there = att_got[...].reshape(tokens, part)
@@ -200,11 +246,18 @@
             preferred_element_type=jnp.float32,
         )
         for m in range(micro_count):
-            gate = gates[m, table[1 + m]][:, cols].astype(jnp.float32)
-            result[m, :, cols] = (
+            gate = gates[sets[m]][m : m + 1, cols].astype(jnp.float32)
+            value = (
                 stream[m, :, cols].astype(jnp.float32)
                 + gate * mixed[m * view_tok : (m + 1) * view_tok]
             ).astype(jnp.bfloat16)
+            if last:
+                value = jnp.where(newest, value, keep[m, :, cols])
+            result[m, :, cols] = value
+
+
+def tied(value, *others):
+    return lax.optimization_barrier((value,) + others)[0]
 
 
 def paired_body(
@@ -221,6 +274,7 @@
     core = place % 2
     chip = place // 2
     mine = core ^ group
+    middle = (chip == 1) | (chip == 2)
     line_axes = ("groups", "seq")
 
     def along(steps):
@@ -231,13 +285,15 @@
             for a, b in steps
         ]
 
-    def across(chips):
-        return [
-            (g * seq_count + 2 * a + c, (1 - g) * seq_count + 2 * a + 1 - c)
-            for g in range(2)
-            for c in range(2)
-            for a in chips
-        ]
+    opposite = [
+        (g * seq_count + 2 * a + c, (1 - g) * seq_count + 2 * a + 1 - c)
+        for g in range(2)
+        for c in range(2)
+        for a in range(seq_count // 2)
+    ]
+    outer = along([(0, 1), (1, 0), (2, 3), (3, 2)])
+    inner = along([(1, 2), (2, 1)])
+    outward_steps = along([(1, 0), (2, 3)])
 
     def send(value, pairs):
         return lax.ppermute(value, line_axes, pairs)
@@ -247,124 +303,126 @@
         (i + 1, i) for i in range(1, seq_count - 1, 2)
     ]
 
-    halves = qkv_weight[0].reshape(rows, 3, 2, part)
-    home = lax.dynamic_index_in_dim(halves, mine, 2, False).reshape(rows, 3 * part)
-    lent = lax.dynamic_index_in_dim(halves, 1 - mine, 2, False).reshape(rows, 3 * part)
-
-    o_first = send(home, along([(0, 1), (1, 0), (2, 3), (3, 2)]))
-    o_mid1 = send(home, along([(1, 2), (2, 1)]))
+    by_kind = jnp.transpose(qkv_weight[0], (1, 0, 2))
+    home = [
+        lax.dynamic_slice(by_kind, (kind, 0, mine * part), (1, rows, part))[0]
+        for kind in range(3)
+    ]
+    lent = lax.dynamic_slice(by_kind, (0, 0, (1 - mine) * part), (3, rows, part))
+
+    pair = lax.ppermute(stream, "seq", swap_cores)
+    halo = lax.ppermute(stream, "seq", swap_edges)
     home_pair = lax.ppermute(lent, "seq", swap_cores)
-    o_mid2 = send(o_first, along([(1, 2), (2, 1)]))
-    o_end1 = send(o_mid1, along([(1, 0), (2, 3)]))
-    d_first = send(o_first, across(range(4)))
-    d_mid1 = send(o_mid1, across([1, 2]))
-    d_end1 = send(o_end1, across([0, 3]))
-    o_end2 = send(o_mid2, along([(1, 0), (2, 3)]))
-    d_mid2 = send(o_mid2, across([1, 2]))
-    d_end2 = send(o_end2, across([0, 3]))
-
-    middle = ((chip == 1) | (chip == 2)).astype(jnp.int32)
-    first_chip = chip ^ 1
-    second_chip = jnp.where(middle == 1, 3 - chip, chip ^ 2)
-    third_chip = jnp.where(middle == 1, (3 - chip) ^ 1, 3 - chip)
-    order = []
-    for other in (chip, first_chip, second_chip, third_chip):
-        order += [2 * other + core, 2 * other + 1 - core]
-
-    owners = jnp.stack([view_sets(set_views[m], seq_count) for m in range(micro_count)])
-    outward = jnp.where(core == 0, -1, 1)
-    pair_place = place + outward * -1
-    halo_place = place + outward
-    pair_halo_place = pair_place - outward
-    sets, masks = [], []
-
-    def owner(m, where):
-        return owners[m, jnp.clip(where, 0, seq_count - 1)]
-
-    def inside(where):
-        return (where >= 0) & (where < seq_count)
-
-    for m in range(micro_count):
-        own_set, pair_set = owner(m, place), owner(m, pair_place)
-        halo_set, pair_halo_set = owner(m, halo_place), owner(m, pair_halo_place)
-        sets += [own_set, pair_set, halo_set, pair_halo_set]
-        masks += [
-            own_set == pair_set,
-            inside(halo_place) & (own_set == halo_set),
-            inside(pair_halo_place) & (pair_set == pair_halo_set),
-        ]
-    table = jnp.stack(
-        [middle] + order + sets + [m.astype(jnp.int32) for m in masks]
-    ).astype(jnp.int32)
-    gate_table = jnp.stack(
-        [mine] + [owner(m, place) for m in range(micro_count)]
-    ).astype(jnp.int32)
-    gates = set_gate[0][:, :, None, :]
+    pair_halo = lax.ppermute(halo, "seq", swap_cores)
+    first_exchange = (pair, halo, pair_halo)
+
+    from_outer, from_inner = [], []
+    across_first, inner_next, outer_next = [], [], []
+    for kind in range(3):
+        ready = home[kind]
+        if kind == 2:
+            ready = tied(ready, from_outer[0], from_inner[0])
+        from_outer.append(send(ready, outer))
+        from_inner.append(send(ready, inner))
+    before = ()
+    for kind in range(3):
+        a = tied(from_outer[kind], from_inner[kind], *before)
+        b = tied(from_inner[kind], from_outer[kind], *before)
+        across_first.append(send(a, opposite))
+        inner_next.append(send(a, inner))
+        outer_next.append(send(b, outward_steps))
+        before = (from_outer[kind], from_inner[kind])
+    second, across_second, outer_last = [], [], []
+    for kind in range(3):
+        before = before + (across_first[kind],)
+        a = tied(inner_next[kind], outer_next[kind], *before)
+        b = tied(outer_next[kind], inner_next[kind], *before)
+        outer_last.append(send(a, outward_steps))
+        second.append(jnp.where(middle, from_inner[kind], b))
+        across_second.append(send(second[kind], opposite))
+        before = (inner_next[kind], outer_next[kind])
+    third, across_third = [], []
+    for kind in range(3):
+        a = tied(outer_last[kind], across_second[kind], *before)
+        third.append(jnp.where(middle, inner_next[kind], a))
+        across_third.append(send(third[kind], opposite))
+        before = (outer_last[kind],)
+
+    pieces = (
+        home
+        + [home_pair[kind] for kind in range(3)]
+        + from_outer
+        + across_first
+        + second
+        + across_second
+        + third
+        + across_third
+    )
+
+    section_place = lax.axis_index("section")
+    gates = jnp.transpose(set_gate[0], (1, 0, 2))
 
     vmem = pl.BlockSpec(memory_space=pltpu.VMEM)
     smem = pl.BlockSpec(memory_space=pltpu.SMEM)
-    anywhere = pl.BlockSpec(memory_space=pl.ANY)
+    anywhere = pl.BlockSpec(memory_space=pltpu.HBM)
     half_shape = jax.ShapeDtypeStruct((micro_count, view_tok, part), jnp.bfloat16)
     attend = pl.pallas_call(
         attend_kernel,
         out_shape=(half_shape, half_shape),
-        in_specs=[smem] + [vmem] * 6 + [anywhere] * 12,
+        in_specs=[smem] + [anywhere] * 5 + [vmem] + [anywhere] * 24,
         out_specs=(vmem, vmem),
         scratch_shapes=[
             pltpu.VMEM((width, 3 * part), jnp.bfloat16),
             pltpu.VMEM((4 * micro_count * view_tok, width), jnp.bfloat16),
-            pltpu.SemaphoreType.DMA((8,)),
+            pltpu.VMEM((4,) + stream.shape, jnp.bfloat16),
+            pltpu.VMEM(modulation.shape[1:], jnp.bfloat16),
+            pltpu.SemaphoreType.DMA((24,)),
+            pltpu.SemaphoreType.DMA((5,)),
         ],
-        compiler_params=pltpu.CompilerParams(vmem_limit_bytes=40 * 1024 * 1024),
+        compiler_params=pltpu.CompilerParams(vmem_limit_bytes=60 * 1024 * 1024),
         name="attend",
     )
-    project = pl.pallas_call(
-        project_kernel,
-        out_shape=jax.ShapeDtypeStruct(stream.shape, jnp.bfloat16),
-        in_specs=[smem] + [vmem] * 4 + [anywhere],
-        out_specs=vmem,
-        scratch_shapes=[
-            pltpu.VMEM((width, width), jnp.bfloat16),
-            pltpu.SemaphoreType.DMA((3,)),
-        ],
-        compiler_params=pltpu.CompilerParams(vmem_limit_bytes=24 * 1024 * 1024),
-        name="project",
-    )
-
-    section_place = lax.axis_index("section")
+
+    def project(last, *operands):
+        spare = [pltpu.VMEM(stream.shape, jnp.bfloat16)] if last else []
+        return pl.pallas_call(
+            functools.partial(project_kernel, last),
+            out_shape=jax.ShapeDtypeStruct(stream.shape, jnp.bfloat16),
+            in_specs=[smem] + [anywhere] * (len(operands) - 1),
+            out_specs=vmem,
+            scratch_shapes=[
+                pltpu.VMEM((width, width), jnp.bfloat16),
+                pltpu.VMEM((micro_count, view_tok, part), jnp.bfloat16),
+                pltpu.VMEM((micro_count, view_tok, part), jnp.bfloat16),
+                pltpu.VMEM(stream.shape, jnp.bfloat16),
+                pltpu.VMEM(gates.shape, jnp.bfloat16),
+            ]
+            + spare
+            + [pltpu.SemaphoreType.DMA((3,)), pltpu.SemaphoreType.DMA((5,))],
+            compiler_params=pltpu.CompilerParams(vmem_limit_bytes=60 * 1024 * 1024),
+            name="project",
+        )(*operands)
+
     own = stream
     hidden = None
     for moment in range(section_count):
-        halo = lax.ppermute(own, "seq", swap_edges)
-        pair = lax.ppermute(own, "seq", swap_cores)
-        pair_halo = lax.ppermute(halo, "seq", swap_cores)
+        if moment > 0:
+            halo = lax.ppermute(own, "seq", swap_edges)
+            pair = lax.ppermute(own, "seq", swap_cores)
+            pair_halo = lax.ppermute(halo, "seq", swap_cores)
         att_own, att_pair = attend(
-            table,
-            own,
-            pair,
-            halo,
-            pair_halo,
-            modulation[0],
-            norm_gain[0],
-            home,
-            home_pair,
-            o_first,
-            o_mid1,
-            o_end1,
-            o_mid2,
-            o_end2,
-            d_first,
-            d_mid1,
-            d_end1,
-            d_mid2,
-            d_end2,
+            set_views, own, pair, halo, pair_halo, modulation[0], norm_gain[0], *pieces
         )
         att_got = lax.ppermute(att_pair, "seq", swap_cores)
-        result = project(gate_table, att_own, att_got, own, gates, out_weight[0])
-        if moment == 0:
-            hidden = result
+        operands = (set_views, att_own, att_got, own, gates, out_weight[0])
+        if moment > 0 and moment + 1 == section_count:
+            hidden = project(True, *operands, hidden)
         else:
-            hidden = jnp.where(section_place == moment, result, hidden)
+            result = project(False, *operands)
+            if moment == 0:
+                hidden = result
+            else:
+                hidden = jnp.where(section_place == moment, result, hidden)
         if moment + 1 < section_count:
             own = lax.ppermute(
                 result, "section", [(i, i + 1) for i in range(section_count - 1)]

time: 206 us -> 158 us (0.77)
  waiting for transfers between devices: 90.2 us -> 48.2 us
  local copies, waits for them, and re-layouts: 23.9 us -> 5.2 us
  starting transfers between devices: 53 us -> 64.6 us
  Pallas kernels: 26.3 us -> 34.3 us
  between operations: 7.73 us -> 0.63 us
    ppermute x10 -> x24, waiting for transfers between devices: 65.6 us -> 28.4 us  [send(): return lax.ppermute(value, line_axes, pairs)]
    ppermute x10 -> x24, starting transfers between devices: 22.1 us -> 53.5 us  [send(): return lax.ppermute(value, line_axes, pairs)]
    ppermute x2, starting transfers between devices: 17.2 us -> 1.39 us  [paired_body(): pair_halo = lax.ppermute(halo, 'seq', swap_cores)]
    another operation x3 -> x0, local copies, waits for them, and re-layouts: 9.05 us -> none  [the longest x1 5.03 us: paired_body(): jnp.stack([middle] + order + sets + [m.astype(jnp.int32) for m in masks])]
    pallas_call x4, Pallas kernels: 26.3 us -> 34.3 us  [the longest x2 24.5 us: paired_body(): attend(set_views, own, pair, halo, pair_halo, modulation[0], norm_gain[0]...]
    unnamed x36 -> x66, local copies, waits for them, and re-layouts: 10.5 us -> 2.85 us
    ppermute x2 -> x1, starting transfers between devices: 9.61 us -> 1.98 us  [paired_body(): halo = lax.ppermute(own, 'seq', swap_edges)]
    ppermute x2 -> x1, waiting for transfers between devices: 11.1 us -> 4.73 us  [paired_body(): halo = lax.ppermute(own, 'seq', swap_edges)]
  transfers between devices with their start and end apart: 20 -> 34, of which waited for: 10 -> 15; matrix products, arithmetic and copies ran while one was open for 5% -> 3% of each run, Pallas kernels for 0% -> 0%
where the time goes in v2:
time: 158 us; the launch traced here: 156 us
  starting transfers between devices  64.6 us (41%)
  waiting for transfers between devices  48.2 us (31%)
  Pallas kernels  34.3 us (22%)
  local copies, waits for them, and re-layouts  5.2 us (3%)
  other arithmetic  3.09 us (2%)
    ppermute x24, starting transfers between devices, send(): return lax.ppermute(value, line_axes, pairs)  53.5 us
    ppermute x24, waiting for transfers between devices, send(): return lax.ppermute(value, line_axes, pairs)  28.4 us
    pallas_call x2, Pallas kernels, paired_body(): attend(set_views, own, pair, halo, pair_halo, modulation[0], norm_gain[0]...  24.5 us
    ppermute x1, waiting for transfers between devices, paired_body(): lax.ppermute(result, 'section', [(i, i + 1) for i in range(section_count...  11.1 us
    pallas_call x2, Pallas kernels, project(): pl.pallas_call(functools.partial(project_kernel, last), out_shape=jax.Sha...  9.76 us
    ppermute x1, waiting for transfers between devices, paired_body(): halo = lax.ppermute(own, 'seq', swap_edges)  4.73 us
  transfers between devices with their start and end apart: 34, of which 15 were waited for; matrix products, arithmetic and copies ran while one was open for 3% of the time, Pallas kernels for 0%

profile of v2, /device:TPU:11, one launch (start us, length us, event | category | flops | bytes accessed | tf_op | source)
XLA Modules:
  0.0 156.0 jit_solution(13137938829860173032)
XLA Ops:
  1.4 3.2 %collective-permute-start.6 = (bf16[192,768]{1,0:T(8,128)(2,1)S(1)}, bf16[192,768]{1,0:T(8,128)(2,1)}, u32[]{:S(2)}, u32[]{:S(2)}) collective-permute-start(bf16[192,768]{1,0:T(8,128)(2,1)S(1)} %get-tuple-element.47.refs_7_), channel_id=1, source_target_pairs={{4,8},{8,4},{6,10},{10,6},{20,24},{24,20},{22,26},{26,22},{5,9},{9... | collective-permute-start | bytes 884744 | tf_op jit(solution)/shard_map/ppermute | solution.py:299
  4.7 2.6 %collective-permute-start.9 = (bf16[192,768]{1,0:T(8,128)(2,1)S(1)}, bf16[192,768]{1,0:T(8,128)(2,1)S(1)}, u32[]{:S(2)}, u32[]{:S(2)}) collective-permute-start(bf16[192,768]{1,0:T(8,128)(2,1)S(1)} %get-tuple-element.46.refs_8_), channel_id=1, source_target_pairs={{4,8},{8,4},{6,10},{10,6},{20,24},{24,20},{22,26},{26,22},{5,9},{9... | collective-permute-start | bytes 884744 | tf_op jit(solution)/shard_map/ppermute | solution.py:299
  7.3 3.9 %collective-permute-done.6 = bf16[192,768]{1,0:T(8,128)(2,1)} collective-permute-done((bf16[192,768]{1,0:T(8,128)(2,1)S(1)}, bf16[192,768]{1,0:T(8,128)(2,1)}, u32[]{:S(2)}, u32[]{:S(2)}) %collective-permute-start.6) | collective-permute-done | bytes 294944 | tf_op jit(solution)/shard_map/ppermute | solution.py:299
  14.5 3.1 %collective-permute-start.14 = (bf16[192,768]{1,0:T(8,128)(2,1)S(1)}, bf16[192,768]{1,0:T(8,128)(2,1)}, u32[]{:S(2)}, u32[]{:S(2)}) collective-permute-start(bf16[192,768]{1,0:T(8,128)(2,1)S(1)} %collective-permute-done.4.refs_13_), channel_id=1, source_target_pairs={{4,8},{8,4},{6,10},{10,6},{20,24},{24,20},{22,26},{26,22},{5,9},{9... | collective-permute-start | bytes 884744 | tf_op jit(solution)/shard_map/ppermute | solution.py:299
  17.7 5.0 %collective-permute-start.8 = (bf16[192,768]{1,0:T(8,128)(2,1)S(1)}, bf16[192,768]{1,0:T(8,128)(2,1)}, u32[]{:S(2)}, u32[]{:S(2)}) collective-permute-start(bf16[192,768]{1,0:T(8,128)(2,1)S(1)} %collective-permute-done.4.refs_13_), channel_id=1, source_target_pairs={{0,18},{4,22},{8,26},{12,30},{2,16},{6,20},{10,24},{14,28},{16,2},... | collective-permute-start | bytes 884744 | tf_op jit(solution)/shard_map/ppermute | solution.py:299
  24.8 3.2 %collective-permute-start.16 = (bf16[192,768]{1,0:T(8,128)(2,1)S(1)}, bf16[192,768]{1,0:T(8,128)(2,1)}, u32[]{:S(2)}, u32[]{:S(2)}) collective-permute-start(bf16[192,768]{1,0:T(8,128)(2,1)S(1)} %collective-permute-done.5.refs_14_), channel_id=1, source_target_pairs={{4,8},{8,4},{6,10},{10,6},{20,24},{24,20},{22,26},{26,22},{5,9},{9... | collective-permute-start | bytes 884744 | tf_op jit(solution)/shard_map/ppermute | solution.py:299
  28.1 3.1 %collective-permute-start.10 = (bf16[192,768]{1,0:T(8,128)(2,1)S(1)}, bf16[192,768]{1,0:T(8,128)(2,1)}, u32[]{:S(2)}, u32[]{:S(2)}) collective-permute-start(bf16[192,768]{1,0:T(8,128)(2,1)S(1)} %collective-permute-done.5.refs_14_), channel_id=1, source_target_pairs={{0,18},{4,22},{8,26},{12,30},{2,16},{6,20},{10,24},{14,28},{16,2},... | collective-permute-start | bytes 884744 | tf_op jit(solution)/shard_map/ppermute | solution.py:299
  32.6 3.0 %collective-permute-start.18 = (bf16[192,768]{1,0:T(8,128)(2,1)S(1)}, bf16[192,768]{1,0:T(8,128)(2,1)S(1)}, u32[]{:S(2)}, u32[]{:S(2)}) collective-permute-start(bf16[192,768]{1,0:T(8,128)(2,1)S(1)} %collective-permute-done.7.refs_15_), channel_id=1, source_target_pairs={{4,8},{8,4},{6,10},{10,6},{20,24},{24,20},{22,26},{26,22},{5,9},{9... | collective-permute-start | bytes 884744 | tf_op jit(solution)/shard_map/ppermute | solution.py:299
  35.6 3.3 %collective-permute-start.12 = (bf16[192,768]{1,0:T(8,128)(2,1)S(1)}, bf16[192,768]{1,0:T(8,128)(2,1)S(1)}, u32[]{:S(2)}, u32[]{:S(2)}) collective-permute-start(bf16[192,768]{1,0:T(8,128)(2,1)S(1)} %collective-permute-done.7.refs_15_), channel_id=1, source_target_pairs={{0,18},{4,22},{8,26},{12,30},{2,16},{6,20},{10,24},{14,28},{16,2},... | collective-permute-start | bytes 884744 | tf_op jit(solution)/shard_map/ppermute | solution.py:299
  41.9 2.7 %collective-permute-start.1 = (bf16[2,64,1536]{2,1,0:T(8,128)(2,1)}, bf16[2,64,1536]{2,1,0:T(8,128)(2,1)S(1)}, u32[]{:S(2)}, u32[]{:S(2)}) collective-permute-start(bf16[2,64,1536]{2,1,0:T(8,128)(2,1)} %refs_3_.1), channel_id=1, source_target_pairs={{2,4},{6,8},{10,12},{4,2},{8,6},{12,10},{3,5},{7,9},{11,13},{5,3},... | collective-permute-start | bytes 1179656 | tf_op jit(solution)/shard_map/ppermute | solution.py:314
  44.6 2.6 %collective-permute-start.22 = (bf16[192,768]{1,0:T(8,128)(2,1)}, bf16[192,768]{1,0:T(8,128)(2,1)S(1)}, u32[]{:S(2)}, u32[]{:S(2)}) collective-permute-start(bf16[192,768]{1,0:T(8,128)(2,1)} %collective-permute-done.14), channel_id=1, source_target_pairs={{4,0},{8,12},{6,2},{10,14},{20,16},{24,28},{22,18},{26,30},{5,1},{... | collective-permute-start | bytes 884744 | tf_op jit(solution)/shard_map/ppermute | solution.py:299
  49.1 4.0 %collective-permute-done.19.refs_22_ = bf16[192,768]{1,0:T(8,128)(2,1)S(1)} collective-permute-done((bf16[192,768]{1,0:T(8,128)(2,1)S(1)}, bf16[192,768]{1,0:T(8,128)(2,1)S(1)}, u32[]{:S(2)}, u32[]{:S(2)}) %collective-permute-start.19) | collective-permute-done | bytes 294944 | tf_op jit(solution)/shard_map/ppermute | solution.py:299
  54.7 7.9 %collective-permute-start.21 = (bf16[192,768]{1,0:T(8,128)(2,1)S(1)}, bf16[192,768]{1,0:T(8,128)(2,1)S(1)}, u32[]{:S(2)}, u32[]{:S(2)}) collective-permute-start(bf16[192,768]{1,0:T(8,128)(2,1)S(1)} %broadcast_select_fusion.3.refs_21_), channel_id=1, source_target_pairs={{0,18},{4,22},{8,26},{12,30},{2,16},{6,20},{10,24},{14,28},{16,2},... | collective-permute-start | bytes 884744 | tf_op jit(solution)/shard_map/ppermute | solution.py:299
  62.5 4.0 %collective-permute-start.24 = (bf16[192,768]{1,0:T(8,128)(2,1)S(1)}, bf16[192,768]{1,0:T(8,128)(2,1)S(1)}, u32[]{:S(2)}, u32[]{:S(2)}) collective-permute-start(bf16[192,768]{1,0:T(8,128)(2,1)S(1)} %collective-permute-done.18), channel_id=1, source_target_pairs={{4,0},{8,12},{6,2},{10,14},{20,16},{24,28},{22,18},{26,30},{5,1},{... | collective-permute-start | bytes 884744 | tf_op jit(solution)/shard_map/ppermute | solution.py:299
  75.3 3.9 %collective-permute-done.25.refs_28_ = bf16[192,768]{1,0:T(8,128)(2,1)S(1)} collective-permute-done((bf16[192,768]{1,0:T(8,128)(2,1)S(1)}, bf16[192,768]{1,0:T(8,128)(2,1)S(1)}, u32[]{:S(2)}, u32[]{:S(2)}) %collective-permute-start.25) | collective-permute-done | bytes 294944 | tf_op jit(solution)/shard_map/ppermute | solution.py:299
  79.2 6.3 %collective-permute-done.26.refs_29_ = bf16[192,768]{1,0:T(8,128)(2,1)S(1)} collective-permute-done((bf16[192,768]{1,0:T(8,128)(2,1)S(1)}, bf16[192,768]{1,0:T(8,128)(2,1)S(1)}, u32[]{:S(2)}, u32[]{:S(2)}) %collective-permute-start.26) | collective-permute-done | bytes 294944 | tf_op jit(solution)/shard_map/ppermute | solution.py:299
  85.5 5.8 %collective-permute-done.27.refs_30_ = bf16[192,768]{1,0:T(8,128)(2,1)S(1)} collective-permute-done((bf16[192,768]{1,0:T(8,128)(2,1)S(1)}, bf16[192,768]{1,0:T(8,128)(2,1)S(1)}, u32[]{:S(2)}, u32[]{:S(2)}) %collective-permute-start.27) | collective-permute-done | bytes 294944 | tf_op jit(solution)/shard_map/ppermute | solution.py:299
  92.0 12.3 %attend.2 = (bf16[2,64,768]{2,1,0:T(8,128)(2,1)}, bf16[2,64,768]{2,1,0:T(8,128)(2,1)}) custom-call(s32[2,6]{1,0:T(2,128)} %refs_0_.7, bf16[2,64,1536]{2,1,0:T(8,128)(2,1)} %refs_3_.1, bf16[2,64,1536]{2,1,0:T(8,128)(2,1)} %copy-done.22, bf16[2,64,1536]{2,1,0:T(8,128)(2,1)} %copy-done.21, bf16[2,64,1536]{2,1,0:T(8,128)(2,1)} %copy-done.23, ...), custom_call_target="tpu_custom_call" | custom-call | tf_op jit(solution)/shard_map/attend/pallas_call | solution.py:413
  106.7 4.8 %project.2.refs_6_ = bf16[2,64,1536]{2,1,0:T(8,128)(2,1)} custom-call(s32[2,6]{1,0:T(2,128)} %refs_0_.7, bf16[2,64,768]{2,1,0:T(8,128)(2,1)} %get-tuple-element.41.refs_1_, bf16[2,64,768]{2,1,0:T(8,128)(2,1)} %copy-done.32, bf16[2,64,1536]{2,1,0:T(8,128)(2,1)} %refs_3_.1, bf16[6,2,1536]{2,1,0:T(2,128)(2,1)} %bitcast.27, bf16[1536,1536]{1,0:T(8,128)(2,1)} %bitcast.23), custom_call_target="tpu_custom_call" | custom-call | tf_op jit(solution)/shard_map/project/pallas_call | solution.py:388
  112.8 11.1 %collective-permute-done.29.refs_1_.refs_3_ = bf16[2,64,1536]{2,1,0:T(8,128)(2,1)S(1)} collective-permute-done((bf16[2,64,1536]{2,1,0:T(8,128)(2,1)}, bf16[2,64,1536]{2,1,0:T(8,128)(2,1)S(1)}, u32[]{:S(2)}, u32[]{:S(2)}) %collective-permute-start.29) | collective-permute-done | bytes 393248 | tf_op jit(solution)/shard_map/ppermute | solution.py:427
  125.9 2.7 %collective-permute-start.30 = (bf16[2,64,1536]{2,1,0:T(8,128)(2,1)S(1)}, bf16[2,64,1536]{2,1,0:T(8,128)(2,1)S(1)}, u32[]{:S(2)}, u32[]{:S(2)}) collective-permute-start(bf16[2,64,1536]{2,1,0:T(8,128)(2,1)S(1)} %collective-permute-done.29.refs_1_.refs_3_), channel_id=1, source_target_pairs={{0,2},{2,0},{4,6},{6,4},{8,10},{10,8},{12,14},{14,12},{1,3},{3,1},... | collective-permute-start | bytes 1179656 | tf_op jit(solution)/shard_map/ppermute | solution.py:411
  128.6 4.7 %collective-permute-done.31.refs_3_ = bf16[2,64,1536]{2,1,0:T(8,128)(2,1)S(1)} collective-permute-done((bf16[2,64,1536]{2,1,0:T(8,128)(2,1)S(1)}, bf16[2,64,1536]{2,1,0:T(8,128)(2,1)S(1)}, u32[]{:S(2)}, u32[]{:S(2)}) %collective-permute-start.31) | collective-permute-done | bytes 393248 | tf_op jit(solution)/shard_map/ppermute | solution.py:410
  136.3 12.3 %attend.3 = (bf16[2,64,768]{2,1,0:T(8,128)(2,1)}, bf16[2,64,768]{2,1,0:T(8,128)(2,1)}) custom-call(s32[2,6]{1,0:T(2,128)} %refs_0_.7, bf16[2,64,1536]{2,1,0:T(8,128)(2,1)} %copy-done.10, bf16[2,64,1536]{2,1,0:T(8,128)(2,1)} %copy-done.25, bf16[2,64,1536]{2,1,0:T(8,128)(2,1)} %copy-done.24, bf16[2,64,1536]{2,1,0:T(8,128)(2,1)} %copy-done.26, ...), custom_call_target="tpu_custom_call" | custom-call | tf_op jit(solution)/shard_map/attend/pallas_call | solution.py:413
  151.0 5.0 %project.3 = bf16[2,64,1536]{2,1,0:T(8,128)(2,1)} custom-call(s32[2,6]{1,0:T(2,128)} %refs_0_.7, bf16[2,64,768]{2,1,0:T(8,128)(2,1)} %get-tuple-element.43.refs_1_, bf16[2,64,768]{2,1,0:T(8,128)(2,1)} %copy-done.31, bf16[2,64,1536]{2,1,0:T(8,128)(2,1)} %copy-done.10, bf16[6,2,1536]{2,1,0:T(2,128)(2,1)} %bitcast.28, bf16[1536,1536]{1,0:T(8,128)(2,1)} %bitcast.24, ...), custom_call_target="tpu_custom_call" | custom-call | tf_op jit(solution)/shard_map/project/pallas_call | solution.py:388
  (123 shorter events, 35.0 us)
Async XLA Ops:
  1.4 9.9 %collective-permute-start.6 = (bf16[192,768]{1,0:T(8,128)(2,1)S(1)}, bf16[192,768]{1,0:T(8,128)(2,1)}, u32[]{:S(2)}, u32[]{:S(2)}) collective-permute-start(bf16[192,768]{1,0:T(8,128)(2,1)S(1)} %get-tuple-element.47.refs_7_), channel_id=1, source_target_pairs={{4,8},{8,4},{6,10},{10,6},{20,24},{24,20},{22,26},{26,22},{5,9},{9... | collective-permute-start | bytes 884744 | tf_op jit(solution)/shard_map/ppermute | solution.py:299
  4.7 13.0 %collective-permute-start.9 = (bf16[192,768]{1,0:T(8,128)(2,1)S(1)}, bf16[192,768]{1,0:T(8,128)(2,1)S(1)}, u32[]{:S(2)}, u32[]{:S(2)}) collective-permute-start(bf16[192,768]{1,0:T(8,128)(2,1)S(1)} %get-tuple-element.46.refs_8_), channel_id=1, source_target_pairs={{4,8},{8,4},{6,10},{10,6},{20,24},{24,20},{22,26},{26,22},{5,9},{9... | collective-permute-start | bytes 884744 | tf_op jit(solution)/shard_map/ppermute | solution.py:299
  7.3 15.4 %collective-permute-start.5 = (bf16[192,768]{1,0:T(8,128)(2,1)S(1)}, bf16[192,768]{1,0:T(8,128)(2,1)S(1)}, u32[]{:S(2)}, u32[]{:S(2)}) collective-permute-start(bf16[192,768]{1,0:T(8,128)(2,1)S(1)} %get-tuple-element.46.refs_8_), channel_id=1, source_target_pairs={{0,4},{4,0},{8,12},{12,8},{2,6},{6,2},{10,14},{14,10},{16,20},{20,... | collective-permute-start | bytes 884744 | tf_op jit(solution)/shard_map/ppermute | solution.py:299
  12.3 12.5 %collective-permute-start.11 = (bf16[192,768]{1,0:T(8,128)(2,1)S(1)}, bf16[192,768]{1,0:T(8,128)(2,1)S(1)}, u32[]{:S(2)}, u32[]{:S(2)}) collective-permute-start(bf16[192,768]{1,0:T(8,128)(2,1)S(1)} %get-tuple-element.25.refs_9_), channel_id=1, source_target_pairs={{4,8},{8,4},{6,10},{10,6},{20,24},{24,20},{22,26},{26,22},{5,9},{9... | collective-permute-start | bytes 884744 | tf_op jit(solution)/shard_map/ppermute | solution.py:299
  14.4 13.6 %collective-permute-start.7 = (bf16[192,768]{1,0:T(8,128)(2,1)S(1)}, bf16[192,768]{1,0:T(8,128)(2,1)S(1)}, u32[]{:S(2)}, u32[]{:S(2)}) collective-permute-start(bf16[192,768]{1,0:T(8,128)(2,1)S(1)} %get-tuple-element.25.refs_9_), channel_id=1, source_target_pairs={{0,4},{4,0},{8,12},{12,8},{2,6},{6,2},{10,14},{14,10},{16,20},{20,... | collective-permute-start | bytes 884744 | tf_op jit(solution)/shard_map/ppermute | solution.py:299
  14.5 16.7 %collective-permute-start.14 = (bf16[192,768]{1,0:T(8,128)(2,1)S(1)}, bf16[192,768]{1,0:T(8,128)(2,1)}, u32[]{:S(2)}, u32[]{:S(2)}) collective-permute-start(bf16[192,768]{1,0:T(8,128)(2,1)S(1)} %collective-permute-done.4.refs_13_), channel_id=1, source_target_pairs={{4,8},{8,4},{6,10},{10,6},{20,24},{24,20},{22,26},{26,22},{5,9},{9... | collective-permute-start | bytes 884744 | tf_op jit(solution)/shard_map/ppermute | solution.py:299
  17.7 14.9 %collective-permute-start.8 = (bf16[192,768]{1,0:T(8,128)(2,1)S(1)}, bf16[192,768]{1,0:T(8,128)(2,1)}, u32[]{:S(2)}, u32[]{:S(2)}) collective-permute-start(bf16[192,768]{1,0:T(8,128)(2,1)S(1)} %collective-permute-done.4.refs_13_), channel_id=1, source_target_pairs={{0,18},{4,22},{8,26},{12,30},{2,16},{6,20},{10,24},{14,28},{16,2},... | collective-permute-start | bytes 884744 | tf_op jit(solution)/shard_map/ppermute | solution.py:299
  22.7 12.9 %collective-permute-start.13 = (bf16[192,768]{1,0:T(8,128)(2,1)}, bf16[192,768]{1,0:T(8,128)(2,1)}, u32[]{:S(2)}, u32[]{:S(2)}) collective-permute-start(bf16[192,768]{1,0:T(8,128)(2,1)} %collective-permute-done.6), channel_id=1, source_target_pairs={{4,0},{8,12},{6,2},{10,14},{20,16},{24,28},{22,18},{26,30},{5,1},{... | collective-permute-start | bytes 884744 | tf_op jit(solution)/shard_map/ppermute | solution.py:299
  24.8 15.1 %collective-permute-start.16 = (bf16[192,768]{1,0:T(8,128)(2,1)S(1)}, bf16[192,768]{1,0:T(8,128)(2,1)}, u32[]{:S(2)}, u32[]{:S(2)}) collective-permute-start(bf16[192,768]{1,0:T(8,128)(2,1)S(1)} %collective-permute-done.5.refs_14_), channel_id=1, source_target_pairs={{4,8},{8,4},{6,10},{10,6},{20,24},{24,20},{22,26},{26,22},{5,9},{9... | collective-permute-start | bytes 884744 | tf_op jit(solution)/shard_map/ppermute | solution.py:299
  28.1 13.2 %collective-permute-start.10 = (bf16[192,768]{1,0:T(8,128)(2,1)S(1)}, bf16[192,768]{1,0:T(8,128)(2,1)}, u32[]{:S(2)}, u32[]{:S(2)}) collective-permute-start(bf16[192,768]{1,0:T(8,128)(2,1)S(1)} %collective-permute-done.5.refs_14_), channel_id=1, source_target_pairs={{0,18},{4,22},{8,26},{12,30},{2,16},{6,20},{10,24},{14,28},{16,2},... | collective-permute-start | bytes 884744 | tf_op jit(solution)/shard_map/ppermute | solution.py:299
  31.2 10.7 %collective-permute-start.15 = (bf16[192,768]{1,0:T(8,128)(2,1)}, bf16[192,768]{1,0:T(8,128)(2,1)S(1)}, u32[]{:S(2)}, u32[]{:S(2)}) collective-permute-start(bf16[192,768]{1,0:T(8,128)(2,1)} %copy-done.29), channel_id=1, source_target_pairs={{4,0},{8,12},{6,2},{10,14},{20,16},{24,28},{22,18},{26,30},{5,1},{... | collective-permute-start | bytes 884744 | tf_op jit(solution)/shard_map/ppermute | solution.py:299
  32.6 12.0 %collective-permute-start.18 = (bf16[192,768]{1,0:T(8,128)(2,1)S(1)}, bf16[192,768]{1,0:T(8,128)(2,1)S(1)}, u32[]{:S(2)}, u32[]{:S(2)}) collective-permute-start(bf16[192,768]{1,0:T(8,128)(2,1)S(1)} %collective-permute-done.7.refs_15_), channel_id=1, source_target_pairs={{4,8},{8,4},{6,10},{10,6},{20,24},{24,20},{22,26},{26,22},{5,9},{9... | collective-permute-start | bytes 884744 | tf_op jit(solution)/shard_map/ppermute | solution.py:299
  35.6 11.7 %collective-permute-start.12 = (bf16[192,768]{1,0:T(8,128)(2,1)S(1)}, bf16[192,768]{1,0:T(8,128)(2,1)S(1)}, u32[]{:S(2)}, u32[]{:S(2)}) collective-permute-start(bf16[192,768]{1,0:T(8,128)(2,1)S(1)} %collective-permute-done.7.refs_15_), channel_id=1, source_target_pairs={{0,18},{4,22},{8,26},{12,30},{2,16},{6,20},{10,24},{14,28},{16,2},... | collective-permute-start | bytes 884744 | tf_op jit(solution)/shard_map/ppermute | solution.py:299
  41.2 11.8 %collective-permute-start.19 = (bf16[192,768]{1,0:T(8,128)(2,1)S(1)}, bf16[192,768]{1,0:T(8,128)(2,1)S(1)}, u32[]{:S(2)}, u32[]{:S(2)}) collective-permute-start(bf16[192,768]{1,0:T(8,128)(2,1)S(1)} %broadcast_select_fusion.5.refs_19_), channel_id=1, source_target_pairs={{0,18},{4,22},{8,26},{12,30},{2,16},{6,20},{10,24},{14,28},{16,2},... | collective-permute-start | bytes 884744 | tf_op jit(solution)/shard_map/ppermute | solution.py:299
  41.9 20.6 %collective-permute-start.1 = (bf16[2,64,1536]{2,1,0:T(8,128)(2,1)}, bf16[2,64,1536]{2,1,0:T(8,128)(2,1)S(1)}, u32[]{:S(2)}, u32[]{:S(2)}) collective-permute-start(bf16[2,64,1536]{2,1,0:T(8,128)(2,1)} %refs_3_.1), channel_id=1, source_target_pairs={{2,4},{6,8},{10,12},{4,2},{8,6},{12,10},{3,5},{7,9},{11,13},{5,3},... | collective-permute-start | bytes 1179656 | tf_op jit(solution)/shard_map/ppermute | solution.py:314
  44.6 10.1 %collective-permute-start.22 = (bf16[192,768]{1,0:T(8,128)(2,1)}, bf16[192,768]{1,0:T(8,128)(2,1)S(1)}, u32[]{:S(2)}, u32[]{:S(2)}) collective-permute-start(bf16[192,768]{1,0:T(8,128)(2,1)} %collective-permute-done.14), channel_id=1, source_target_pairs={{4,0},{8,12},{6,2},{10,14},{20,16},{24,28},{22,18},{26,30},{5,1},{... | collective-permute-start | bytes 884744 | tf_op jit(solution)/shard_map/ppermute | solution.py:299
  47.4 26.2 %collective-permute-start.3 = (bf16[3,192,768]{2,1,0:T(8,128)(2,1)S(1)}, bf16[3,192,768]{2,1,0:T(8,128)(2,1)S(1)}, u32[]{:S(2)}, u32[]{:S(2)}) collective-permute-start(bf16[3,192,768]{2,1,0:T(8,128)(2,1)S(1)} %dynamic-slice_bitcast_fusion), channel_id=1, source_target_pairs={{0,2},{2,0},{4,6},{6,4},{8,10},{10,8},{12,14},{14,12},{1,3},{3,1},... | collective-permute-start | bytes 2654216 | tf_op jit(solution)/shard_map/ppermute | solution.py:315
  48.3 19.2 %collective-permute-start.20 = (bf16[192,768]{1,0:T(8,128)(2,1)S(1)}, bf16[192,768]{1,0:T(8,128)(2,1)S(1)}, u32[]{:S(2)}, u32[]{:S(2)}) collective-permute-start(bf16[192,768]{1,0:T(8,128)(2,1)S(1)} %broadcast_select_fusion.4.refs_20_), channel_id=1, source_target_pairs={{0,18},{4,22},{8,26},{12,30},{2,16},{6,20},{10,24},{14,28},{16,2},... | collective-permute-start | bytes 884744 | tf_op jit(solution)/shard_map/ppermute | solution.py:299
  53.1 14.6 %collective-permute-start.23 = (bf16[192,768]{1,0:T(8,128)(2,1)}, bf16[192,768]{1,0:T(8,128)(2,1)S(1)}, u32[]{:S(2)}, u32[]{:S(2)}) collective-permute-start(bf16[192,768]{1,0:T(8,128)(2,1)} %collective-permute-done.16), channel_id=1, source_target_pairs={{4,0},{8,12},{6,2},{10,14},{20,16},{24,28},{22,18},{26,30},{5,1},{... | collective-permute-start | bytes 884744 | tf_op jit(solution)/shard_map/ppermute | solution.py:299
  54.7 15.0 %collective-permute-start.21 = (bf16[192,768]{1,0:T(8,128)(2,1)S(1)}, bf16[192,768]{1,0:T(8,128)(2,1)S(1)}, u32[]{:S(2)}, u32[]{:S(2)}) collective-permute-start(bf16[192,768]{1,0:T(8,128)(2,1)S(1)} %broadcast_select_fusion.3.refs_21_), channel_id=1, source_target_pairs={{0,18},{4,22},{8,26},{12,30},{2,16},{6,20},{10,24},{14,28},{16,2},... | collective-permute-start | bytes 884744 | tf_op jit(solution)/shard_map/ppermute | solution.py:299
  62.5 9.8 %collective-permute-start.24 = (bf16[192,768]{1,0:T(8,128)(2,1)S(1)}, bf16[192,768]{1,0:T(8,128)(2,1)S(1)}, u32[]{:S(2)}, u32[]{:S(2)}) collective-permute-start(bf16[192,768]{1,0:T(8,128)(2,1)S(1)} %collective-permute-done.18), channel_id=1, source_target_pairs={{4,0},{8,12},{6,2},{10,14},{20,16},{24,28},{22,18},{26,30},{5,1},{... | collective-permute-start | bytes 884744 | tf_op jit(solution)/shard_map/ppermute | solution.py:299
  72.3 13.2 %collective-permute-start.26 = (bf16[192,768]{1,0:T(8,128)(2,1)S(1)}, bf16[192,768]{1,0:T(8,128)(2,1)S(1)}, u32[]{:S(2)}, u32[]{:S(2)}) collective-permute-start(bf16[192,768]{1,0:T(8,128)(2,1)S(1)} %broadcast_select_fusion.1.refs_26_), channel_id=1, source_target_pairs={{0,18},{4,22},{8,26},{12,30},{2,16},{6,20},{10,24},{14,28},{16,2},... | collective-permute-start | bytes 884744 | tf_op jit(solution)/shard_map/ppermute | solution.py:299
  73.6 17.7 %collective-permute-start.27 = (bf16[192,768]{1,0:T(8,128)(2,1)S(1)}, bf16[192,768]{1,0:T(8,128)(2,1)S(1)}, u32[]{:S(2)}, u32[]{:S(2)}) collective-permute-start(bf16[192,768]{1,0:T(8,128)(2,1)S(1)} %broadcast_select_fusion.refs_27_), channel_id=1, source_target_pairs={{0,18},{4,22},{8,26},{12,30},{2,16},{6,20},{10,24},{14,28},{16,2},... | collective-permute-start | bytes 884744 | tf_op jit(solution)/shard_map/ppermute | solution.py:299
  111.5 12.4 %collective-permute-start.29 = (bf16[2,64,1536]{2,1,0:T(8,128)(2,1)}, bf16[2,64,1536]{2,1,0:T(8,128)(2,1)S(1)}, u32[]{:S(2)}, u32[]{:S(2)}) collective-permute-start(bf16[2,64,1536]{2,1,0:T(8,128)(2,1)} %project.2.refs_6_), channel_id=1, source_target_pairs={{0,1},{2,3},{4,5},{6,7},{8,9},{10,11},{12,13},{14,15},{16,17},{18,... | collective-permute-start | bytes 1179656 | tf_op jit(solution)/shard_map/ppermute | solution.py:427
  (43 other events, 641.6 us)

commit v3 on v2

--- a/solution.py
+++ b/solution.py
@@ -68,62 +68,35 @@
     return order, sets, masks
 
 
-def attend_kernel(*refs):
-    views, own, pair, halo, pair_halo, modulation_src, gains = refs[:7]
-    pieces = refs[7:31]
-    att_own, att_pair = refs[31:33]
-    weights, normed, streams, modulation, sems, stream_sems = refs[33:]
-    _, micro_count, view_tok, width = streams.shape
-    rows = weights.shape[0] // 8
-    part = weights.shape[1] // 3
-    head = gains.shape[1]
-    order, sets, masks = attend_table(views)
-
-    def piece(index):
-        start = pl.multiple_of(order[index // 3] * rows, rows)
-        return pltpu.make_async_copy(
-            pieces[index],
-            weights.at[pl.ds(start, rows), pl.ds(index % 3 * part, part)],
-            sems.at[index],
-        )
-
-    sources = (own, pair, halo, pair_halo)
-    scales = pltpu.make_async_copy(modulation_src, modulation, stream_sems.at[4])
-    incoming = [
-        pltpu.make_async_copy(sources[slot], streams.at[slot], stream_sems.at[slot])
-        for slot in range(4)
-    ]
-    scales.start()
-    for slot in range(4):
-        incoming[slot].start()
-    for index in range(24):
-        piece(index).start()
-
+def normalise(source, m, slot, modulation, sets, normed, dtype=jnp.bfloat16):
+    micro_count, view_tok, _ = source.shape
+    wide = source[m].astype(jnp.float32)
+    average = jnp.mean(wide, axis=-1, keepdims=True)
+    squares = jnp.mean(wide * wide, axis=-1, keepdims=True)
+    spread = squares - average * average
+    factors = modulation[m, sets[m][slot]].astype(jnp.float32)
+    value = (wide - average) * lax.rsqrt(spread + epsilon) * (
+        1.0 + factors[1:2]
+    ) + factors[0:1]
     half = 2 * micro_count * view_tok
-    scales.wait()
-    for slot in range(4):
-        incoming[slot].wait()
-        for m in range(micro_count):
-            wide = streams[slot, m].astype(jnp.float32)
-            average = jnp.mean(wide, axis=-1, keepdims=True)
-            squares = jnp.mean(wide * wide, axis=-1, keepdims=True)
-            spread = squares - average * average
-            factors = modulation[m, sets[m][slot]].astype(jnp.float32)
-            value = (wide - average) * lax.rsqrt(spread + epsilon) * (
-                1.0 + factors[1:2]
-            ) + factors[0:1]
-            first = half * (slot // 2) + (2 * m + slot % 2) * view_tok
-            normed[first : first + view_tok, :] = value.astype(jnp.bfloat16)
-
-    for index in range(24):
-        piece(index).wait()
-
+    first = half * (slot // 2) + (2 * m + slot % 2) * view_tok
+    normed[first : first + view_tok, :] = value.astype(dtype)
+
+
+def norm_kernel(views, own, pair, halo, pair_halo, modulation, normed):
+    _, sets, _ = attend_table(views)
+    for slot, source in enumerate((own, pair, halo, pair_halo)):
+        for m in range(source.shape[0]):
+            normalise(source, m, slot, modulation, sets, normed)
+
+
+def set_masks(masks, view_tok):
     two = 2 * view_tok
     low_row = lax.broadcasted_iota(jnp.int32, (two, two), 0) < view_tok
     low_col = lax.broadcasted_iota(jnp.int32, (two, two), 1) < view_tok
     near_masks, far_masks = [], []
-    for m in range(micro_count):
-        together, below, above = (jnp.where(mask, 1.0, 0.0) for mask in masks[m])
+    for found in masks:
+        together, below, above = (jnp.where(mask, 1.0, 0.0) for mask in found)
         near_masks.append(jnp.where(low_row == low_col, 1.0, together))
         far_masks.append(
             jnp.where(
@@ -132,6 +105,15 @@
                 jnp.where(low_row | low_col, 0.0, above),
             )
         )
+    return near_masks, far_masks
+
+
+def attend_heads(normed, weights, gains, near_masks, far_masks, view_tok, outputs):
+    micro_count = len(near_masks)
+    part = weights.shape[1] // 3
+    head = gains.shape[1]
+    two = 2 * view_tok
+    half = micro_count * two
 
     def unit(values, gain):
         return (
@@ -148,42 +130,99 @@
             a, b, (((1,), (1,)), ((), ())), preferred_element_type=jnp.float32
         )
 
-    query_gain = gains[0:1, :]
-    key_gain = gains[1:2, :]
-    block = 2 * head
-
-    def heads(step, carry):
-        offset = pl.multiple_of(step * block, block)
-        raw_q = dot(normed[0:half, :], weights[:, pl.ds(offset, block)])
-        raw_k = dot(normed[...], weights[:, pl.ds(part + offset, block)])
-        raw_v = dot(normed[...], weights[:, pl.ds(2 * part + offset, block)])
-        outs = [[None] * 2 for _ in range(micro_count)]
-        for i in range(2):
-            cols = slice(i * head, (i + 1) * head)
-            queries = unit(raw_q[:, cols], query_gain)
-            keys = unit(raw_k[:, cols], key_gain)
-            values = raw_v[:, cols].astype(jnp.bfloat16)
-            for m in range(micro_count):
-                near = slice(m * two, (m + 1) * two)
-                far = slice(half + m * two, half + (m + 1) * two)
-                q = queries[near]
-                scale = head ** (-0.5)
-                e_near = jnp.exp(dot_t(q, keys[near]) * scale) * near_masks[m]
-                e_far = jnp.exp(dot_t(q, keys[far]) * scale) * far_masks[m]
-                total = jnp.sum(e_near, axis=-1, keepdims=True) + jnp.sum(
-                    e_far, axis=-1, keepdims=True
+    raw_q = dot(normed[0:half, :], weights[:, 0:part])
+    raw_k = dot(normed[...], weights[:, part : 2 * part])
+    raw_v = dot(normed[...], weights[:, 2 * part : 3 * part])
+    count = part // head
+    outs = [[None] * count for _ in range(micro_count)]
+    for i in range(count):
+        cols = slice(i * head, (i + 1) * head)
+        queries = unit(raw_q[:, cols], gains[0:1, :])
+        keys = unit(raw_k[:, cols], gains[1:2, :])
+        values = raw_v[:, cols].astype(jnp.bfloat16)
+        for m in range(micro_count):
+            near = slice(m * two, (m + 1) * two)
+            far = slice(half + m * two, half + (m + 1) * two)
+            q = queries[near]
+            scale = head ** (-0.5)
+            e_near = jnp.exp(dot_t(q, keys[near]) * scale) * near_masks[m]
+            e_far = jnp.exp(dot_t(q, keys[far]) * scale) * far_masks[m]
+            total = jnp.sum(e_near, axis=-1, keepdims=True) + jnp.sum(
+                e_far, axis=-1, keepdims=True
+            )
+            mixed = dot(e_near.astype(jnp.bfloat16), values[near]) + dot(
+                e_far.astype(jnp.bfloat16), values[far]
+            )
+            outs[m][i] = (mixed / total).astype(jnp.bfloat16)
+    att_own, att_pair, offset = outputs
+    for m in range(micro_count):
+        joined = jnp.concatenate(outs[m], axis=1)
+        att_own[m, :, offset : offset + part] = joined[:view_tok]
+        att_pair[m, :, offset : offset + part] = joined[view_tok:]
+
+
+def attend_part_kernel(index, *refs):
+    views, normed, gains = refs[:3]
+    pieces = refs[3:11]
+    att_own, att_pair, weights, sems = refs[-4:]
+    rows, part = pieces[0].shape[1:]
+    view_tok = att_own.shape[1]
+    order, _, masks = attend_table(views)
+    moves = []
+    for slot in range(8):
+        start = pl.multiple_of(order[slot] * rows, rows)
+        for kind in range(3):
+            moves.append(
+                pltpu.make_async_copy(
+                    pieces[slot].at[kind],
+                    weights.at[pl.ds(start, rows), pl.ds(kind * part, part)],
+                    sems.at[3 * slot + kind],
                 )
-                mixed = dot(e_near.astype(jnp.bfloat16), values[near]) + dot(
-                    e_far.astype(jnp.bfloat16), values[far]
-                )
-                outs[m][i] = (mixed / total).astype(jnp.bfloat16)
+            )
+    for move in moves:
+        move.start()
+    near_masks, far_masks = set_masks(masks, view_tok)
+    for move in moves:
+        move.wait()
+    attend_heads(
+        normed,
+        weights,
+        gains,
+        near_masks,
+        far_masks,
+        view_tok,
+        (att_own, att_pair, index * part),
+    )
+
+
+def attend_kernel(*refs):
+    views, own, pair, halo, pair_halo, modulation, gains = refs[:7]
+    weights = refs[7:10]
+    att_own, att_pair, normed, streams, sems = refs[10:]
+    micro_count, view_tok, _ = own.shape
+    _, sets, masks = attend_table(views)
+    incoming = [
+        pltpu.make_async_copy(source, streams.at[slot], sems.at[slot])
+        for slot, source in enumerate((own, pair, halo, pair_halo))
+    ]
+    for move in incoming:
+        move.start()
+    near_masks, far_masks = set_masks(masks, view_tok)
+    for slot in range(4):
+        incoming[slot].wait()
         for m in range(micro_count):
-            joined = jnp.concatenate(outs[m], axis=1)
-            att_own[m, :, pl.ds(offset, block)] = joined[:view_tok]
-            att_pair[m, :, pl.ds(offset, block)] = joined[view_tok:]
-        return carry
-
-    lax.fori_loop(0, part // block, heads, 0)
+            normalise(streams.at[slot], m, slot, modulation, sets, normed)
+    part = weights[0].shape[1] // 3
+    for index in range(3):
+        attend_heads(
+            normed,
+            weights[index],
+            gains,
+            near_masks,
+            far_masks,
+            view_tok,
+            (att_own, att_pair, index * part),
+        )
 
 
 def project_kernel(last, *refs):
@@ -191,26 +230,19 @@
     refs = refs[6:]
     if last:
         keep_src, refs = refs[0], refs[1:]
-    result, weights, att_own, att_got, stream, gates = refs[:6]
-    refs = refs[6:]
+    result, att_own, att_got, stream, gates = refs[:5]
+    refs = refs[5:]
     if last:
         keep, refs = refs[0], refs[1:]
-    sems, small_sems = refs
+    (small_sems,) = refs
     micro_count, view_tok, part = att_own.shape
     width = out_weight.shape[1]
     place = lax.axis_index("seq")
     mine = (place + lax.axis_index("groups")) % 2
     newest = lax.axis_index("section") == lax.axis_size("section") - 1
     sets = [owner_of(views, m, place) for m in range(views.shape[0])]
-    blocks = sems.shape[0]
+    blocks = 3
     block = width // blocks
-
-    def piece(index):
-        return pltpu.make_async_copy(
-            out_weight.at[:, pl.ds(index * block, block)],
-            weights.at[:, pl.ds(index * block, block)],
-            sems.at[index],
-        )
 
     moves = [
         (att_own_src, att_own),
@@ -226,8 +258,6 @@
     ]
     for copy in copies:
         copy.start()
-    for index in range(blocks):
-        piece(index).start()
     for copy in copies:
         copy.wait()
     tokens = micro_count * view_tok
@@ -236,13 +266,12 @@
     first = pl.multiple_of(mine * part, part)
     second = pl.multiple_of((1 - mine) * part, part)
     for index in range(blocks):
-        piece(index).wait()
         cols = slice(index * block, (index + 1) * block)
         mixed = jnp.dot(
-            here, weights[pl.ds(first, part), cols], preferred_element_type=jnp.float32
+            here, out_weight[pl.ds(first, part), cols], preferred_element_type=jnp.float32
         ) + jnp.dot(
             there,
-            weights[pl.ds(second, part), cols],
+            out_weight[pl.ds(second, part), cols],
             preferred_element_type=jnp.float32,
         )
         for m in range(micro_count):
@@ -304,15 +333,19 @@
     ]
 
     by_kind = jnp.transpose(qkv_weight[0], (1, 0, 2))
-    home = [
-        lax.dynamic_slice(by_kind, (kind, 0, mine * part), (1, rows, part))[0]
-        for kind in range(3)
-    ]
-    lent = lax.dynamic_slice(by_kind, (0, 0, (1 - mine) * part), (3, rows, part))
+    third_part = part // 3
+
+    def columns(which, index):
+        return lax.dynamic_slice(
+            by_kind, (0, 0, which * part + index * third_part), (3, rows, third_part)
+        )
+
+    home = [columns(mine, index) for index in range(3)]
+    lent = [columns(1 - mine, index) for index in range(3)]
 
     pair = lax.ppermute(stream, "seq", swap_cores)
     halo = lax.ppermute(stream, "seq", swap_edges)
-    home_pair = lax.ppermute(lent, "seq", swap_cores)
+    home_pair = lax.ppermute(jnp.stack(lent), "seq", swap_cores)
     pair_halo = lax.ppermute(halo, "seq", swap_cores)
     first_exchange = (pair, halo, pair_halo)
 
@@ -348,58 +381,75 @@
         across_third.append(send(third[kind], opposite))
         before = (outer_last[kind],)
 
-    pieces = (
-        home
-        + [home_pair[kind] for kind in range(3)]
-        + from_outer
-        + across_first
-        + second
-        + across_second
-        + third
-        + across_third
-    )
-
     section_place = lax.axis_index("section")
     gates = jnp.transpose(set_gate[0], (1, 0, 2))
 
     vmem = pl.BlockSpec(memory_space=pltpu.VMEM)
     smem = pl.BlockSpec(memory_space=pltpu.SMEM)
-    anywhere = pl.BlockSpec(memory_space=pltpu.HBM)
+    anywhere = pl.BlockSpec(memory_space=pl.ANY)
     half_shape = jax.ShapeDtypeStruct((micro_count, view_tok, part), jnp.bfloat16)
+    normed_shape = (4 * micro_count * view_tok, width)
+    mega = 1024 * 1024
+
+    def limit(size):
+        return pltpu.CompilerParams(vmem_limit_bytes=size * mega)
+
+    norm = pl.pallas_call(
+        norm_kernel,
+        out_shape=jax.ShapeDtypeStruct(normed_shape, jnp.bfloat16),
+        in_specs=[smem] + [vmem] * 5,
+        out_specs=vmem,
+        compiler_params=limit(12),
+        name="norm",
+    )
+
+    def attend_part(index, normed, pieces, earlier):
+        return pl.pallas_call(
+            functools.partial(attend_part_kernel, index),
+            out_shape=(
+                half_shape,
+                half_shape,
+                jax.ShapeDtypeStruct((width, part), jnp.bfloat16),
+            ),
+            in_specs=[smem, vmem, vmem] + [anywhere] * 8 + [vmem] * len(earlier),
+            out_specs=(vmem, vmem, vmem),
+            scratch_shapes=[pltpu.SemaphoreType.DMA((24,))],
+            input_output_aliases={11: 0, 12: 1} if earlier else {},
+            compiler_params=limit(20),
+            name="attend_part",
+        )(set_views, normed, norm_gain[0], *pieces, *earlier)
+
     attend = pl.pallas_call(
         attend_kernel,
         out_shape=(half_shape, half_shape),
-        in_specs=[smem] + [anywhere] * 5 + [vmem] + [anywhere] * 24,
+        in_specs=[smem] + [anywhere] * 4 + [vmem] * 5,
         out_specs=(vmem, vmem),
         scratch_shapes=[
-            pltpu.VMEM((width, 3 * part), jnp.bfloat16),
-            pltpu.VMEM((4 * micro_count * view_tok, width), jnp.bfloat16),
+            pltpu.VMEM(normed_shape, jnp.bfloat16),
             pltpu.VMEM((4,) + stream.shape, jnp.bfloat16),
-            pltpu.VMEM(modulation.shape[1:], jnp.bfloat16),
-            pltpu.SemaphoreType.DMA((24,)),
-            pltpu.SemaphoreType.DMA((5,)),
+            pltpu.SemaphoreType.DMA((4,)),
         ],
-        compiler_params=pltpu.CompilerParams(vmem_limit_bytes=60 * 1024 * 1024),
+        compiler_params=limit(24),
         name="attend",
     )
 
     def project(last, *operands):
         spare = [pltpu.VMEM(stream.shape, jnp.bfloat16)] if last else []
+        in_specs = [smem] + [anywhere] * 4 + [vmem] + [anywhere] * last
         return pl.pallas_call(
             functools.partial(project_kernel, last),
             out_shape=jax.ShapeDtypeStruct(stream.shape, jnp.bfloat16),
-            in_specs=[smem] + [anywhere] * (len(operands) - 1),
+            in_specs=in_specs,
             out_specs=vmem,
             scratch_shapes=[
-                pltpu.VMEM((width, width), jnp.bfloat16),
                 pltpu.VMEM((micro_count, view_tok, part), jnp.bfloat16),
                 pltpu.VMEM((micro_count, view_tok, part), jnp.bfloat16),
                 pltpu.VMEM(stream.shape, jnp.bfloat16),
                 pltpu.VMEM(gates.shape, jnp.bfloat16),
             ]
             + spare
-            + [pltpu.SemaphoreType.DMA((3,)), pltpu.SemaphoreType.DMA((5,))],
-            compiler_params=pltpu.CompilerParams(vmem_limit_bytes=60 * 1024 * 1024),
+            + [pltpu.SemaphoreType.DMA((5,))],
+            compiler_params=limit(12),
             name="project",
         )(*operands)
 
@@ -410,9 +460,33 @@
             halo = lax.ppermute(own, "seq", swap_edges)
             pair = lax.ppermute(own, "seq", swap_cores)
             pair_halo = lax.ppermute(halo, "seq", swap_cores)
-        att_own, att_pair = attend(
-            set_views, own, pair, halo, pair_halo, modulation[0], norm_gain[0], *pieces
-        )
+            att_own, att_pair = attend(
+                set_views,
+                own,
+                pair,
+                halo,
+                pair_halo,
+                modulation[0],
+                norm_gain[0],
+                *assembled,
+            )
+        else:
+            normed = norm(set_views, own, pair, halo, pair_halo, modulation[0])
+            earlier, assembled = (), []
+            for index in range(3):
+                pieces = [
+                    home[index],
+                    home_pair[index],
+                    from_outer[index],
+                    across_first[index],
+                    second[index],
+                    across_second[index],
+                    third[index],
+                    across_third[index],
+                ]
+                *earlier, joined = attend_part(index, normed, pieces, earlier)
+                assembled.append(joined)
+            att_own, att_pair = earlier
         att_got = lax.ppermute(att_pair, "seq", swap_cores)
         operands = (set_views, att_own, att_got, own, gates, out_weight[0])
         if moment > 0 and moment + 1 == section_count:

time: 158 us -> 138 us (0.87)
  starting transfers between devices: 64.6 us -> 51.5 us
  Pallas kernels: 34.3 us -> 25.1 us
  waiting for transfers between devices: 48.2 us -> 53 us
  local copies, waits for them, and re-layouts: 5.2 us -> 1.68 us
    pallas_call x2 -> x1, Pallas kernels: 24.5 us -> 8.15 us  [paired_body(): attend(set_views, own, pair, halo, pair_halo, modulation[0], norm_gain[0]...]
    ppermute x24, starting transfers between devices: 53.5 us -> 40.5 us  [send(): return lax.ppermute(value, line_axes, pairs)]
    pallas_call x0 -> x4, Pallas kernels: none -> 11.7 us  [the longest x3 10 us: attend_part(): pl.pallas_call(functools.partial(attend_part_kernel, index), out_shape=(h...]
    ppermute x24, waiting for transfers between devices: 28.4 us -> 33.5 us  [send(): return lax.ppermute(value, line_axes, pairs)]
    pallas_call x2, Pallas kernels: 9.76 us -> 5.24 us  [project(): pl.pallas_call(functools.partial(project_kernel, last), out_shape=jax.Sha...]
    unnamed x66 -> x20, local copies, waits for them, and re-layouts: 2.85 us -> 0.05 us
    squeeze x2 -> x1, local copies, waits for them, and re-layouts: 2.29 us -> 0.06 us  [paired_body(): home_pair[index]]
    select_n x3, other arithmetic: 1.06 us -> 3.01 us  [paired_body(): second.append(jnp.where(middle, from_inner[kind], b))]
  transfers between devices with their start and end apart: 34 -> 34, of which waited for: 15 -> 16; matrix products, arithmetic and copies ran while one was open for 3% -> 3% of each run, Pallas kernels for 0% -> 6%
where the time goes in v3:
time: 138 us; the launch traced here: 136 us
  waiting for transfers between devices  53 us (38%)
  starting transfers between devices  51.5 us (37%)
  Pallas kernels  25.1 us (18%)
  other arithmetic  4.14 us (3%)
  local copies, waits for them, and re-layouts  1.68 us (1%)
    ppermute x24, starting transfers between devices, send(): return lax.ppermute(value, line_axes, pairs)  40.5 us
    ppermute x24, waiting for transfers between devices, send(): return lax.ppermute(value, line_axes, pairs)  33.5 us
    ppermute x1, waiting for transfers between devices, paired_body(): lax.ppermute(result, 'section', [(i, i + 1) for i in range(section_count...  11.2 us
    pallas_call x3, Pallas kernels, attend_part(): pl.pallas_call(functools.partial(attend_part_kernel, index), out_shape=(h...  10 us
    pallas_call x1, Pallas kernels, paired_body(): attend(set_views, own, pair, halo, pair_halo, modulation[0], norm_gain[0]...  8.15 us
    pallas_call x2, Pallas kernels, project(): pl.pallas_call(functools.partial(project_kernel, last), out_shape=jax.Sha...  5.24 us
    ppermute x1, waiting for transfers between devices, paired_body(): halo = lax.ppermute(own, 'seq', swap_edges)  4.43 us
    ppermute x1, starting transfers between devices, paired_body(): halo = lax.ppermute(own, 'seq', swap_edges)  3.09 us
  transfers between devices with their start and end apart: 34, of which 16 were waited for; matrix products, arithmetic and copies ran while one was open for 3% of the time, Pallas kernels for 6%

profile of v3, /device:TPU:11, one launch (start us, length us, event | category | flops | bytes accessed | tf_op | source)
XLA Modules:
  0.0 136.0 jit_solution(10606233686574068592)
XLA Ops:
  1.6 3.3 %collective-permute-start.5 = (bf16[3,192,256]{2,1,0:T(8,128)(2,1)S(1)}, bf16[3,192,256]{2,1,0:T(8,128)(2,1)}, u32[]{:S(2)}, u32[]{:S(2)}) collective-permute-start(bf16[3,192,256]{2,1,0:T(8,128)(2,1)S(1)} %get-tuple-element.64.refs_3_), channel_id=1, source_target_pairs={{4,8},{8,4},{6,10},{10,6},{20,24},{24,20},{22,26},{26,22},{5,9},{9... | collective-permute-start | bytes 884744 | tf_op jit(solution)/shard_map/ppermute | solution.py:328
  5.0 2.6 %collective-permute-start.9 = (bf16[3,192,256]{2,1,0:T(8,128)(2,1)S(1)}, bf16[3,192,256]{2,1,0:T(8,128)(2,1)}, u32[]{:S(2)}, u32[]{:S(2)}) collective-permute-start(bf16[3,192,256]{2,1,0:T(8,128)(2,1)S(1)} %get-tuple-element.59.refs_3_), channel_id=1, source_target_pairs={{4,8},{8,4},{6,10},{10,6},{20,24},{24,20},{22,26},{26,22},{5,9},{9... | collective-permute-start | bytes 884744 | tf_op jit(solution)/shard_map/ppermute | solution.py:328
  7.8 3.8 %collective-permute-done.5 = bf16[3,192,256]{2,1,0:T(8,128)(2,1)} collective-permute-done((bf16[3,192,256]{2,1,0:T(8,128)(2,1)S(1)}, bf16[3,192,256]{2,1,0:T(8,128)(2,1)}, u32[]{:S(2)}, u32[]{:S(2)}) %collective-permute-start.5) | collective-permute-done | bytes 294944 | tf_op jit(solution)/shard_map/ppermute | solution.py:328
  12.7 2.1 %collective-permute-start.7 = (bf16[3,192,256]{2,1,0:T(8,128)(2,1)S(1)}, bf16[3,192,256]{2,1,0:T(8,128)(2,1)S(1)}, u32[]{:S(2)}, u32[]{:S(2)}) collective-permute-start(bf16[3,192,256]{2,1,0:T(8,128)(2,1)S(1)} %get-tuple-element.32.refs_3_), channel_id=1, source_target_pairs={{4,8},{8,4},{6,10},{10,6},{20,24},{24,20},{22,26},{26,22},{5,9},{9... | collective-permute-start | bytes 884744 | tf_op jit(solution)/shard_map/ppermute | solution.py:328
  14.9 3.0 %collective-permute-done.9 = bf16[3,192,256]{2,1,0:T(8,128)(2,1)} collective-permute-done((bf16[3,192,256]{2,1,0:T(8,128)(2,1)S(1)}, bf16[3,192,256]{2,1,0:T(8,128)(2,1)}, u32[]{:S(2)}, u32[]{:S(2)}) %collective-permute-start.9) | collective-permute-done | bytes 294944 | tf_op jit(solution)/shard_map/ppermute | solution.py:328
  19.0 4.3 %collective-permute-start.19 = (bf16[3,192,256]{2,1,0:T(8,128)(2,1)S(1)}, bf16[3,192,256]{2,1,0:T(8,128)(2,1)S(1)}, u32[]{:S(2)}, u32[]{:S(2)}) collective-permute-start(bf16[3,192,256]{2,1,0:T(8,128)(2,1)S(1)} %collective-permute-done.8.refs_5_), channel_id=1, source_target_pairs={{0,18},{4,22},{8,26},{12,30},{2,16},{6,20},{10,24},{14,28},{16,2},... | collective-permute-start | bytes 884744 | tf_op jit(solution)/shard_map/ppermute | solution.py:328
  27.4 3.2 %collective-permute-start.17 = (bf16[3,192,256]{2,1,0:T(8,128)(2,1)S(1)}, bf16[3,192,256]{2,1,0:T(8,128)(2,1)S(1)}, u32[]{:S(2)}, u32[]{:S(2)}) collective-permute-start(bf16[3,192,256]{2,1,0:T(8,128)(2,1)S(1)} %collective-permute-done.4.refs_5_), channel_id=1, source_target_pairs={{4,8},{8,4},{6,10},{10,6},{20,24},{24,20},{22,26},{26,22},{5,9},{9... | collective-permute-start | bytes 884744 | tf_op jit(solution)/shard_map/ppermute | solution.py:328
  34.2 2.1 %collective-permute-start.12 = (bf16[3,192,256]{2,1,0:T(8,128)(2,1)S(1)}, bf16[3,192,256]{2,1,0:T(8,128)(2,1)S(1)}, u32[]{:S(2)}, u32[]{:S(2)}) collective-permute-start(bf16[3,192,256]{2,1,0:T(8,128)(2,1)S(1)} %collective-permute-done.6.refs_5_), channel_id=1, source_target_pairs={{4,8},{8,4},{6,10},{10,6},{20,24},{24,20},{22,26},{26,22},{5,9},{9... | collective-permute-start | bytes 884744 | tf_op jit(solution)/shard_map/ppermute | solution.py:328
  38.4 2.1 %collective-permute-done.17 = bf16[3,192,256]{2,1,0:T(8,128)(2,1)S(1)} collective-permute-done((bf16[3,192,256]{2,1,0:T(8,128)(2,1)S(1)}, bf16[3,192,256]{2,1,0:T(8,128)(2,1)S(1)}, u32[]{:S(2)}, u32[]{:S(2)}) %collective-permute-start.17) | collective-permute-done | bytes 294944 | tf_op jit(solution)/shard_map/ppermute | solution.py:328
  48.5 2.9 %collective-permute-start.1 = (bf16[2,64,1536]{2,1,0:T(8,128)(2,1)S(1)}, bf16[2,64,1536]{2,1,0:T(8,128)(2,1)S(1)}, u32[]{:S(2)}, u32[]{:S(2)}) collective-permute-start(bf16[2,64,1536]{2,1,0:T(8,128)(2,1)S(1)} %copy-done), channel_id=1, source_target_pairs={{2,4},{6,8},{10,12},{4,2},{8,6},{12,10},{3,5},{7,9},{11,13},{5,3},... | collective-permute-start | bytes 1179656 | tf_op jit(solution)/shard_map/ppermute | solution.py:347
  51.5 3.7 %collective-permute-done.20 = bf16[3,192,256]{2,1,0:T(8,128)(2,1)S(1)} collective-permute-done((bf16[3,192,256]{2,1,0:T(8,128)(2,1)}, bf16[3,192,256]{2,1,0:T(8,128)(2,1)S(1)}, u32[]{:S(2)}, u32[]{:S(2)}) %collective-permute-start.20) | collective-permute-done | bytes 294944 | tf_op jit(solution)/shard_map/ppermute | solution.py:328
  58.0 3.4 %collective-permute-done.24 = bf16[3,192,256]{2,1,0:T(8,128)(2,1)S(1)} collective-permute-done((bf16[3,192,256]{2,1,0:T(8,128)(2,1)S(1)}, bf16[3,192,256]{2,1,0:T(8,128)(2,1)S(1)}, u32[]{:S(2)}, u32[]{:S(2)}) %collective-permute-start.24) | collective-permute-done | bytes 294944 | tf_op jit(solution)/shard_map/ppermute | solution.py:328
  61.4 4.1 %collective-permute-start.16 = (bf16[3,192,256]{2,1,0:T(8,128)(2,1)S(1)}, bf16[3,192,256]{2,1,0:T(8,128)(2,1)S(1)}, u32[]{:S(2)}, u32[]{:S(2)}) collective-permute-start(bf16[3,192,256]{2,1,0:T(8,128)(2,1)S(1)} %collective-permute-done.12), channel_id=1, source_target_pairs={{4,0},{8,12},{6,2},{10,14},{20,16},{24,28},{22,18},{26,30},{5,1},{... | collective-permute-start | bytes 884744 | tf_op jit(solution)/shard_map/ppermute | solution.py:328
  66.2 3.1 %collective-permute-done.15.refs_8_ = bf16[3,192,256]{2,1,0:T(8,128)(2,1)S(1)} collective-permute-done((bf16[3,192,256]{2,1,0:T(8,128)(2,1)S(1)}, bf16[3,192,256]{2,1,0:T(8,128)(2,1)S(1)}, u32[]{:S(2)}, u32[]{:S(2)}) %collective-permute-start.15) | collective-permute-done | bytes 294944 | tf_op jit(solution)/shard_map/ppermute | solution.py:328
  75.6 9.7 %collective-permute-done.27.refs_10_ = bf16[3,192,256]{2,1,0:T(8,128)(2,1)S(1)} collective-permute-done((bf16[3,192,256]{2,1,0:T(8,128)(2,1)S(1)}, bf16[3,192,256]{2,1,0:T(8,128)(2,1)S(1)}, u32[]{:S(2)}, u32[]{:S(2)}) %collective-permute-start.27) | collective-permute-done | bytes 294944 | tf_op jit(solution)/shard_map/ppermute | solution.py:328
  85.3 3.3 %attend_part.3 = (bf16[2,64,768]{2,1,0:T(8,128)(2,1)S(1)}, bf16[2,64,768]{2,1,0:T(8,128)(2,1)S(1)}, bf16[1536,768]{1,0:T(8,128)(2,1)S(1)}) custom-call(s32[2,6]{1,0:T(2,128)S(1)} %copy-done.3, bf16[512,1536]{1,0:T(8,128)(2,1)S(1)} %norm.1.refs_1_, f32[2,128]{1,0:T(2,128)S(1)} %bitcast.51, bf16[3,192,256]{2,1,0:T(8,128)(2,1)S(1)} %get-tuple-element.64.refs_3_, ...), custom_call_target="tpu_custom_call" | custom-call | tf_op jit(solution)/shard_map/attend_part/pallas_call | solution.py:407
  88.7 3.4 %attend_part.4 = (bf16[2,64,768]{2,1,0:T(8,128)(2,1)S(1)}, bf16[2,64,768]{2,1,0:T(8,128)(2,1)S(1)}, bf16[1536,768]{1,0:T(8,128)(2,1)S(1)}) custom-call(s32[2,6]{1,0:T(2,128)S(1)} %copy-done.3, bf16[512,1536]{1,0:T(8,128)(2,1)S(1)} %norm.1.refs_1_, f32[2,128]{1,0:T(2,128)S(1)} %bitcast.52, ...), custom_call_target="tpu_custom_call", output_to_operand_aliasing={{0}: (11, {}), {1}: (12, {})} | custom-call | tf_op jit(solution)/shard_map/attend_part/pallas_call | solution.py:407
  92.1 3.4 %attend_part.5 = (bf16[2,64,768]{2,1,0:T(8,128)(2,1)S(1)}, bf16[2,64,768]{2,1,0:T(8,128)(2,1)S(1)}, bf16[1536,768]{1,0:T(8,128)(2,1)S(1)}) custom-call(s32[2,6]{1,0:T(2,128)S(1)} %copy-done.3, bf16[512,1536]{1,0:T(8,128)(2,1)S(1)} %norm.1.refs_1_, f32[2,128]{1,0:T(2,128)S(1)} %bitcast.53, ...), custom_call_target="tpu_custom_call", output_to_operand_aliasing={{0}: (11, {}), {1}: (12, {})} | custom-call | tf_op jit(solution)/shard_map/attend_part/pallas_call | solution.py:407
  96.9 2.1 %project.2.refs_6_ = bf16[2,64,1536]{2,1,0:T(8,128)(2,1)S(1)} custom-call(s32[2,6]{1,0:T(2,128)S(1)} %copy-done.3, bf16[2,64,768]{2,1,0:T(8,128)(2,1)S(1)} %get-tuple-element.52.refs_1_, bf16[2,64,768]{2,1,0:T(8,128)(2,1)S(1)} %collective-permute-done.28.refs_2_, bf16[2,64,1536]{2,1,0:T(8,128)(2,1)S(1)} %copy-done, bf16[6,2,1536]{2,1,0:T(2,128)(2,1)S(1)} %bitcast.49, ...), custom_call_target="tpu_custom_call" | custom-call | tf_op jit(solution)/shard_map/project/pallas_call | solution.py:439
  100.4 11.2 %collective-permute-done.29.refs_1_.refs_3_ = bf16[2,64,1536]{2,1,0:T(8,128)(2,1)S(1)} collective-permute-done((bf16[2,64,1536]{2,1,0:T(8,128)(2,1)S(1)}, bf16[2,64,1536]{2,1,0:T(8,128)(2,1)S(1)}, u32[]{:S(2)}, u32[]{:S(2)}) %collective-permute-start.29) | collective-permute-done | bytes 393248 | tf_op jit(solution)/shard_map/ppermute | solution.py:501
  111.6 3.1 %collective-permute-start.31 = (bf16[2,64,1536]{2,1,0:T(8,128)(2,1)S(1)}, bf16[2,64,1536]{2,1,0:T(8,128)(2,1)S(1)}, u32[]{:S(2)}, u32[]{:S(2)}) collective-permute-start(bf16[2,64,1536]{2,1,0:T(8,128)(2,1)S(1)} %collective-permute-done.29.refs_1_.refs_3_), channel_id=1, source_target_pairs={{2,4},{6,8},{10,12},{4,2},{8,6},{12,10},{3,5},{7,9},{11,13},{5,3},... | collective-permute-start | bytes 1179656 | tf_op jit(solution)/shard_map/ppermute | solution.py:460
  116.5 4.4 %collective-permute-done.31.refs_3_ = bf16[2,64,1536]{2,1,0:T(8,128)(2,1)S(1)} collective-permute-done((bf16[2,64,1536]{2,1,0:T(8,128)(2,1)S(1)}, bf16[2,64,1536]{2,1,0:T(8,128)(2,1)S(1)}, u32[]{:S(2)}, u32[]{:S(2)}) %collective-permute-start.31) | collective-permute-done | bytes 393248 | tf_op jit(solution)/shard_map/ppermute | solution.py:460
  123.1 8.2 %attend.1 = (bf16[2,64,768]{2,1,0:T(8,128)(2,1)S(1)}, bf16[2,64,768]{2,1,0:T(8,128)(2,1)S(1)}) custom-call(s32[2,6]{1,0:T(2,128)S(1)} %copy-done.3, bf16[2,64,1536]{2,1,0:T(8,128)(2,1)S(1)} %collective-permute-done.29.refs_1_.refs_3_, bf16[2,64,1536]{2,1,0:T(8,128)(2,1)S(1)} %collective-permute-done.30.refs_2_, ...), custom_call_target="tpu_custom_call" | custom-call | tf_op jit(solution)/shard_map/attend/pallas_call | solution.py:463
  132.7 3.1 %project.3 = bf16[2,64,1536]{2,1,0:T(8,128)(2,1)} custom-call(s32[2,6]{1,0:T(2,128)S(1)} %copy-done.3, bf16[2,64,768]{2,1,0:T(8,128)(2,1)S(1)} %get-tuple-element.57.refs_1_, bf16[2,64,768]{2,1,0:T(8,128)(2,1)S(1)} %collective-permute-done.33.refs_2_, bf16[2,64,1536]{2,1,0:T(8,128)(2,1)S(1)} %collective-permute-done.29.refs_1_.refs_3_, ...), custom_call_target="tpu_custom_call" | custom-call | tf_op jit(solution)/shard_map/project/pallas_call | solution.py:439
  (81 shorter events, 39.8 us)
Async XLA Ops:
  5.0 12.9 %collective-permute-start.9 = (bf16[3,192,256]{2,1,0:T(8,128)(2,1)S(1)}, bf16[3,192,256]{2,1,0:T(8,128)(2,1)}, u32[]{:S(2)}, u32[]{:S(2)}) collective-permute-start(bf16[3,192,256]{2,1,0:T(8,128)(2,1)S(1)} %get-tuple-element.59.refs_3_), channel_id=1, source_target_pairs={{4,8},{8,4},{6,10},{10,6},{20,24},{24,20},{22,26},{26,22},{5,9},{9... | collective-permute-start | bytes 884744 | tf_op jit(solution)/shard_map/ppermute | solution.py:328
  7.6 11.4 %collective-permute-start.8 = (bf16[3,192,256]{2,1,0:T(8,128)(2,1)S(1)}, bf16[3,192,256]{2,1,0:T(8,128)(2,1)S(1)}, u32[]{:S(2)}, u32[]{:S(2)}) collective-permute-start(bf16[3,192,256]{2,1,0:T(8,128)(2,1)S(1)} %get-tuple-element.59.refs_3_), channel_id=1, source_target_pairs={{0,4},{4,0},{8,12},{12,8},{2,6},{6,2},{10,14},{14,10},{16,20},{20,... | collective-permute-start | bytes 884744 | tf_op jit(solution)/shard_map/ppermute | solution.py:328
  12.7 14.8 %collective-permute-start.7 = (bf16[3,192,256]{2,1,0:T(8,128)(2,1)S(1)}, bf16[3,192,256]{2,1,0:T(8,128)(2,1)S(1)}, u32[]{:S(2)}, u32[]{:S(2)}) collective-permute-start(bf16[3,192,256]{2,1,0:T(8,128)(2,1)S(1)} %get-tuple-element.32.refs_3_), channel_id=1, source_target_pairs={{4,8},{8,4},{6,10},{10,6},{20,24},{24,20},{22,26},{26,22},{5,9},{9... | collective-permute-start | bytes 884744 | tf_op jit(solution)/shard_map/ppermute | solution.py:328
  14.8 15.9 %collective-permute-start.6 = (bf16[3,192,256]{2,1,0:T(8,128)(2,1)S(1)}, bf16[3,192,256]{2,1,0:T(8,128)(2,1)S(1)}, u32[]{:S(2)}, u32[]{:S(2)}) collective-permute-start(bf16[3,192,256]{2,1,0:T(8,128)(2,1)S(1)} %get-tuple-element.32.refs_3_), channel_id=1, source_target_pairs={{0,4},{4,0},{8,12},{12,8},{2,6},{6,2},{10,14},{14,10},{16,20},{20,... | collective-permute-start | bytes 884744 | tf_op jit(solution)/shard_map/ppermute | solution.py:328
  19.0 13.7 %collective-permute-start.19 = (bf16[3,192,256]{2,1,0:T(8,128)(2,1)S(1)}, bf16[3,192,256]{2,1,0:T(8,128)(2,1)S(1)}, u32[]{:S(2)}, u32[]{:S(2)}) collective-permute-start(bf16[3,192,256]{2,1,0:T(8,128)(2,1)S(1)} %collective-permute-done.8.refs_5_), channel_id=1, source_target_pairs={{0,18},{4,22},{8,26},{12,30},{2,16},{6,20},{10,24},{14,28},{16,2},... | collective-permute-start | bytes 884744 | tf_op jit(solution)/shard_map/ppermute | solution.py:328
  23.3 10.9 %collective-permute-start.13 = (bf16[3,192,256]{2,1,0:T(8,128)(2,1)S(1)}, bf16[3,192,256]{2,1,0:T(8,128)(2,1)S(1)}, u32[]{:S(2)}, u32[]{:S(2)}) collective-permute-start(bf16[3,192,256]{2,1,0:T(8,128)(2,1)S(1)} %collective-permute-done.8.refs_5_), channel_id=1, source_target_pairs={{4,8},{8,4},{6,10},{10,6},{20,24},{24,20},{22,26},{26,22},{5,9},{9... | collective-permute-start | bytes 884744 | tf_op jit(solution)/shard_map/ppermute | solution.py:328
  25.4 11.9 %collective-permute-start.14 = (bf16[3,192,256]{2,1,0:T(8,128)(2,1)}, bf16[3,192,256]{2,1,0:T(8,128)(2,1)}, u32[]{:S(2)}, u32[]{:S(2)}) collective-permute-start(bf16[3,192,256]{2,1,0:T(8,128)(2,1)} %collective-permute-done.9), channel_id=1, source_target_pairs={{4,0},{8,12},{6,2},{10,14},{20,16},{24,28},{22,18},{26,30},{5,1},{... | collective-permute-start | bytes 884744 | tf_op jit(solution)/shard_map/ppermute | solution.py:328
  27.4 13.1 %collective-permute-start.17 = (bf16[3,192,256]{2,1,0:T(8,128)(2,1)S(1)}, bf16[3,192,256]{2,1,0:T(8,128)(2,1)S(1)}, u32[]{:S(2)}, u32[]{:S(2)}) collective-permute-start(bf16[3,192,256]{2,1,0:T(8,128)(2,1)S(1)} %collective-permute-done.4.refs_5_), channel_id=1, source_target_pairs={{4,8},{8,4},{6,10},{10,6},{20,24},{24,20},{22,26},{26,22},{5,9},{9... | collective-permute-start | bytes 884744 | tf_op jit(solution)/shard_map/ppermute | solution.py:328
  30.7 11.2 %collective-permute-start.18 = (bf16[3,192,256]{2,1,0:T(8,128)(2,1)}, bf16[3,192,256]{2,1,0:T(8,128)(2,1)}, u32[]{:S(2)}, u32[]{:S(2)}) collective-permute-start(bf16[3,192,256]{2,1,0:T(8,128)(2,1)} %collective-permute-done.5), channel_id=1, source_target_pairs={{4,0},{8,12},{6,2},{10,14},{20,16},{24,28},{22,18},{26,30},{5,1},{... | collective-permute-start | bytes 884744 | tf_op jit(solution)/shard_map/ppermute | solution.py:328
  32.7 11.9 %collective-permute-start.23 = (bf16[3,192,256]{2,1,0:T(8,128)(2,1)S(1)}, bf16[3,192,256]{2,1,0:T(8,128)(2,1)S(1)}, u32[]{:S(2)}, u32[]{:S(2)}) collective-permute-start(bf16[3,192,256]{2,1,0:T(8,128)(2,1)S(1)} %collective-permute-done.4.refs_5_), channel_id=1, source_target_pairs={{0,18},{4,22},{8,26},{12,30},{2,16},{6,20},{10,24},{14,28},{16,2},... | collective-permute-start | bytes 884744 | tf_op jit(solution)/shard_map/ppermute | solution.py:328
  34.2 12.0 %collective-permute-start.12 = (bf16[3,192,256]{2,1,0:T(8,128)(2,1)S(1)}, bf16[3,192,256]{2,1,0:T(8,128)(2,1)S(1)}, u32[]{:S(2)}, u32[]{:S(2)}) collective-permute-start(bf16[3,192,256]{2,1,0:T(8,128)(2,1)S(1)} %collective-permute-done.6.refs_5_), channel_id=1, source_target_pairs={{4,8},{8,4},{6,10},{10,6},{20,24},{24,20},{22,26},{26,22},{5,9},{9... | collective-permute-start | bytes 884744 | tf_op jit(solution)/shard_map/ppermute | solution.py:328
  37.3 11.2 %collective-permute-start.10 = (bf16[3,192,256]{2,1,0:T(8,128)(2,1)S(1)}, bf16[3,192,256]{2,1,0:T(8,128)(2,1)S(1)}, u32[]{:S(2)}, u32[]{:S(2)}) collective-permute-start(bf16[3,192,256]{2,1,0:T(8,128)(2,1)S(1)} %collective-permute-done.6.refs_5_), channel_id=1, source_target_pairs={{0,18},{4,22},{8,26},{12,30},{2,16},{6,20},{10,24},{14,28},{16,2},... | collective-permute-start | bytes 884744 | tf_op jit(solution)/shard_map/ppermute | solution.py:328
  40.5 10.9 %collective-permute-start.11 = (bf16[3,192,256]{2,1,0:T(8,128)(2,1)}, bf16[3,192,256]{2,1,0:T(8,128)(2,1)S(1)}, u32[]{:S(2)}, u32[]{:S(2)}) collective-permute-start(bf16[3,192,256]{2,1,0:T(8,128)(2,1)} %copy-done.5), channel_id=1, source_target_pairs={{4,0},{8,12},{6,2},{10,14},{20,16},{24,28},{22,18},{26,30},{5,1},{... | collective-permute-start | bytes 884744 | tf_op jit(solution)/shard_map/ppermute | solution.py:328
  41.8 13.4 %collective-permute-start.20 = (bf16[3,192,256]{2,1,0:T(8,128)(2,1)}, bf16[3,192,256]{2,1,0:T(8,128)(2,1)S(1)}, u32[]{:S(2)}, u32[]{:S(2)}) collective-permute-start(bf16[3,192,256]{2,1,0:T(8,128)(2,1)} %copy-done.6), channel_id=1, source_target_pairs={{4,0},{8,12},{6,2},{10,14},{20,16},{24,28},{22,18},{26,30},{5,1},{... | collective-permute-start | bytes 884744 | tf_op jit(solution)/shard_map/ppermute | solution.py:328
  44.5 13.1 %collective-permute-start.22 = (bf16[3,192,256]{2,1,0:T(8,128)(2,1)S(1)}, bf16[3,192,256]{2,1,0:T(8,128)(2,1)S(1)}, u32[]{:S(2)}, u32[]{:S(2)}) collective-permute-start(bf16[3,192,256]{2,1,0:T(8,128)(2,1)S(1)} %broadcast_select_fusion.3.refs_7_), channel_id=1, source_target_pairs={{0,18},{4,22},{8,26},{12,30},{2,16},{6,20},{10,24},{14,28},{16,2},... | collective-permute-start | bytes 884744 | tf_op jit(solution)/shard_map/ppermute | solution.py:328
  46.2 15.2 %collective-permute-start.24 = (bf16[3,192,256]{2,1,0:T(8,128)(2,1)S(1)}, bf16[3,192,256]{2,1,0:T(8,128)(2,1)S(1)}, u32[]{:S(2)}, u32[]{:S(2)}) collective-permute-start(bf16[3,192,256]{2,1,0:T(8,128)(2,1)S(1)} %collective-permute-done.17), channel_id=1, source_target_pairs={{4,0},{8,12},{6,2},{10,14},{20,16},{24,28},{22,18},{26,30},{5,1},{... | collective-permute-start | bytes 884744 | tf_op jit(solution)/shard_map/ppermute | solution.py:328
  48.5 17.1 %collective-permute-start.1 = (bf16[2,64,1536]{2,1,0:T(8,128)(2,1)S(1)}, bf16[2,64,1536]{2,1,0:T(8,128)(2,1)S(1)}, u32[]{:S(2)}, u32[]{:S(2)}) collective-permute-start(bf16[2,64,1536]{2,1,0:T(8,128)(2,1)S(1)} %copy-done), channel_id=1, source_target_pairs={{2,4},{6,8},{10,12},{4,2},{8,6},{12,10},{3,5},{7,9},{11,13},{5,3},... | collective-permute-start | bytes 1179656 | tf_op jit(solution)/shard_map/ppermute | solution.py:347
  51.4 24.1 %collective-permute-start.3 = (bf16[3,3,192,256]{3,2,1,0:T(8,128)(2,1)}, bf16[3,3,192,256]{3,2,1,0:T(8,128)(2,1)S(1)}, u32[]{:S(2)}, u32[]{:S(2)}) collective-permute-start(bf16[3,3,192,256]{3,2,1,0:T(8,128)(2,1)} %pad_maximum_fusion), channel_id=1, source_target_pairs={{0,2},{2,0},{4,6},{6,4},{8,10},{10,8},{12,14},{14,12},{1,3},{3,1},... | collective-permute-start | bytes 2654216 | tf_op jit(solution)/shard_map/ppermute | solution.py:348
  57.6 11.7 %collective-permute-start.15 = (bf16[3,192,256]{2,1,0:T(8,128)(2,1)S(1)}, bf16[3,192,256]{2,1,0:T(8,128)(2,1)S(1)}, u32[]{:S(2)}, u32[]{:S(2)}) collective-permute-start(bf16[3,192,256]{2,1,0:T(8,128)(2,1)S(1)} %broadcast_select_fusion.5.refs_7_), channel_id=1, source_target_pairs={{0,18},{4,22},{8,26},{12,30},{2,16},{6,20},{10,24},{14,28},{16,2},... | collective-permute-start | bytes 884744 | tf_op jit(solution)/shard_map/ppermute | solution.py:328
  61.4 10.6 %collective-permute-start.16 = (bf16[3,192,256]{2,1,0:T(8,128)(2,1)S(1)}, bf16[3,192,256]{2,1,0:T(8,128)(2,1)S(1)}, u32[]{:S(2)}, u32[]{:S(2)}) collective-permute-start(bf16[3,192,256]{2,1,0:T(8,128)(2,1)S(1)} %collective-permute-done.12), channel_id=1, source_target_pairs={{4,0},{8,12},{6,2},{10,14},{20,16},{24,28},{22,18},{26,30},{5,1},{... | collective-permute-start | bytes 884744 | tf_op jit(solution)/shard_map/ppermute | solution.py:328
  69.3 19.3 %collective-permute-start.25 = (bf16[3,192,256]{2,1,0:T(8,128)(2,1)S(1)}, bf16[3,192,256]{2,1,0:T(8,128)(2,1)S(1)}, u32[]{:S(2)}, u32[]{:S(2)}) collective-permute-start(bf16[3,192,256]{2,1,0:T(8,128)(2,1)S(1)} %broadcast_select_fusion.2.refs_9_), channel_id=1, source_target_pairs={{0,18},{4,22},{8,26},{12,30},{2,16},{6,20},{10,24},{14,28},{16,2},... | collective-permute-start | bytes 884744 | tf_op jit(solution)/shard_map/ppermute | solution.py:328
  72.0 13.3 %collective-permute-start.27 = (bf16[3,192,256]{2,1,0:T(8,128)(2,1)S(1)}, bf16[3,192,256]{2,1,0:T(8,128)(2,1)S(1)}, u32[]{:S(2)}, u32[]{:S(2)}) collective-permute-start(bf16[3,192,256]{2,1,0:T(8,128)(2,1)S(1)} %broadcast_select_fusion.refs_9_), channel_id=1, source_target_pairs={{0,18},{4,22},{8,26},{12,30},{2,16},{6,20},{10,24},{14,28},{16,2},... | collective-permute-start | bytes 884744 | tf_op jit(solution)/shard_map/ppermute | solution.py:328
  72.3 19.7 %collective-permute-start.21 = (bf16[3,192,256]{2,1,0:T(8,128)(2,1)S(1)}, bf16[3,192,256]{2,1,0:T(8,128)(2,1)S(1)}, u32[]{:S(2)}, u32[]{:S(2)}) collective-permute-start(bf16[3,192,256]{2,1,0:T(8,128)(2,1)S(1)} %broadcast_select_fusion.4.refs_9_), channel_id=1, source_target_pairs={{0,18},{4,22},{8,26},{12,30},{2,16},{6,20},{10,24},{14,28},{16,2},... | collective-permute-start | bytes 884744 | tf_op jit(solution)/shard_map/ppermute | solution.py:328
  99.1 12.5 %collective-permute-start.29 = (bf16[2,64,1536]{2,1,0:T(8,128)(2,1)S(1)}, bf16[2,64,1536]{2,1,0:T(8,128)(2,1)S(1)}, u32[]{:S(2)}, u32[]{:S(2)}) collective-permute-start(bf16[2,64,1536]{2,1,0:T(8,128)(2,1)S(1)} %project.2.refs_6_), channel_id=1, source_target_pairs={{0,1},{2,3},{4,5},{6,7},{8,9},{10,11},{12,13},{14,15},{16,17},{18,... | collective-permute-start | bytes 1179656 | tf_op jit(solution)/shard_map/ppermute | solution.py:501
  (20 other events, 243.5 us)

commit v4 on v3

--- a/solution.py
+++ b/solution.py
@@ -161,7 +161,7 @@
         att_pair[m, :, offset : offset + part] = joined[view_tok:]
 
 
-def attend_part_kernel(index, *refs):
+def attend_part_kernel(offset, *refs):
     views, normed, gains = refs[:3]
     pieces = refs[3:11]
     att_own, att_pair, weights, sems = refs[-4:]
@@ -172,9 +172,12 @@
     for slot in range(8):
         start = pl.multiple_of(order[slot] * rows, rows)
         for kind in range(3):
+            source = pieces[slot].at[kind]
+            if slot == 1:
+                source = source.at[:, pl.ds(offset, part)]
             moves.append(
                 pltpu.make_async_copy(
-                    pieces[slot].at[kind],
+                    source,
                     weights.at[pl.ds(start, rows), pl.ds(kind * part, part)],
                     sems.at[3 * slot + kind],
                 )
@@ -191,7 +194,7 @@
         near_masks,
         far_masks,
         view_tok,
-        (att_own, att_pair, index * part),
+        (att_own, att_pair, offset),
     )
 
 
@@ -212,7 +215,7 @@
         incoming[slot].wait()
         for m in range(micro_count):
             normalise(streams.at[slot], m, slot, modulation, sets, normed)
-    part = weights[0].shape[1] // 3
+    offset = 0
     for index in range(3):
         attend_heads(
             normed,
@@ -221,8 +224,9 @@
             near_masks,
             far_masks,
             view_tok,
-            (att_own, att_pair, index * part),
-        )
+            (att_own, att_pair, offset),
+        )
+        offset += weights[index].shape[1] // 3
 
 
 def project_kernel(last, *refs):
@@ -333,26 +337,44 @@
     ]
 
     by_kind = jnp.transpose(qkv_weight[0], (1, 0, 2))
-    third_part = part // 3
-
-    def columns(which, index):
+    unit_heads = part // head // 6
+    cuts = [0, 2, 4, 6]
+    cuts = [cut * unit_heads * head for cut in cuts]
+
+    def columns(index):
+        begin, size = cuts[index], cuts[index + 1] - cuts[index]
         return lax.dynamic_slice(
-            by_kind, (0, 0, which * part + index * third_part), (3, rows, third_part)
-        )
-
-    home = [columns(mine, index) for index in range(3)]
-    lent = [columns(1 - mine, index) for index in range(3)]
+            by_kind, (0, 0, mine * part + begin), (3, rows, size)
+        )
+
+    home = [columns(index) for index in range(3)]
+    lent = lax.dynamic_slice(by_kind, (0, 0, (1 - mine) * part), (3, rows, part))
+
+    def lend(pairs):
+        pairs = [
+            (a * section_count + section_count - 1, b * section_count) for a, b in pairs
+        ]
+        return lax.ppermute(stream, ("seq", "section"), pairs)
 
     pair = lax.ppermute(stream, "seq", swap_cores)
-    halo = lax.ppermute(stream, "seq", swap_edges)
-    home_pair = lax.ppermute(jnp.stack(lent), "seq", swap_cores)
-    pair_halo = lax.ppermute(halo, "seq", swap_cores)
-    first_exchange = (pair, halo, pair_halo)
+    halo = lend(swap_edges)
+    pair_halo = lend([(a, b ^ 1) for a, b in swap_edges])
+    home_pair = lax.ppermute(lent, "seq", swap_cores)
+
+    crossings = []
+
+    def cross(value):
+        if len(crossings) >= 2:
+            value = tied(value, crossings[-2])
+        crossings.append(send(value, opposite))
+        return crossings[-1]
 
     from_outer, from_inner = [], []
     across_first, inner_next, outer_next = [], [], []
     for kind in range(3):
         ready = home[kind]
+        if kind == 1:
+            ready = tied(ready, pair)
         if kind == 2:
             ready = tied(ready, from_outer[0], from_inner[0])
         from_outer.append(send(ready, outer))
@@ -361,7 +383,7 @@
     for kind in range(3):
         a = tied(from_outer[kind], from_inner[kind], *before)
         b = tied(from_inner[kind], from_outer[kind], *before)
-        across_first.append(send(a, opposite))
+        across_first.append(cross(a))
         inner_next.append(send(a, inner))
         outer_next.append(send(b, outward_steps))
         before = (from_outer[kind], from_inner[kind])
@@ -372,13 +394,13 @@
         b = tied(outer_next[kind], inner_next[kind], *before)
         outer_last.append(send(a, outward_steps))
         second.append(jnp.where(middle, from_inner[kind], b))
-        across_second.append(send(second[kind], opposite))
+        across_second.append(cross(second[kind]))
         before = (inner_next[kind], outer_next[kind])
     third, across_third = [], []
     for kind in range(3):
         a = tied(outer_last[kind], across_second[kind], *before)
         third.append(jnp.where(middle, inner_next[kind], a))
-        across_third.append(send(third[kind], opposite))
+        across_third.append(cross(third[kind]))
         before = (outer_last[kind],)
 
     section_place = lax.axis_index("section")
@@ -405,11 +427,13 @@
 
     def attend_part(index, normed, pieces, earlier):
         return pl.pallas_call(
-            functools.partial(attend_part_kernel, index),
+            functools.partial(attend_part_kernel, cuts[index]),
             out_shape=(
                 half_shape,
                 half_shape,
-                jax.ShapeDtypeStruct((width, part), jnp.bfloat16),
+                jax.ShapeDtypeStruct(
+                    (width, 3 * (cuts[index + 1] - cuts[index])), jnp.bfloat16
+                ),
             ),
             in_specs=[smem, vmem, vmem] + [anywhere] * 8 + [vmem] * len(earlier),
             out_specs=(vmem, vmem, vmem),
@@ -476,7 +500,7 @@
             for index in range(3):
                 pieces = [
                     home[index],
-                    home_pair[index],
+                    home_pair,
                     from_outer[index],
                     across_first[index],
                     second[index],

time: 138 us -> 133 us (0.964)
  waiting for transfers between devices: 53 us -> 41 us
  starting transfers between devices: 51.5 us -> 58.2 us
  local copies, waits for them, and re-layouts: 1.68 us -> 3.4 us
    ppermute x24, waiting for transfers between devices: 33.5 us -> 19 us  [send(): return lax.ppermute(value, line_axes, pairs)]
    ppermute x24, starting transfers between devices: 40.5 us -> 48.5 us  [send(): return lax.ppermute(value, line_axes, pairs)]
    dynamic_slice x1 -> x2, local copies, waits for them, and re-layouts: 1.56 us -> 3.35 us  [the longest x1 2.14 us: paired_body(): lax.dynamic_slice(by_kind, (0, 0, (1 - mine) * part), (3, rows, part))]
    ppermute x1, starting transfers between devices: 1.85 us -> 0.07 us  [paired_body(): pair = lax.ppermute(own, 'seq', swap_cores)]
    ppermute x1, waiting for transfers between devices: 4.43 us -> 6.2 us  [paired_body(): halo = lax.ppermute(own, 'seq', swap_edges)]
    ppermute x2 -> x3, starting transfers between devices: 3 us -> 3.36 us  [the longest x2 2.97 us: lend(): return lax.ppermute(stream, ('seq', 'section'), pairs)]
  transfers between devices with their start and end apart: 34 -> 34, of which waited for: 16 -> 13; matrix products, arithmetic and copies ran while one was open for 3% -> 6% of each run, Pallas kernels for 6% -> 6%
where the time goes in v4:
time: 133 us; the launch traced here: 132 us
  starting transfers between devices  58.2 us (44%)
  waiting for transfers between devices  41 us (31%)
  Pallas kernels  25 us (19%)
  other arithmetic  4.05 us (3%)
  local copies, waits for them, and re-layouts  3.4 us (3%)
    ppermute x24, starting transfers between devices, send(): return lax.ppermute(value, line_axes, pairs)  48.5 us
    ppermute x24, waiting for transfers between devices, send(): return lax.ppermute(value, line_axes, pairs)  19 us
    ppermute x1, waiting for transfers between devices, paired_body(): lax.ppermute(result, 'section', [(i, i + 1) for i in range(section_count...  12.1 us
    pallas_call x3, Pallas kernels, attend_part(): pl.pallas_call(functools.partial(attend_part_kernel, cuts[index]), out_sh...  9.99 us
    pallas_call x1, Pallas kernels, paired_body(): attend(set_views, own, pair, halo, pair_halo, modulation[0], norm_gain[0]...  8.14 us
    ppermute x1, waiting for transfers between devices, paired_body(): halo = lax.ppermute(own, 'seq', swap_edges)  6.2 us
    pallas_call x2, Pallas kernels, project(): pl.pallas_call(functools.partial(project_kernel, last), out_shape=jax.Sha...  5.24 us
    ppermute x1, starting transfers between devices, paired_body(): halo = lax.ppermute(own, 'seq', swap_edges)  3.09 us
  transfers between devices with their start and end apart: 34, of which 13 were waited for; matrix products, arithmetic and copies ran while one was open for 6% of the time, Pallas kernels for 6%

profile of v4, /device:TPU:11, one launch (start us, length us, event | category | flops | bytes accessed | tf_op | source)
XLA Modules:
  0.0 132.2 jit_solution(3900263218539536898)
XLA Ops:
  1.9 3.2 %collective-permute-start.5 = (bf16[3,192,256]{2,1,0:T(8,128)(2,1)S(1)}, bf16[3,192,256]{2,1,0:T(8,128)(2,1)}, u32[]{:S(2)}, u32[]{:S(2)}) collective-permute-start(bf16[3,192,256]{2,1,0:T(8,128)(2,1)S(1)} %get-tuple-element.77.refs_3_), channel_id=1, source_target_pairs={{4,8},{8,4},{6,10},{10,6},{20,24},{24,20},{22,26},{26,22},{5,9},{9... | collective-permute-start | bytes 884744 | tf_op jit(solution)/shard_map/ppermute | solution.py:332
  5.2 2.6 %collective-permute-start.9 = (bf16[3,192,256]{2,1,0:T(8,128)(2,1)S(1)}, bf16[3,192,256]{2,1,0:T(8,128)(2,1)S(1)}, u32[]{:S(2)}, u32[]{:S(2)}) collective-permute-start(bf16[3,192,256]{2,1,0:T(8,128)(2,1)S(1)} %get-tuple-element.41.refs_3_), channel_id=1, source_target_pairs={{4,8},{8,4},{6,10},{10,6},{20,24},{24,20},{22,26},{26,22},{5,9},{9... | collective-permute-start | bytes 884744 | tf_op jit(solution)/shard_map/ppermute | solution.py:332
  7.8 4.7 %collective-permute-done.5 = bf16[3,192,256]{2,1,0:T(8,128)(2,1)} collective-permute-done((bf16[3,192,256]{2,1,0:T(8,128)(2,1)S(1)}, bf16[3,192,256]{2,1,0:T(8,128)(2,1)}, u32[]{:S(2)}, u32[]{:S(2)}) %collective-permute-start.5) | collective-permute-done | bytes 294944 | tf_op jit(solution)/shard_map/ppermute | solution.py:332
  13.5 2.2 %collective-permute-start.7 = (bf16[3,192,256]{2,1,0:T(8,128)(2,1)S(1)}, bf16[3,192,256]{2,1,0:T(8,128)(2,1)}, u32[]{:S(2)}, u32[]{:S(2)}) collective-permute-start(bf16[3,192,256]{2,1,0:T(8,128)(2,1)S(1)} %get-tuple-element.40.refs_3_), channel_id=1, source_target_pairs={{4,8},{8,4},{6,10},{10,6},{20,24},{24,20},{22,26},{26,22},{5,9},{9... | collective-permute-start | bytes 884744 | tf_op jit(solution)/shard_map/ppermute | solution.py:332
  15.8 3.0 %collective-permute-start.17 = (bf16[3,192,256]{2,1,0:T(8,128)(2,1)S(1)}, bf16[3,192,256]{2,1,0:T(8,128)(2,1)S(1)}, u32[]{:S(2)}, u32[]{:S(2)}) collective-permute-start(bf16[3,192,256]{2,1,0:T(8,128)(2,1)S(1)} %collective-permute-done.4.refs_5_), channel_id=1, source_target_pairs={{4,8},{8,4},{6,10},{10,6},{20,24},{24,20},{22,26},{26,22},{5,9},{9... | collective-permute-start | bytes 884744 | tf_op jit(solution)/shard_map/ppermute | solution.py:332
  18.9 3.6 %collective-permute-start.10 = (bf16[3,192,256]{2,1,0:T(8,128)(2,1)S(1)}, bf16[3,192,256]{2,1,0:T(8,128)(2,1)S(1)}, u32[]{:S(2)}, u32[]{:S(2)}) collective-permute-start(bf16[3,192,256]{2,1,0:T(8,128)(2,1)S(1)} %collective-permute-done.4.refs_5_), channel_id=1, source_target_pairs={{0,18},{4,22},{8,26},{12,30},{2,16},{6,20},{10,24},{14,28},{16,2},... | collective-permute-start | bytes 884744 | tf_op jit(solution)/shard_map/ppermute | solution.py:332
  24.4 3.9 %collective-permute-start.18 = (bf16[3,192,256]{2,1,0:T(8,128)(2,1)S(1)}, bf16[3,192,256]{2,1,0:T(8,128)(2,1)S(1)}, u32[]{:S(2)}, u32[]{:S(2)}) collective-permute-start(bf16[3,192,256]{2,1,0:T(8,128)(2,1)S(1)} %collective-permute-done.8.refs_5_), channel_id=1, source_target_pairs={{0,18},{4,22},{8,26},{12,30},{2,16},{6,20},{10,24},{14,28},{16,2},... | collective-permute-start | bytes 884744 | tf_op jit(solution)/shard_map/ppermute | solution.py:332
  28.4 2.4 %collective-permute-start.14 = (bf16[3,192,256]{2,1,0:T(8,128)(2,1)S(1)}, bf16[3,192,256]{2,1,0:T(8,128)(2,1)}, u32[]{:S(2)}, u32[]{:S(2)}) collective-permute-start(bf16[3,192,256]{2,1,0:T(8,128)(2,1)S(1)} %collective-permute-done.8.refs_5_), channel_id=1, source_target_pairs={{4,8},{8,4},{6,10},{10,6},{20,24},{24,20},{22,26},{26,22},{5,9},{9... | collective-permute-start | bytes 884744 | tf_op jit(solution)/shard_map/ppermute | solution.py:332
  32.9 2.1 %dynamic-slice_bitcast_fusion = bf16[3,192,768]{2,1,0:T(8,128)(2,1)} fusion(bf16[1,192,3,1536]{3,1,2,0:T(8,128)(2,1)} %param.11, s32[]{:T(128)S(6)} %select_n.53), kind=kLoop, calls=%fused_computation | loop fusion | bytes 1769476 | tf_op jit(solution)/shard_map/dynamic_slice | solution.py:351
  35.0 3.7 %collective-permute-start.13 = (bf16[3,192,256]{2,1,0:T(8,128)(2,1)S(1)}, bf16[3,192,256]{2,1,0:T(8,128)(2,1)S(1)}, u32[]{:S(2)}, u32[]{:S(2)}) collective-permute-start(bf16[3,192,256]{2,1,0:T(8,128)(2,1)S(1)} %collective-permute-done.6.refs_5_), channel_id=1, source_target_pairs={{4,8},{8,4},{6,10},{10,6},{20,24},{24,20},{22,26},{26,22},{5,9},{9... | collective-permute-start | bytes 884744 | tf_op jit(solution)/shard_map/ppermute | solution.py:332
  40.1 2.6 %collective-permute-start.11 = (bf16[3,192,256]{2,1,0:T(8,128)(2,1)S(1)}, bf16[3,192,256]{2,1,0:T(8,128)(2,1)S(1)}, u32[]{:S(2)}, u32[]{:S(2)}) collective-permute-start(bf16[3,192,256]{2,1,0:T(8,128)(2,1)S(1)} %collective-permute-done.6.refs_5_), channel_id=1, source_target_pairs={{0,18},{4,22},{8,26},{12,30},{2,16},{6,20},{10,24},{14,28},{16,2},... | collective-permute-start | bytes 884744 | tf_op jit(solution)/shard_map/ppermute | solution.py:332
  46.7 3.8 %collective-permute-done.11.refs_6_ = bf16[3,192,256]{2,1,0:T(8,128)(2,1)S(1)} collective-permute-done((bf16[3,192,256]{2,1,0:T(8,128)(2,1)S(1)}, bf16[3,192,256]{2,1,0:T(8,128)(2,1)S(1)}, u32[]{:S(2)}, u32[]{:S(2)}) %collective-permute-start.11) | collective-permute-done | bytes 294944 | tf_op jit(solution)/shard_map/ppermute | solution.py:332
  51.8 2.9 %collective-permute-start.24 = (bf16[3,192,256]{2,1,0:T(8,128)(2,1)S(1)}, bf16[3,192,256]{2,1,0:T(8,128)(2,1)S(1)}, u32[]{:S(2)}, u32[]{:S(2)}) collective-permute-start(bf16[3,192,256]{2,1,0:T(8,128)(2,1)S(1)} %broadcast_select_fusion.1.refs_7_), channel_id=1, source_target_pairs={{0,18},{4,22},{8,26},{12,30},{2,16},{6,20},{10,24},{14,28},{16,2},... | collective-permute-start | bytes 884744 | tf_op jit(solution)/shard_map/ppermute | solution.py:332
  63.1 4.2 %collective-permute-start.25 = (bf16[3,192,256]{2,1,0:T(8,128)(2,1)S(1)}, bf16[3,192,256]{2,1,0:T(8,128)(2,1)S(1)}, u32[]{:S(2)}, u32[]{:S(2)}) collective-permute-start(bf16[3,192,256]{2,1,0:T(8,128)(2,1)S(1)} %broadcast_select_fusion.2.refs_9_), channel_id=1, source_target_pairs={{0,18},{4,22},{8,26},{12,30},{2,16},{6,20},{10,24},{14,28},{16,2},... | collective-permute-start | bytes 884744 | tf_op jit(solution)/shard_map/ppermute | solution.py:332
  71.0 4.8 %collective-permute-done.25.refs_10_ = bf16[3,192,256]{2,1,0:T(8,128)(2,1)S(1)} collective-permute-done((bf16[3,192,256]{2,1,0:T(8,128)(2,1)S(1)}, bf16[3,192,256]{2,1,0:T(8,128)(2,1)S(1)}, u32[]{:S(2)}, u32[]{:S(2)}) %collective-permute-start.25) | collective-permute-done | bytes 294944 | tf_op jit(solution)/shard_map/ppermute | solution.py:332
  79.1 3.3 %attend_part.3 = (bf16[2,64,768]{2,1,0:T(8,128)(2,1)S(1)}, bf16[2,64,768]{2,1,0:T(8,128)(2,1)S(1)}, bf16[1536,768]{1,0:T(8,128)(2,1)S(1)}) custom-call(s32[2,6]{1,0:T(2,128)S(1)} %copy-done.3, bf16[512,1536]{1,0:T(8,128)(2,1)S(1)} %norm.1.refs_1_, f32[2,128]{1,0:T(2,128)S(1)} %bitcast.31, bf16[3,192,256]{2,1,0:T(8,128)(2,1)S(1)} %get-tuple-element.77.refs_3_, ...), custom_call_target="tpu_custom_call" | custom-call | tf_op jit(solution)/shard_map/attend_part/pallas_call | solution.py:429
  82.5 3.3 %attend_part.4 = (bf16[2,64,768]{2,1,0:T(8,128)(2,1)S(1)}, bf16[2,64,768]{2,1,0:T(8,128)(2,1)S(1)}, bf16[1536,768]{1,0:T(8,128)(2,1)S(1)}) custom-call(s32[2,6]{1,0:T(2,128)S(1)} %copy-done.3, bf16[512,1536]{1,0:T(8,128)(2,1)S(1)} %norm.1.refs_1_, f32[2,128]{1,0:T(2,128)S(1)} %bitcast.32, ...), custom_call_target="tpu_custom_call", output_to_operand_aliasing={{0}: (11, {}), {1}: (12, {})} | custom-call | tf_op jit(solution)/shard_map/attend_part/pallas_call | solution.py:429
  87.8 3.3 %attend_part.5 = (bf16[2,64,768]{2,1,0:T(8,128)(2,1)S(1)}, bf16[2,64,768]{2,1,0:T(8,128)(2,1)S(1)}, bf16[1536,768]{1,0:T(8,128)(2,1)S(1)}) custom-call(s32[2,6]{1,0:T(2,128)S(1)} %copy-done.3, bf16[512,1536]{1,0:T(8,128)(2,1)S(1)} %norm.1.refs_1_, f32[2,128]{1,0:T(2,128)S(1)} %bitcast.33, ...), custom_call_target="tpu_custom_call", output_to_operand_aliasing={{0}: (11, {}), {1}: (12, {})} | custom-call | tf_op jit(solution)/shard_map/attend_part/pallas_call | solution.py:429
  92.6 2.2 %project.2.refs_6_ = bf16[2,64,1536]{2,1,0:T(8,128)(2,1)S(1)} custom-call(s32[2,6]{1,0:T(2,128)S(1)} %copy-done.3, bf16[2,64,768]{2,1,0:T(8,128)(2,1)S(1)} %get-tuple-element.68.refs_1_, bf16[2,64,768]{2,1,0:T(8,128)(2,1)S(1)} %collective-permute-done.28.refs_2_, bf16[2,64,1536]{2,1,0:T(8,128)(2,1)S(1)} %copy-done, bf16[6,2,1536]{2,1,0:T(2,128)(2,1)S(1)} %bitcast.29, ...), custom_call_target="tpu_custom_call" | custom-call | tf_op jit(solution)/shard_map/project/pallas_call | solution.py:463
  96.1 12.1 %collective-permute-done.29.refs_1_.refs_3_ = bf16[2,64,1536]{2,1,0:T(8,128)(2,1)S(1)} collective-permute-done((bf16[2,64,1536]{2,1,0:T(8,128)(2,1)S(1)}, bf16[2,64,1536]{2,1,0:T(8,128)(2,1)S(1)}, u32[]{:S(2)}, u32[]{:S(2)}) %collective-permute-start.29) | collective-permute-done | bytes 393248 | tf_op jit(solution)/shard_map/ppermute | solution.py:525
  108.2 3.1 %collective-permute-start.31 = (bf16[2,64,1536]{2,1,0:T(8,128)(2,1)S(1)}, bf16[2,64,1536]{2,1,0:T(8,128)(2,1)S(1)}, u32[]{:S(2)}, u32[]{:S(2)}) collective-permute-start(bf16[2,64,1536]{2,1,0:T(8,128)(2,1)S(1)} %collective-permute-done.29.refs_1_.refs_3_), channel_id=1, source_target_pairs={{2,4},{6,8},{10,12},{4,2},{8,6},{12,10},{3,5},{7,9},{11,13},{5,3},... | collective-permute-start | bytes 1179656 | tf_op jit(solution)/shard_map/ppermute | solution.py:484
  111.3 6.2 %collective-permute-done.31.refs_3_ = bf16[2,64,1536]{2,1,0:T(8,128)(2,1)S(1)} collective-permute-done((bf16[2,64,1536]{2,1,0:T(8,128)(2,1)S(1)}, bf16[2,64,1536]{2,1,0:T(8,128)(2,1)S(1)}, u32[]{:S(2)}, u32[]{:S(2)}) %collective-permute-start.31) | collective-permute-done | bytes 393248 | tf_op jit(solution)/shard_map/ppermute | solution.py:484
  119.3 8.1 %attend.1 = (bf16[2,64,768]{2,1,0:T(8,128)(2,1)S(1)}, bf16[2,64,768]{2,1,0:T(8,128)(2,1)S(1)}) custom-call(s32[2,6]{1,0:T(2,128)S(1)} %copy-done.3, bf16[2,64,1536]{2,1,0:T(8,128)(2,1)S(1)} %collective-permute-done.29.refs_1_.refs_3_, bf16[2,64,1536]{2,1,0:T(8,128)(2,1)S(1)} %collective-permute-done.30.refs_2_, ...), custom_call_target="tpu_custom_call" | custom-call | tf_op jit(solution)/shard_map/attend/pallas_call | solution.py:487
  129.0 3.1 %project.3 = bf16[2,64,1536]{2,1,0:T(8,128)(2,1)} custom-call(s32[2,6]{1,0:T(2,128)S(1)} %copy-done.3, bf16[2,64,768]{2,1,0:T(8,128)(2,1)S(1)} %get-tuple-element.73.refs_1_, bf16[2,64,768]{2,1,0:T(8,128)(2,1)S(1)} %collective-permute-done.33.refs_2_, bf16[2,64,1536]{2,1,0:T(8,128)(2,1)S(1)} %collective-permute-done.29.refs_1_.refs_3_, ...), custom_call_target="tpu_custom_call" | custom-call | tf_op jit(solution)/shard_map/project/pallas_call | solution.py:463
  (76 shorter events, 37.0 us)
Async XLA Ops:
  1.9 10.6 %collective-permute-start.5 = (bf16[3,192,256]{2,1,0:T(8,128)(2,1)S(1)}, bf16[3,192,256]{2,1,0:T(8,128)(2,1)}, u32[]{:S(2)}, u32[]{:S(2)}) collective-permute-start(bf16[3,192,256]{2,1,0:T(8,128)(2,1)S(1)} %get-tuple-element.77.refs_3_), channel_id=1, source_target_pairs={{4,8},{8,4},{6,10},{10,6},{20,24},{24,20},{22,26},{26,22},{5,9},{9... | collective-permute-start | bytes 884744 | tf_op jit(solution)/shard_map/ppermute | solution.py:332
  5.2 13.7 %collective-permute-start.9 = (bf16[3,192,256]{2,1,0:T(8,128)(2,1)S(1)}, bf16[3,192,256]{2,1,0:T(8,128)(2,1)S(1)}, u32[]{:S(2)}, u32[]{:S(2)}) collective-permute-start(bf16[3,192,256]{2,1,0:T(8,128)(2,1)S(1)} %get-tuple-element.41.refs_3_), channel_id=1, source_target_pairs={{4,8},{8,4},{6,10},{10,6},{20,24},{24,20},{22,26},{26,22},{5,9},{9... | collective-permute-start | bytes 884744 | tf_op jit(solution)/shard_map/ppermute | solution.py:332
  7.8 14.7 %collective-permute-start.8 = (bf16[3,192,256]{2,1,0:T(8,128)(2,1)S(1)}, bf16[3,192,256]{2,1,0:T(8,128)(2,1)S(1)}, u32[]{:S(2)}, u32[]{:S(2)}) collective-permute-start(bf16[3,192,256]{2,1,0:T(8,128)(2,1)S(1)} %get-tuple-element.41.refs_3_), channel_id=1, source_target_pairs={{0,4},{4,0},{8,12},{12,8},{2,6},{6,2},{10,14},{14,10},{16,20},{20,... | collective-permute-start | bytes 884744 | tf_op jit(solution)/shard_map/ppermute | solution.py:332
  13.5 11.0 %collective-permute-start.7 = (bf16[3,192,256]{2,1,0:T(8,128)(2,1)S(1)}, bf16[3,192,256]{2,1,0:T(8,128)(2,1)}, u32[]{:S(2)}, u32[]{:S(2)}) collective-permute-start(bf16[3,192,256]{2,1,0:T(8,128)(2,1)S(1)} %get-tuple-element.40.refs_3_), channel_id=1, source_target_pairs={{4,8},{8,4},{6,10},{10,6},{20,24},{24,20},{22,26},{26,22},{5,9},{9... | collective-permute-start | bytes 884744 | tf_op jit(solution)/shard_map/ppermute | solution.py:332
  15.7 12.6 %collective-permute-start.6 = (bf16[3,192,256]{2,1,0:T(8,128)(2,1)S(1)}, bf16[3,192,256]{2,1,0:T(8,128)(2,1)S(1)}, u32[]{:S(2)}, u32[]{:S(2)}) collective-permute-start(bf16[3,192,256]{2,1,0:T(8,128)(2,1)S(1)} %get-tuple-element.40.refs_3_), channel_id=1, source_target_pairs={{0,4},{4,0},{8,12},{12,8},{2,6},{6,2},{10,14},{14,10},{16,20},{20,... | collective-permute-start | bytes 884744 | tf_op jit(solution)/shard_map/ppermute | solution.py:332
  15.8 15.0 %collective-permute-start.17 = (bf16[3,192,256]{2,1,0:T(8,128)(2,1)S(1)}, bf16[3,192,256]{2,1,0:T(8,128)(2,1)S(1)}, u32[]{:S(2)}, u32[]{:S(2)}) collective-permute-start(bf16[3,192,256]{2,1,0:T(8,128)(2,1)S(1)} %collective-permute-done.4.refs_5_), channel_id=1, source_target_pairs={{4,8},{8,4},{6,10},{10,6},{20,24},{24,20},{22,26},{26,22},{5,9},{9... | collective-permute-start | bytes 884744 | tf_op jit(solution)/shard_map/ppermute | solution.py:332
  18.9 16.1 %collective-permute-start.10 = (bf16[3,192,256]{2,1,0:T(8,128)(2,1)S(1)}, bf16[3,192,256]{2,1,0:T(8,128)(2,1)S(1)}, u32[]{:S(2)}, u32[]{:S(2)}) collective-permute-start(bf16[3,192,256]{2,1,0:T(8,128)(2,1)S(1)} %collective-permute-done.4.refs_5_), channel_id=1, source_target_pairs={{0,18},{4,22},{8,26},{12,30},{2,16},{6,20},{10,24},{14,28},{16,2},... | collective-permute-start | bytes 884744 | tf_op jit(solution)/shard_map/ppermute | solution.py:332
  22.4 12.6 %collective-permute-start.16 = (bf16[3,192,256]{2,1,0:T(8,128)(2,1)}, bf16[3,192,256]{2,1,0:T(8,128)(2,1)}, u32[]{:S(2)}, u32[]{:S(2)}) collective-permute-start(bf16[3,192,256]{2,1,0:T(8,128)(2,1)} %collective-permute-done.5), channel_id=1, source_target_pairs={{4,0},{8,12},{6,2},{10,14},{20,16},{24,28},{22,18},{26,30},{5,1},{... | collective-permute-start | bytes 884744 | tf_op jit(solution)/shard_map/ppermute | solution.py:332
  24.4 15.6 %collective-permute-start.18 = (bf16[3,192,256]{2,1,0:T(8,128)(2,1)S(1)}, bf16[3,192,256]{2,1,0:T(8,128)(2,1)S(1)}, u32[]{:S(2)}, u32[]{:S(2)}) collective-permute-start(bf16[3,192,256]{2,1,0:T(8,128)(2,1)S(1)} %collective-permute-done.8.refs_5_), channel_id=1, source_target_pairs={{0,18},{4,22},{8,26},{12,30},{2,16},{6,20},{10,24},{14,28},{16,2},... | collective-permute-start | bytes 884744 | tf_op jit(solution)/shard_map/ppermute | solution.py:332
  28.4 15.4 %collective-permute-start.14 = (bf16[3,192,256]{2,1,0:T(8,128)(2,1)S(1)}, bf16[3,192,256]{2,1,0:T(8,128)(2,1)}, u32[]{:S(2)}, u32[]{:S(2)}) collective-permute-start(bf16[3,192,256]{2,1,0:T(8,128)(2,1)S(1)} %collective-permute-done.8.refs_5_), channel_id=1, source_target_pairs={{4,8},{8,4},{6,10},{10,6},{20,24},{24,20},{22,26},{26,22},{5,9},{9... | collective-permute-start | bytes 884744 | tf_op jit(solution)/shard_map/ppermute | solution.py:332
  30.8 14.4 %collective-permute-start.15 = (bf16[3,192,256]{2,1,0:T(8,128)(2,1)}, bf16[3,192,256]{2,1,0:T(8,128)(2,1)}, u32[]{:S(2)}, u32[]{:S(2)}) collective-permute-start(bf16[3,192,256]{2,1,0:T(8,128)(2,1)} %copy-done.5), channel_id=1, source_target_pairs={{4,0},{8,12},{6,2},{10,14},{20,16},{24,28},{22,18},{26,30},{5,1},{... | collective-permute-start | bytes 884744 | tf_op jit(solution)/shard_map/ppermute | solution.py:332
  35.0 11.3 %collective-permute-start.13 = (bf16[3,192,256]{2,1,0:T(8,128)(2,1)S(1)}, bf16[3,192,256]{2,1,0:T(8,128)(2,1)S(1)}, u32[]{:S(2)}, u32[]{:S(2)}) collective-permute-start(bf16[3,192,256]{2,1,0:T(8,128)(2,1)S(1)} %collective-permute-done.6.refs_5_), channel_id=1, source_target_pairs={{4,8},{8,4},{6,10},{10,6},{20,24},{24,20},{22,26},{26,22},{5,9},{9... | collective-permute-start | bytes 884744 | tf_op jit(solution)/shard_map/ppermute | solution.py:332
  40.1 10.4 %collective-permute-start.11 = (bf16[3,192,256]{2,1,0:T(8,128)(2,1)S(1)}, bf16[3,192,256]{2,1,0:T(8,128)(2,1)S(1)}, u32[]{:S(2)}, u32[]{:S(2)}) collective-permute-start(bf16[3,192,256]{2,1,0:T(8,128)(2,1)S(1)} %collective-permute-done.6.refs_5_), channel_id=1, source_target_pairs={{0,18},{4,22},{8,26},{12,30},{2,16},{6,20},{10,24},{14,28},{16,2},... | collective-permute-start | bytes 884744 | tf_op jit(solution)/shard_map/ppermute | solution.py:332
  43.8 14.4 %collective-permute-start.23 = (bf16[3,192,256]{2,1,0:T(8,128)(2,1)S(1)}, bf16[3,192,256]{2,1,0:T(8,128)(2,1)S(1)}, u32[]{:S(2)}, u32[]{:S(2)}) collective-permute-start(bf16[3,192,256]{2,1,0:T(8,128)(2,1)S(1)} %collective-permute-done.17), channel_id=1, source_target_pairs={{4,0},{8,12},{6,2},{10,14},{20,16},{24,28},{22,18},{26,30},{5,1},{... | collective-permute-start | bytes 884744 | tf_op jit(solution)/shard_map/ppermute | solution.py:332
  45.2 11.6 %collective-permute-start.19 = (bf16[3,192,256]{2,1,0:T(8,128)(2,1)S(1)}, bf16[3,192,256]{2,1,0:T(8,128)(2,1)S(1)}, u32[]{:S(2)}, u32[]{:S(2)}) collective-permute-start(bf16[3,192,256]{2,1,0:T(8,128)(2,1)S(1)} %broadcast_select_fusion.4.refs_7_), channel_id=1, source_target_pairs={{0,18},{4,22},{8,26},{12,30},{2,16},{6,20},{10,24},{14,28},{16,2},... | collective-permute-start | bytes 884744 | tf_op jit(solution)/shard_map/ppermute | solution.py:332
  46.3 32.7 %collective-permute-start.3 = (bf16[3,192,768]{2,1,0:T(8,128)(2,1)}, bf16[3,192,768]{2,1,0:T(8,128)(2,1)S(1)}, u32[]{:S(2)}, u32[]{:S(2)}) collective-permute-start(bf16[3,192,768]{2,1,0:T(8,128)(2,1)} %dynamic-slice_bitcast_fusion), channel_id=1, source_target_pairs={{0,2},{2,0},{4,6},{6,4},{8,10},{10,8},{12,14},{14,12},{1,3},{3,1},... | collective-permute-start | bytes 2654216 | tf_op jit(solution)/shard_map/ppermute | solution.py:362
  51.8 11.3 %collective-permute-start.24 = (bf16[3,192,256]{2,1,0:T(8,128)(2,1)S(1)}, bf16[3,192,256]{2,1,0:T(8,128)(2,1)S(1)}, u32[]{:S(2)}, u32[]{:S(2)}) collective-permute-start(bf16[3,192,256]{2,1,0:T(8,128)(2,1)S(1)} %broadcast_select_fusion.1.refs_7_), channel_id=1, source_target_pairs={{0,18},{4,22},{8,26},{12,30},{2,16},{6,20},{10,24},{14,28},{16,2},... | collective-permute-start | bytes 884744 | tf_op jit(solution)/shard_map/ppermute | solution.py:332
  56.8 11.6 %collective-permute-start.21 = (bf16[3,192,256]{2,1,0:T(8,128)(2,1)S(1)}, bf16[3,192,256]{2,1,0:T(8,128)(2,1)S(1)}, u32[]{:S(2)}, u32[]{:S(2)}) collective-permute-start(bf16[3,192,256]{2,1,0:T(8,128)(2,1)S(1)} %collective-permute-done.13), channel_id=1, source_target_pairs={{4,0},{8,12},{6,2},{10,14},{20,16},{24,28},{22,18},{26,30},{5,1},{... | collective-permute-start | bytes 884744 | tf_op jit(solution)/shard_map/ppermute | solution.py:332
  58.1 11.6 %collective-permute-start.20 = (bf16[3,192,256]{2,1,0:T(8,128)(2,1)S(1)}, bf16[3,192,256]{2,1,0:T(8,128)(2,1)S(1)}, u32[]{:S(2)}, u32[]{:S(2)}) collective-permute-start(bf16[3,192,256]{2,1,0:T(8,128)(2,1)S(1)} %broadcast_select_fusion.5.refs_7_), channel_id=1, source_target_pairs={{0,18},{4,22},{8,26},{12,30},{2,16},{6,20},{10,24},{14,28},{16,2},... | collective-permute-start | bytes 884744 | tf_op jit(solution)/shard_map/ppermute | solution.py:332
  59.8 17.5 %collective-permute-start.2 = (bf16[2,64,1536]{2,1,0:T(8,128)(2,1)S(1)}, bf16[2,64,1536]{2,1,0:T(8,128)(2,1)S(1)}, u32[]{:S(2)}, u32[]{:S(2)}) collective-permute-start(bf16[2,64,1536]{2,1,0:T(8,128)(2,1)S(1)} %copy-done), channel_id=1, source_target_pairs={{3,6},{7,10},{11,14},{5,0},{9,4},{13,8},{19,22},{23,26},{27,30},{2... | collective-permute-start | bytes 1179656 | tf_op jit(solution)/shard_map/ppermute | solution.py:357
  63.1 12.6 %collective-permute-start.25 = (bf16[3,192,256]{2,1,0:T(8,128)(2,1)S(1)}, bf16[3,192,256]{2,1,0:T(8,128)(2,1)S(1)}, u32[]{:S(2)}, u32[]{:S(2)}) collective-permute-start(bf16[3,192,256]{2,1,0:T(8,128)(2,1)S(1)} %broadcast_select_fusion.2.refs_9_), channel_id=1, source_target_pairs={{0,18},{4,22},{8,26},{12,30},{2,16},{6,20},{10,24},{14,28},{16,2},... | collective-permute-start | bytes 884744 | tf_op jit(solution)/shard_map/ppermute | solution.py:332
  69.7 12.7 %collective-permute-start.27 = (bf16[3,192,256]{2,1,0:T(8,128)(2,1)S(1)}, bf16[3,192,256]{2,1,0:T(8,128)(2,1)S(1)}, u32[]{:S(2)}, u32[]{:S(2)}) collective-permute-start(bf16[3,192,256]{2,1,0:T(8,128)(2,1)S(1)} %broadcast_select_fusion.refs_9_), channel_id=1, source_target_pairs={{0,18},{4,22},{8,26},{12,30},{2,16},{6,20},{10,24},{14,28},{16,2},... | collective-permute-start | bytes 884744 | tf_op jit(solution)/shard_map/ppermute | solution.py:332
  75.8 12.0 %collective-permute-start.26 = (bf16[3,192,256]{2,1,0:T(8,128)(2,1)S(1)}, bf16[3,192,256]{2,1,0:T(8,128)(2,1)S(1)}, u32[]{:S(2)}, u32[]{:S(2)}) collective-permute-start(bf16[3,192,256]{2,1,0:T(8,128)(2,1)S(1)} %broadcast_select_fusion.3.refs_9_), channel_id=1, source_target_pairs={{0,18},{4,22},{8,26},{12,30},{2,16},{6,20},{10,24},{14,28},{16,2},... | collective-permute-start | bytes 884744 | tf_op jit(solution)/shard_map/ppermute | solution.py:332
  94.8 13.4 %collective-permute-start.29 = (bf16[2,64,1536]{2,1,0:T(8,128)(2,1)S(1)}, bf16[2,64,1536]{2,1,0:T(8,128)(2,1)S(1)}, u32[]{:S(2)}, u32[]{:S(2)}) collective-permute-start(bf16[2,64,1536]{2,1,0:T(8,128)(2,1)S(1)} %project.2.refs_6_), channel_id=1, source_target_pairs={{0,1},{2,3},{4,5},{6,7},{8,9},{10,11},{12,13},{14,15},{16,17},{18,... | collective-permute-start | bytes 1179656 | tf_op jit(solution)/shard_map/ppermute | solution.py:525
  (18 other events, 216.7 us)

commit v5 on v4

--- a/solution.py
+++ b/solution.py
@@ -108,57 +108,70 @@
     return near_masks, far_masks
 
 
-def attend_heads(normed, weights, gains, near_masks, far_masks, view_tok, outputs):
+def unit_rows(values, gain):
+    scale = lax.rsqrt(jnp.mean(values * values, axis=-1, keepdims=True) + epsilon)
+    return (values * scale * gain).astype(jnp.bfloat16)
+
+
+def dot(a, b):
+    return jnp.dot(a, b, preferred_element_type=jnp.float32)
+
+
+def exponents(queries, keys, mask):
+    scores = lax.dot_general(
+        queries, keys, (((1,), (1,)), ((), ())), preferred_element_type=jnp.float32
+    )
+    return jnp.exp(scores * queries.shape[1] ** (-0.5)) * mask
+
+
+def raw_heads(normed, weights, micro_count, view_tok):
+    part = weights.shape[1] // 3
+    half = 2 * micro_count * view_tok
+    return (
+        dot(normed[0:half, :], weights[:, 0:part]),
+        dot(normed[...], weights[:, part : 2 * part]),
+        dot(normed[...], weights[:, 2 * part : 3 * part]),
+    )
+
+
+def attend_heads(raw, gains, near_masks, far_masks, view_tok, outputs):
+    raw_q, raw_k, raw_v = raw
     micro_count = len(near_masks)
-    part = weights.shape[1] // 3
+    part = raw_q.shape[1]
     head = gains.shape[1]
     two = 2 * view_tok
     half = micro_count * two
-
-    def unit(values, gain):
-        return (
-            values
-            * lax.rsqrt(jnp.mean(values * values, axis=-1, keepdims=True) + epsilon)
-            * gain
-        ).astype(jnp.bfloat16)
-
-    def dot(a, b):
-        return jnp.dot(a, b, preferred_element_type=jnp.float32)
-
-    def dot_t(a, b):
-        return lax.dot_general(
-            a, b, (((1,), (1,)), ((), ())), preferred_element_type=jnp.float32
-        )
-
-    raw_q = dot(normed[0:half, :], weights[:, 0:part])
-    raw_k = dot(normed[...], weights[:, part : 2 * part])
-    raw_v = dot(normed[...], weights[:, 2 * part : 3 * part])
-    count = part // head
-    outs = [[None] * count for _ in range(micro_count)]
-    for i in range(count):
+    att_own, att_pair, offset = outputs
+    cases = []
+    for i in range(part // head):
         cols = slice(i * head, (i + 1) * head)
-        queries = unit(raw_q[:, cols], gains[0:1, :])
-        keys = unit(raw_k[:, cols], gains[1:2, :])
+        queries = unit_rows(raw_q[:, cols], gains[0:1, :])
+        keys = unit_rows(raw_k[:, cols], gains[1:2, :])
         values = raw_v[:, cols].astype(jnp.bfloat16)
         for m in range(micro_count):
             near = slice(m * two, (m + 1) * two)
             far = slice(half + m * two, half + (m + 1) * two)
-            q = queries[near]
-            scale = head ** (-0.5)
-            e_near = jnp.exp(dot_t(q, keys[near]) * scale) * near_masks[m]
-            e_far = jnp.exp(dot_t(q, keys[far]) * scale) * far_masks[m]
-            total = jnp.sum(e_near, axis=-1, keepdims=True) + jnp.sum(
-                e_far, axis=-1, keepdims=True
+            cases.append((i, m, queries[near], keys, values, near, far))
+    weights = []
+    for i, m, queries, keys, values, near, far in cases:
+        weights.append(
+            (
+                exponents(queries, keys[near], near_masks[m]),
+                exponents(queries, keys[far], far_masks[m]),
             )
-            mixed = dot(e_near.astype(jnp.bfloat16), values[near]) + dot(
-                e_far.astype(jnp.bfloat16), values[far]
-            )
-            outs[m][i] = (mixed / total).astype(jnp.bfloat16)
-    att_own, att_pair, offset = outputs
-    for m in range(micro_count):
-        joined = jnp.concatenate(outs[m], axis=1)
-        att_own[m, :, offset : offset + part] = joined[:view_tok]
-        att_pair[m, :, offset : offset + part] = joined[view_tok:]
+        )
+    for case, (e_near, e_far) in zip(cases, weights):
+        i, m, queries, keys, values, near, far = case
+        total = jnp.sum(e_near, axis=-1, keepdims=True) + jnp.sum(
+            e_far, axis=-1, keepdims=True
+        )
+        mixed = dot(e_near.astype(jnp.bfloat16), values[near]) + dot(
+            e_far.astype(jnp.bfloat16), values[far]
+        )
+        attended = (mixed / total).astype(jnp.bfloat16)
+        put = slice(offset + i * head, offset + (i + 1) * head)
+        att_own[m, :, put] = attended[:view_tok]
+        att_pair[m, :, put] = attended[view_tok:]
 
 
 def attend_part_kernel(offset, *refs):
@@ -188,8 +201,7 @@
     for move in moves:
         move.wait()
     attend_heads(
-        normed,
-        weights,
+        raw_heads(normed, weights, att_own.shape[0], view_tok),
         gains,
         near_masks,
         far_masks,
@@ -216,10 +228,13 @@
         for m in range(micro_count):
             normalise(streams.at[slot], m, slot, modulation, sets, normed)
     offset = 0
+    raw = raw_heads(normed, weights[0], micro_count, view_tok)
     for index in range(3):
+        current = raw
+        if index < 2:
+            raw = raw_heads(normed, weights[index + 1], micro_count, view_tok)
         attend_heads(
-            normed,
-            weights[index],
+            current,
             gains,
             near_masks,
             far_masks,
@@ -262,7 +277,7 @@
     ]
     for copy in copies:
         copy.start()
-    for copy in copies:
+    for copy in copies[:2]:
         copy.wait()
     tokens = micro_count * view_tok
     here = att_own[...].reshape(tokens, part)
@@ -278,6 +293,9 @@
             out_weight[pl.ds(second, part), cols],
             preferred_element_type=jnp.float32,
         )
+        if index == 0:
+            for copy in copies[2:]:
+                copy.wait()
         for m in range(micro_count):
             gate = gates[sets[m]][m : m + 1, cols].astype(jnp.float32)
             value = (
@@ -390,8 +408,8 @@
     second, across_second, outer_last = [], [], []
     for kind in range(3):
         before = before + (across_first[kind],)
-        a = tied(inner_next[kind], outer_next[kind], *before)
-        b = tied(outer_next[kind], inner_next[kind], *before)
+        a = tied(inner_next[kind], *before)
+        b = tied(outer_next[kind], *before)
         outer_last.append(send(a, outward_steps))
         second.append(jnp.where(middle, from_inner[kind], b))
         across_second.append(cross(second[kind]))

time: 133 us -> 131 us (0.985)
  Pallas kernels: 25 us -> 22.1 us
    ppermute x24, starting transfers between devices: 48.5 us -> 45.5 us  [send(): return lax.ppermute(value, line_axes, pairs)]
    ppermute x24, waiting for transfers between devices: 19 us -> 21.1 us  [send(): return lax.ppermute(value, line_axes, pairs)]
    ppermute x2, starting transfers between devices: 2.97 us -> 4.9 us  [lend(): return lax.ppermute(stream, ('seq', 'section'), pairs)]
    pallas_call x1, Pallas kernels: 8.14 us -> 6.43 us  [paired_body(): attend(set_views, own, pair, halo, pair_halo, modulation[0], norm_gain[0]...]
    pallas_call x3, Pallas kernels: 9.99 us -> 8.42 us  [attend_part(): pl.pallas_call(functools.partial(attend_part_kernel, cuts[index]), out_sh...]
  transfers between devices with their start and end apart: 34 -> 34, of which waited for: 13 -> 14; matrix products, arithmetic and copies ran while one was open for 6% -> 5% of each run, Pallas kernels for 6% -> 6%
where the time goes in v5:
time: 131 us; the launch traced here: 130 us
  starting transfers between devices  59.5 us (45%)
  waiting for transfers between devices  41.5 us (32%)
  Pallas kernels  22.1 us (17%)
  local copies, waits for them, and re-layouts  3.41 us (3%)
  other arithmetic  3.1 us (2%)
    ppermute x24, starting transfers between devices, send(): return lax.ppermute(value, line_axes, pairs)  45.5 us
    ppermute x24, waiting for transfers between devices, send(): return lax.ppermute(value, line_axes, pairs)  21.1 us
    ppermute x1, waiting for transfers between devices, paired_body(): lax.ppermute(result, 'section', [(i, i + 1) for i in range(section_count...  10.9 us
    pallas_call x3, Pallas kernels, attend_part(): pl.pallas_call(functools.partial(attend_part_kernel, cuts[index]), out_sh...  8.42 us
    pallas_call x1, Pallas kernels, paired_body(): attend(set_views, own, pair, halo, pair_halo, modulation[0], norm_gain[0]...  6.43 us
    ppermute x1, waiting for transfers between devices, paired_body(): halo = lax.ppermute(own, 'seq', swap_edges)  5.71 us
    pallas_call x2, Pallas kernels, project(): pl.pallas_call(functools.partial(project_kernel, last), out_shape=jax.Sha...  5.63 us
    ppermute x2, starting transfers between devices, lend(): return lax.ppermute(stream, ('seq', 'section'), pairs)  4.9 us
  transfers between devices with their start and end apart: 34, of which 14 were waited for; matrix products, arithmetic and copies ran while one was open for 5% of the time, Pallas kernels for 6%

profile of v5, /device:TPU:11, one launch (start us, length us, event | category | flops | bytes accessed | tf_op | source)
XLA Modules:
  0.0 130.2 jit_solution(14038200287712344503)
XLA Ops:
  1.9 3.2 %collective-permute-start.5 = (bf16[3,192,256]{2,1,0:T(8,128)(2,1)S(1)}, bf16[3,192,256]{2,1,0:T(8,128)(2,1)}, u32[]{:S(2)}, u32[]{:S(2)}) collective-permute-start(bf16[3,192,256]{2,1,0:T(8,128)(2,1)S(1)} %get-tuple-element.77.refs_3_), channel_id=1, source_target_pairs={{4,8},{8,4},{6,10},{10,6},{20,24},{24,20},{22,26},{26,22},{5,9},{9... | collective-permute-start | bytes 884744 | tf_op jit(solution)/shard_map/ppermute | solution.py:350
  5.2 2.6 %collective-permute-start.9 = (bf16[3,192,256]{2,1,0:T(8,128)(2,1)S(1)}, bf16[3,192,256]{2,1,0:T(8,128)(2,1)S(1)}, u32[]{:S(2)}, u32[]{:S(2)}) collective-permute-start(bf16[3,192,256]{2,1,0:T(8,128)(2,1)S(1)} %get-tuple-element.41.refs_3_), channel_id=1, source_target_pairs={{4,8},{8,4},{6,10},{10,6},{20,24},{24,20},{22,26},{26,22},{5,9},{9... | collective-permute-start | bytes 884744 | tf_op jit(solution)/shard_map/ppermute | solution.py:350
  7.8 4.7 %collective-permute-done.5 = bf16[3,192,256]{2,1,0:T(8,128)(2,1)} collective-permute-done((bf16[3,192,256]{2,1,0:T(8,128)(2,1)S(1)}, bf16[3,192,256]{2,1,0:T(8,128)(2,1)}, u32[]{:S(2)}, u32[]{:S(2)}) %collective-permute-start.5) | collective-permute-done | bytes 294944 | tf_op jit(solution)/shard_map/ppermute | solution.py:350
  13.5 2.2 %collective-permute-start.7 = (bf16[3,192,256]{2,1,0:T(8,128)(2,1)S(1)}, bf16[3,192,256]{2,1,0:T(8,128)(2,1)}, u32[]{:S(2)}, u32[]{:S(2)}) collective-permute-start(bf16[3,192,256]{2,1,0:T(8,128)(2,1)S(1)} %get-tuple-element.40.refs_3_), channel_id=1, source_target_pairs={{4,8},{8,4},{6,10},{10,6},{20,24},{24,20},{22,26},{26,22},{5,9},{9... | collective-permute-start | bytes 884744 | tf_op jit(solution)/shard_map/ppermute | solution.py:350
  15.8 3.1 %collective-permute-start.10 = (bf16[3,192,256]{2,1,0:T(8,128)(2,1)S(1)}, bf16[3,192,256]{2,1,0:T(8,128)(2,1)S(1)}, u32[]{:S(2)}, u32[]{:S(2)}) collective-permute-start(bf16[3,192,256]{2,1,0:T(8,128)(2,1)S(1)} %collective-permute-done.4.refs_5_), channel_id=1, source_target_pairs={{0,18},{4,22},{8,26},{12,30},{2,16},{6,20},{10,24},{14,28},{16,2},... | collective-permute-start | bytes 884744 | tf_op jit(solution)/shard_map/ppermute | solution.py:350
  18.9 4.3 %collective-permute-start.15 = (bf16[3,192,256]{2,1,0:T(8,128)(2,1)}, bf16[3,192,256]{2,1,0:T(8,128)(2,1)}, u32[]{:S(2)}, u32[]{:S(2)}) collective-permute-start(bf16[3,192,256]{2,1,0:T(8,128)(2,1)} %collective-permute-done.5), channel_id=1, source_target_pairs={{4,0},{8,12},{6,2},{10,14},{20,16},{24,28},{22,18},{26,30},{5,1},{... | collective-permute-start | bytes 884744 | tf_op jit(solution)/shard_map/ppermute | solution.py:350
  23.2 3.2 %collective-permute-start.21 = (bf16[3,192,256]{2,1,0:T(8,128)(2,1)S(1)}, bf16[3,192,256]{2,1,0:T(8,128)(2,1)S(1)}, u32[]{:S(2)}, u32[]{:S(2)}) collective-permute-start(bf16[3,192,256]{2,1,0:T(8,128)(2,1)S(1)} %collective-permute-done.4.refs_5_), channel_id=1, source_target_pairs={{4,8},{8,4},{6,10},{10,6},{20,24},{24,20},{22,26},{26,22},{5,9},{9... | collective-permute-start | bytes 884744 | tf_op jit(solution)/shard_map/ppermute | solution.py:350
  26.5 2.6 %collective-permute-start.12 = (bf16[3,192,256]{2,1,0:T(8,128)(2,1)}, bf16[3,192,256]{2,1,0:T(8,128)(2,1)}, u32[]{:S(2)}, u32[]{:S(2)}) collective-permute-start(bf16[3,192,256]{2,1,0:T(8,128)(2,1)} %collective-permute-done.7), channel_id=1, source_target_pairs={{4,0},{8,12},{6,2},{10,14},{20,16},{24,28},{22,18},{26,30},{5,1},{... | collective-permute-start | bytes 884744 | tf_op jit(solution)/shard_map/ppermute | solution.py:350
  29.1 2.6 %collective-permute-start.16 = (bf16[3,192,256]{2,1,0:T(8,128)(2,1)S(1)}, bf16[3,192,256]{2,1,0:T(8,128)(2,1)S(1)}, u32[]{:S(2)}, u32[]{:S(2)}) collective-permute-start(bf16[3,192,256]{2,1,0:T(8,128)(2,1)S(1)} %collective-permute-done.8.refs_5_), channel_id=1, source_target_pairs={{0,18},{4,22},{8,26},{12,30},{2,16},{6,20},{10,24},{14,28},{16,2},... | collective-permute-start | bytes 884744 | tf_op jit(solution)/shard_map/ppermute | solution.py:350
  35.8 3.1 %collective-permute-start.13 = (bf16[3,192,256]{2,1,0:T(8,128)(2,1)S(1)}, bf16[3,192,256]{2,1,0:T(8,128)(2,1)S(1)}, u32[]{:S(2)}, u32[]{:S(2)}) collective-permute-start(bf16[3,192,256]{2,1,0:T(8,128)(2,1)S(1)} %collective-permute-done.8.refs_5_), channel_id=1, source_target_pairs={{4,8},{8,4},{6,10},{10,6},{20,24},{24,20},{22,26},{26,22},{5,9},{9... | collective-permute-start | bytes 884744 | tf_op jit(solution)/shard_map/ppermute | solution.py:350
  45.5 3.4 %collective-permute-start.17 = (bf16[3,192,256]{2,1,0:T(8,128)(2,1)S(1)}, bf16[3,192,256]{2,1,0:T(8,128)(2,1)S(1)}, u32[]{:S(2)}, u32[]{:S(2)}) collective-permute-start(bf16[3,192,256]{2,1,0:T(8,128)(2,1)S(1)} %broadcast_select_fusion.4.refs_7_), channel_id=1, source_target_pairs={{0,18},{4,22},{8,26},{12,30},{2,16},{6,20},{10,24},{14,28},{16,2},... | collective-permute-start | bytes 884744 | tf_op jit(solution)/shard_map/ppermute | solution.py:350
  58.3 2.9 %collective-permute-start.2 = (bf16[2,64,1536]{2,1,0:T(8,128)(2,1)S(1)}, bf16[2,64,1536]{2,1,0:T(8,128)(2,1)S(1)}, u32[]{:S(2)}, u32[]{:S(2)}) collective-permute-start(bf16[2,64,1536]{2,1,0:T(8,128)(2,1)S(1)} %copy-done), channel_id=1, source_target_pairs={{3,6},{7,10},{11,14},{5,0},{9,4},{13,8},{19,22},{23,26},{27,30},{2... | collective-permute-start | bytes 1179656 | tf_op jit(solution)/shard_map/ppermute | solution.py:375
  66.6 2.8 %collective-permute-done.18.refs_8_ = bf16[3,192,256]{2,1,0:T(8,128)(2,1)S(1)} collective-permute-done((bf16[3,192,256]{2,1,0:T(8,128)(2,1)S(1)}, bf16[3,192,256]{2,1,0:T(8,128)(2,1)S(1)}, u32[]{:S(2)}, u32[]{:S(2)}) %collective-permute-start.18) | collective-permute-done | bytes 294944 | tf_op jit(solution)/shard_map/ppermute | solution.py:350
  70.9 4.8 %collective-permute-done.25.refs_10_ = bf16[3,192,256]{2,1,0:T(8,128)(2,1)S(1)} collective-permute-done((bf16[3,192,256]{2,1,0:T(8,128)(2,1)S(1)}, bf16[3,192,256]{2,1,0:T(8,128)(2,1)S(1)}, u32[]{:S(2)}, u32[]{:S(2)}) %collective-permute-start.25) | collective-permute-done | bytes 294944 | tf_op jit(solution)/shard_map/ppermute | solution.py:350
  79.2 2.8 %attend_part.3 = (bf16[2,64,768]{2,1,0:T(8,128)(2,1)S(1)}, bf16[2,64,768]{2,1,0:T(8,128)(2,1)S(1)}, bf16[1536,768]{1,0:T(8,128)(2,1)S(1)}) custom-call(s32[2,6]{1,0:T(2,128)S(1)} %copy-done.3, bf16[512,1536]{1,0:T(8,128)(2,1)S(1)} %norm.1.refs_1_, f32[2,128]{1,0:T(2,128)S(1)} %bitcast.31, bf16[3,192,256]{2,1,0:T(8,128)(2,1)S(1)} %get-tuple-element.77.refs_3_, ...), custom_call_target="tpu_custom_call" | custom-call | tf_op jit(solution)/shard_map/attend_part/pallas_call | solution.py:447
  82.1 2.8 %attend_part.4 = (bf16[2,64,768]{2,1,0:T(8,128)(2,1)S(1)}, bf16[2,64,768]{2,1,0:T(8,128)(2,1)S(1)}, bf16[1536,768]{1,0:T(8,128)(2,1)S(1)}) custom-call(s32[2,6]{1,0:T(2,128)S(1)} %copy-done.3, bf16[512,1536]{1,0:T(8,128)(2,1)S(1)} %norm.1.refs_1_, f32[2,128]{1,0:T(2,128)S(1)} %bitcast.32, ...), custom_call_target="tpu_custom_call", output_to_operand_aliasing={{0}: (11, {}), {1}: (12, {})} | custom-call | tf_op jit(solution)/shard_map/attend_part/pallas_call | solution.py:447
  84.9 3.4 %collective-permute-done.26.refs_10_ = bf16[3,192,256]{2,1,0:T(8,128)(2,1)S(1)} collective-permute-done((bf16[3,192,256]{2,1,0:T(8,128)(2,1)S(1)}, bf16[3,192,256]{2,1,0:T(8,128)(2,1)S(1)}, u32[]{:S(2)}, u32[]{:S(2)}) %collective-permute-start.26) | collective-permute-done | bytes 294944 | tf_op jit(solution)/shard_map/ppermute | solution.py:350
  88.2 2.8 %attend_part.5 = (bf16[2,64,768]{2,1,0:T(8,128)(2,1)S(1)}, bf16[2,64,768]{2,1,0:T(8,128)(2,1)S(1)}, bf16[1536,768]{1,0:T(8,128)(2,1)S(1)}) custom-call(s32[2,6]{1,0:T(2,128)S(1)} %copy-done.3, bf16[512,1536]{1,0:T(8,128)(2,1)S(1)} %norm.1.refs_1_, f32[2,128]{1,0:T(2,128)S(1)} %bitcast.33, ...), custom_call_target="tpu_custom_call", output_to_operand_aliasing={{0}: (11, {}), {1}: (12, {})} | custom-call | tf_op jit(solution)/shard_map/attend_part/pallas_call | solution.py:447
  92.6 2.3 %project.2.refs_6_ = bf16[2,64,1536]{2,1,0:T(8,128)(2,1)S(1)} custom-call(s32[2,6]{1,0:T(2,128)S(1)} %copy-done.3, bf16[2,64,768]{2,1,0:T(8,128)(2,1)S(1)} %get-tuple-element.68.refs_1_, bf16[2,64,768]{2,1,0:T(8,128)(2,1)S(1)} %collective-permute-done.28.refs_2_, bf16[2,64,1536]{2,1,0:T(8,128)(2,1)S(1)} %copy-done, bf16[6,2,1536]{2,1,0:T(2,128)(2,1)S(1)} %bitcast.29, ...), custom_call_target="tpu_custom_call" | custom-call | tf_op jit(solution)/shard_map/project/pallas_call | solution.py:481
  96.2 10.9 %collective-permute-done.29.refs_1_.refs_3_ = bf16[2,64,1536]{2,1,0:T(8,128)(2,1)S(1)} collective-permute-done((bf16[2,64,1536]{2,1,0:T(8,128)(2,1)S(1)}, bf16[2,64,1536]{2,1,0:T(8,128)(2,1)S(1)}, u32[]{:S(2)}, u32[]{:S(2)}) %collective-permute-start.29) | collective-permute-done | bytes 393248 | tf_op jit(solution)/shard_map/ppermute | solution.py:543
  107.2 3.6 %collective-permute-start.31 = (bf16[2,64,1536]{2,1,0:T(8,128)(2,1)S(1)}, bf16[2,64,1536]{2,1,0:T(8,128)(2,1)S(1)}, u32[]{:S(2)}, u32[]{:S(2)}) collective-permute-start(bf16[2,64,1536]{2,1,0:T(8,128)(2,1)S(1)} %collective-permute-done.29.refs_1_.refs_3_), channel_id=1, source_target_pairs={{2,4},{6,8},{10,12},{4,2},{8,6},{12,10},{3,5},{7,9},{11,13},{5,3},... | collective-permute-start | bytes 1179656 | tf_op jit(solution)/shard_map/ppermute | solution.py:502
  110.8 5.7 %collective-permute-done.31.refs_3_ = bf16[2,64,1536]{2,1,0:T(8,128)(2,1)S(1)} collective-permute-done((bf16[2,64,1536]{2,1,0:T(8,128)(2,1)S(1)}, bf16[2,64,1536]{2,1,0:T(8,128)(2,1)S(1)}, u32[]{:S(2)}, u32[]{:S(2)}) %collective-permute-start.31) | collective-permute-done | bytes 393248 | tf_op jit(solution)/shard_map/ppermute | solution.py:502
  118.8 6.4 %attend.1 = (bf16[2,64,768]{2,1,0:T(8,128)(2,1)S(1)}, bf16[2,64,768]{2,1,0:T(8,128)(2,1)S(1)}) custom-call(s32[2,6]{1,0:T(2,128)S(1)} %copy-done.3, bf16[2,64,1536]{2,1,0:T(8,128)(2,1)S(1)} %collective-permute-done.29.refs_1_.refs_3_, bf16[2,64,1536]{2,1,0:T(8,128)(2,1)S(1)} %collective-permute-done.30.refs_2_, ...), custom_call_target="tpu_custom_call" | custom-call | tf_op jit(solution)/shard_map/attend/pallas_call | solution.py:505
  126.8 3.3 %project.3 = bf16[2,64,1536]{2,1,0:T(8,128)(2,1)} custom-call(s32[2,6]{1,0:T(2,128)S(1)} %copy-done.3, bf16[2,64,768]{2,1,0:T(8,128)(2,1)S(1)} %get-tuple-element.73.refs_1_, bf16[2,64,768]{2,1,0:T(8,128)(2,1)S(1)} %collective-permute-done.33.refs_2_, bf16[2,64,1536]{2,1,0:T(8,128)(2,1)S(1)} %collective-permute-done.29.refs_1_.refs_3_, ...), custom_call_target="tpu_custom_call" | custom-call | tf_op jit(solution)/shard_map/project/pallas_call | solution.py:481
  (78 shorter events, 40.1 us)
Async XLA Ops:
  1.9 10.6 %collective-permute-start.5 = (bf16[3,192,256]{2,1,0:T(8,128)(2,1)S(1)}, bf16[3,192,256]{2,1,0:T(8,128)(2,1)}, u32[]{:S(2)}, u32[]{:S(2)}) collective-permute-start(bf16[3,192,256]{2,1,0:T(8,128)(2,1)S(1)} %get-tuple-element.77.refs_3_), channel_id=1, source_target_pairs={{4,8},{8,4},{6,10},{10,6},{20,24},{24,20},{22,26},{26,22},{5,9},{9... | collective-permute-start | bytes 884744 | tf_op jit(solution)/shard_map/ppermute | solution.py:350
  5.2 13.7 %collective-permute-start.9 = (bf16[3,192,256]{2,1,0:T(8,128)(2,1)S(1)}, bf16[3,192,256]{2,1,0:T(8,128)(2,1)S(1)}, u32[]{:S(2)}, u32[]{:S(2)}) collective-permute-start(bf16[3,192,256]{2,1,0:T(8,128)(2,1)S(1)} %get-tuple-element.41.refs_3_), channel_id=1, source_target_pairs={{4,8},{8,4},{6,10},{10,6},{20,24},{24,20},{22,26},{26,22},{5,9},{9... | collective-permute-start | bytes 884744 | tf_op jit(solution)/shard_map/ppermute | solution.py:350
  7.8 15.4 %collective-permute-start.8 = (bf16[3,192,256]{2,1,0:T(8,128)(2,1)S(1)}, bf16[3,192,256]{2,1,0:T(8,128)(2,1)S(1)}, u32[]{:S(2)}, u32[]{:S(2)}) collective-permute-start(bf16[3,192,256]{2,1,0:T(8,128)(2,1)S(1)} %get-tuple-element.41.refs_3_), channel_id=1, source_target_pairs={{0,4},{4,0},{8,12},{12,8},{2,6},{6,2},{10,14},{14,10},{16,20},{20,... | collective-permute-start | bytes 884744 | tf_op jit(solution)/shard_map/ppermute | solution.py:350
  13.5 13.0 %collective-permute-start.7 = (bf16[3,192,256]{2,1,0:T(8,128)(2,1)S(1)}, bf16[3,192,256]{2,1,0:T(8,128)(2,1)}, u32[]{:S(2)}, u32[]{:S(2)}) collective-permute-start(bf16[3,192,256]{2,1,0:T(8,128)(2,1)S(1)} %get-tuple-element.40.refs_3_), channel_id=1, source_target_pairs={{4,8},{8,4},{6,10},{10,6},{20,24},{24,20},{22,26},{26,22},{5,9},{9... | collective-permute-start | bytes 884744 | tf_op jit(solution)/shard_map/ppermute | solution.py:350
  15.7 10.7 %collective-permute-start.6 = (bf16[3,192,256]{2,1,0:T(8,128)(2,1)S(1)}, bf16[3,192,256]{2,1,0:T(8,128)(2,1)S(1)}, u32[]{:S(2)}, u32[]{:S(2)}) collective-permute-start(bf16[3,192,256]{2,1,0:T(8,128)(2,1)S(1)} %get-tuple-element.40.refs_3_), channel_id=1, source_target_pairs={{0,4},{4,0},{8,12},{12,8},{2,6},{6,2},{10,14},{14,10},{16,20},{20,... | collective-permute-start | bytes 884744 | tf_op jit(solution)/shard_map/ppermute | solution.py:350
  15.8 15.8 %collective-permute-start.10 = (bf16[3,192,256]{2,1,0:T(8,128)(2,1)S(1)}, bf16[3,192,256]{2,1,0:T(8,128)(2,1)S(1)}, u32[]{:S(2)}, u32[]{:S(2)}) collective-permute-start(bf16[3,192,256]{2,1,0:T(8,128)(2,1)S(1)} %collective-permute-done.4.refs_5_), channel_id=1, source_target_pairs={{0,18},{4,22},{8,26},{12,30},{2,16},{6,20},{10,24},{14,28},{16,2},... | collective-permute-start | bytes 884744 | tf_op jit(solution)/shard_map/ppermute | solution.py:350
  18.9 16.9 %collective-permute-start.15 = (bf16[3,192,256]{2,1,0:T(8,128)(2,1)}, bf16[3,192,256]{2,1,0:T(8,128)(2,1)}, u32[]{:S(2)}, u32[]{:S(2)}) collective-permute-start(bf16[3,192,256]{2,1,0:T(8,128)(2,1)} %collective-permute-done.5), channel_id=1, source_target_pairs={{4,0},{8,12},{6,2},{10,14},{20,16},{24,28},{22,18},{26,30},{5,1},{... | collective-permute-start | bytes 884744 | tf_op jit(solution)/shard_map/ppermute | solution.py:350
  23.2 15.7 %collective-permute-start.21 = (bf16[3,192,256]{2,1,0:T(8,128)(2,1)S(1)}, bf16[3,192,256]{2,1,0:T(8,128)(2,1)S(1)}, u32[]{:S(2)}, u32[]{:S(2)}) collective-permute-start(bf16[3,192,256]{2,1,0:T(8,128)(2,1)S(1)} %collective-permute-done.4.refs_5_), channel_id=1, source_target_pairs={{4,8},{8,4},{6,10},{10,6},{20,24},{24,20},{22,26},{26,22},{5,9},{9... | collective-permute-start | bytes 884744 | tf_op jit(solution)/shard_map/ppermute | solution.py:350
  26.5 19.1 %collective-permute-start.12 = (bf16[3,192,256]{2,1,0:T(8,128)(2,1)}, bf16[3,192,256]{2,1,0:T(8,128)(2,1)}, u32[]{:S(2)}, u32[]{:S(2)}) collective-permute-start(bf16[3,192,256]{2,1,0:T(8,128)(2,1)} %collective-permute-done.7), channel_id=1, source_target_pairs={{4,0},{8,12},{6,2},{10,14},{20,16},{24,28},{22,18},{26,30},{5,1},{... | collective-permute-start | bytes 884744 | tf_op jit(solution)/shard_map/ppermute | solution.py:350
  29.1 11.2 %collective-permute-start.16 = (bf16[3,192,256]{2,1,0:T(8,128)(2,1)S(1)}, bf16[3,192,256]{2,1,0:T(8,128)(2,1)S(1)}, u32[]{:S(2)}, u32[]{:S(2)}) collective-permute-start(bf16[3,192,256]{2,1,0:T(8,128)(2,1)S(1)} %collective-permute-done.8.refs_5_), channel_id=1, source_target_pairs={{0,18},{4,22},{8,26},{12,30},{2,16},{6,20},{10,24},{14,28},{16,2},... | collective-permute-start | bytes 884744 | tf_op jit(solution)/shard_map/ppermute | solution.py:350
  31.7 11.7 %collective-permute-start.14 = (bf16[3,192,256]{2,1,0:T(8,128)(2,1)}, bf16[3,192,256]{2,1,0:T(8,128)(2,1)}, u32[]{:S(2)}, u32[]{:S(2)}) collective-permute-start(bf16[3,192,256]{2,1,0:T(8,128)(2,1)} %copy-done.6), channel_id=1, source_target_pairs={{4,0},{8,12},{6,2},{10,14},{20,16},{24,28},{22,18},{26,30},{5,1},{... | collective-permute-start | bytes 884744 | tf_op jit(solution)/shard_map/ppermute | solution.py:350
  35.8 14.1 %collective-permute-start.13 = (bf16[3,192,256]{2,1,0:T(8,128)(2,1)S(1)}, bf16[3,192,256]{2,1,0:T(8,128)(2,1)S(1)}, u32[]{:S(2)}, u32[]{:S(2)}) collective-permute-start(bf16[3,192,256]{2,1,0:T(8,128)(2,1)S(1)} %collective-permute-done.8.refs_5_), channel_id=1, source_target_pairs={{4,8},{8,4},{6,10},{10,6},{20,24},{24,20},{22,26},{26,22},{5,9},{9... | collective-permute-start | bytes 884744 | tf_op jit(solution)/shard_map/ppermute | solution.py:350
  38.9 11.0 %collective-permute-start.11 = (bf16[3,192,256]{2,1,0:T(8,128)(2,1)S(1)}, bf16[3,192,256]{2,1,0:T(8,128)(2,1)S(1)}, u32[]{:S(2)}, u32[]{:S(2)}) collective-permute-start(bf16[3,192,256]{2,1,0:T(8,128)(2,1)S(1)} %collective-permute-done.6.refs_5_), channel_id=1, source_target_pairs={{0,18},{4,22},{8,26},{12,30},{2,16},{6,20},{10,24},{14,28},{16,2},... | collective-permute-start | bytes 884744 | tf_op jit(solution)/shard_map/ppermute | solution.py:350
  40.3 14.3 %collective-permute-start.23 = (bf16[3,192,256]{2,1,0:T(8,128)(2,1)S(1)}, bf16[3,192,256]{2,1,0:T(8,128)(2,1)S(1)}, u32[]{:S(2)}, u32[]{:S(2)}) collective-permute-start(bf16[3,192,256]{2,1,0:T(8,128)(2,1)S(1)} %collective-permute-done.21), channel_id=1, source_target_pairs={{4,0},{8,12},{6,2},{10,14},{20,16},{24,28},{22,18},{26,30},{5,1},{... | collective-permute-start | bytes 884744 | tf_op jit(solution)/shard_map/ppermute | solution.py:350
  45.5 11.3 %collective-permute-start.17 = (bf16[3,192,256]{2,1,0:T(8,128)(2,1)S(1)}, bf16[3,192,256]{2,1,0:T(8,128)(2,1)S(1)}, u32[]{:S(2)}, u32[]{:S(2)}) collective-permute-start(bf16[3,192,256]{2,1,0:T(8,128)(2,1)S(1)} %broadcast_select_fusion.4.refs_7_), channel_id=1, source_target_pairs={{0,18},{4,22},{8,26},{12,30},{2,16},{6,20},{10,24},{14,28},{16,2},... | collective-permute-start | bytes 884744 | tf_op jit(solution)/shard_map/ppermute | solution.py:350
  51.5 11.6 %collective-permute-start.24 = (bf16[3,192,256]{2,1,0:T(8,128)(2,1)S(1)}, bf16[3,192,256]{2,1,0:T(8,128)(2,1)S(1)}, u32[]{:S(2)}, u32[]{:S(2)}) collective-permute-start(bf16[3,192,256]{2,1,0:T(8,128)(2,1)S(1)} %broadcast_select_fusion.1.refs_7_), channel_id=1, source_target_pairs={{0,18},{4,22},{8,26},{12,30},{2,16},{6,20},{10,24},{14,28},{16,2},... | collective-permute-start | bytes 884744 | tf_op jit(solution)/shard_map/ppermute | solution.py:350
  52.9 26.3 %collective-permute-start.3 = (bf16[3,192,768]{2,1,0:T(8,128)(2,1)S(1)}, bf16[3,192,768]{2,1,0:T(8,128)(2,1)S(1)}, u32[]{:S(2)}, u32[]{:S(2)}) collective-permute-start(bf16[3,192,768]{2,1,0:T(8,128)(2,1)S(1)} %copy-done.5), channel_id=1, source_target_pairs={{0,2},{2,0},{4,6},{6,4},{8,10},{10,8},{12,14},{14,12},{1,3},{3,1},... | collective-permute-start | bytes 2654216 | tf_op jit(solution)/shard_map/ppermute | solution.py:380
  56.8 12.6 %collective-permute-start.18 = (bf16[3,192,256]{2,1,0:T(8,128)(2,1)S(1)}, bf16[3,192,256]{2,1,0:T(8,128)(2,1)S(1)}, u32[]{:S(2)}, u32[]{:S(2)}) collective-permute-start(bf16[3,192,256]{2,1,0:T(8,128)(2,1)S(1)} %broadcast_select_fusion.5.refs_7_), channel_id=1, source_target_pairs={{0,18},{4,22},{8,26},{12,30},{2,16},{6,20},{10,24},{14,28},{16,2},... | collective-permute-start | bytes 884744 | tf_op jit(solution)/shard_map/ppermute | solution.py:350
  58.3 18.9 %collective-permute-start.2 = (bf16[2,64,1536]{2,1,0:T(8,128)(2,1)S(1)}, bf16[2,64,1536]{2,1,0:T(8,128)(2,1)S(1)}, u32[]{:S(2)}, u32[]{:S(2)}) collective-permute-start(bf16[2,64,1536]{2,1,0:T(8,128)(2,1)S(1)} %copy-done), channel_id=1, source_target_pairs={{3,6},{7,10},{11,14},{5,0},{9,4},{13,8},{19,22},{23,26},{27,30},{2... | collective-permute-start | bytes 1179656 | tf_op jit(solution)/shard_map/ppermute | solution.py:375
  63.1 12.6 %collective-permute-start.25 = (bf16[3,192,256]{2,1,0:T(8,128)(2,1)S(1)}, bf16[3,192,256]{2,1,0:T(8,128)(2,1)S(1)}, u32[]{:S(2)}, u32[]{:S(2)}) collective-permute-start(bf16[3,192,256]{2,1,0:T(8,128)(2,1)S(1)} %broadcast_select_fusion.2.refs_9_), channel_id=1, source_target_pairs={{0,18},{4,22},{8,26},{12,30},{2,16},{6,20},{10,24},{14,28},{16,2},... | collective-permute-start | bytes 884744 | tf_op jit(solution)/shard_map/ppermute | solution.py:350
  64.6 12.9 %collective-permute-start.1 = (bf16[2,64,1536]{2,1,0:T(8,128)(2,1)S(1)}, bf16[2,64,1536]{2,1,0:T(8,128)(2,1)S(1)}, u32[]{:S(2)}, u32[]{:S(2)}) collective-permute-start(bf16[2,64,1536]{2,1,0:T(8,128)(2,1)S(1)} %copy-done), channel_id=1, source_target_pairs={{3,4},{7,8},{11,12},{5,2},{9,6},{13,10},{19,20},{23,24},{27,28},{2... | collective-permute-start | bytes 1179656 | tf_op jit(solution)/shard_map/ppermute | solution.py:375
  69.4 12.6 %collective-permute-start.27 = (bf16[3,192,256]{2,1,0:T(8,128)(2,1)S(1)}, bf16[3,192,256]{2,1,0:T(8,128)(2,1)S(1)}, u32[]{:S(2)}, u32[]{:S(2)}) collective-permute-start(bf16[3,192,256]{2,1,0:T(8,128)(2,1)S(1)} %broadcast_select_fusion.refs_9_), channel_id=1, source_target_pairs={{0,18},{4,22},{8,26},{12,30},{2,16},{6,20},{10,24},{14,28},{16,2},... | collective-permute-start | bytes 884744 | tf_op jit(solution)/shard_map/ppermute | solution.py:350
  75.7 12.5 %collective-permute-start.26 = (bf16[3,192,256]{2,1,0:T(8,128)(2,1)S(1)}, bf16[3,192,256]{2,1,0:T(8,128)(2,1)S(1)}, u32[]{:S(2)}, u32[]{:S(2)}) collective-permute-start(bf16[3,192,256]{2,1,0:T(8,128)(2,1)S(1)} %broadcast_select_fusion.3.refs_9_), channel_id=1, source_target_pairs={{0,18},{4,22},{8,26},{12,30},{2,16},{6,20},{10,24},{14,28},{16,2},... | collective-permute-start | bytes 884744 | tf_op jit(solution)/shard_map/ppermute | solution.py:350
  95.0 12.2 %collective-permute-start.29 = (bf16[2,64,1536]{2,1,0:T(8,128)(2,1)S(1)}, bf16[2,64,1536]{2,1,0:T(8,128)(2,1)S(1)}, u32[]{:S(2)}, u32[]{:S(2)}) collective-permute-start(bf16[2,64,1536]{2,1,0:T(8,128)(2,1)S(1)} %project.2.refs_6_), channel_id=1, source_target_pairs={{0,1},{2,3},{4,5},{6,7},{8,9},{10,11},{12,13},{14,15},{16,17},{18,... | collective-permute-start | bytes 1179656 | tf_op jit(solution)/shard_map/ppermute | solution.py:543
  (19 other events, 242.9 us)
